TPU v7x, 128 devices: a whole 4x4x4 slice. The times are simulated.
128 devices in a mesh: gx: 32 (over y, z, x_hi), gy: 4 (over x_lo, core).
Axes of the slice: x: 4 (x_hi: 2, x_lo: 2; x = x_hi * 2 + x_lo), y: 4, z: 4, core: 2. Of those that a mesh axis runs over, the one named last changes fastest.
Arguments:
- density: bfloat16 [32, 4, 3, 20, 128, 128], P('gx', 'gy'), may hold values from -0.3 to 0.8
- neighbours: int32 [32, 4, 3, 20], replicated, may hold values from 0 to 383, as said below
- ent_blocks: bfloat16 [12288, 128, 128], P(('gx', 'gy')), may hold values from -0.59765625 to 0.59765625
- ent_owner: int32 [12288], replicated, may hold values from 0 to 127, as said below
- ent_place: int32 [12288], replicated, may hold values from 0 to 59
Outputs:
- purified: float32 [32, 4, 3, 20, 128, 128], P('gx', 'gy')
Inputs may be any that keep to these rules, and one draw needn't show every extreme that they name: neighbours[x, y, r, 0] is the row's own index (x * 4 + y) * 3 + r; the other 19 entries of a row are distinct rows of devices (x + a mod 32, y + b mod 4) with a and b in -1, 0, 1. `ent_owner`: among the 96 entries d * 96 to d * 96 + 95 of one device d, no owner is named more than 2 times, and some owner exactly 2 times.
All inputs are finite; a program needn't handle non-finite values.
Results may differ from a plain program's by a relative error of at most 0.0059.
Values may be sent and summed in bfloat16 or wider, within the bound.
No kernel may reach another device: no remote copies, remote signals or barrier semaphores. Data moves between devices by JAX's collectives and lax.ppermute only.
A program may use at most 128 MiB of HBM per device.

v0:
```python
import functools

import jax
import jax.numpy as jnp
from jax import lax
from jax.experimental import pallas as pl
from jax.experimental.pallas import tpu as pltpu
from jax.sharding import PartitionSpec as P

C = 2


def pack_kernel(slots_ref, ent_ref, out_ref, staged, load_sems, store_sem):
    count = ent_ref.shape[0]
    parts = load_sems.shape[0]
    size = count // parts
    loads = []
    for p in range(parts):
        rows = pl.ds(p * size, size)
        loads.append(pltpu.make_async_copy(ent_ref.at[rows], staged.at[rows], load_sems.at[p]))
        loads[-1].start()

    def issue(i, carry):
        pltpu.make_async_copy(staged.at[i], out_ref.at[slots_ref[i]], store_sem).start()
        return carry

    for p in range(parts):
        loads[p].wait()
        lax.fori_loop(p * size, (p + 1) * size, issue, 0)
    pltpu.make_async_copy(staged, out_ref.at[pl.ds(0, count)], store_sem).wait()


def pack(ent_blocks, slots, total):
    return pl.pallas_call(
        pack_kernel,
        out_shape=jax.ShapeDtypeStruct((total,) + ent_blocks.shape[1:], ent_blocks.dtype),
        in_specs=[
            pl.BlockSpec(memory_space=pltpu.SMEM),
            pl.BlockSpec(memory_space=pl.ANY),
        ],
        out_specs=pl.BlockSpec(memory_space=pl.ANY),
        scratch_shapes=[
            pltpu.VMEM(ent_blocks.shape, ent_blocks.dtype),
            pltpu.SemaphoreType.DMA((4,)),
            pltpu.SemaphoreType.DMA,
        ],
        name="pack",
    )(slots, ent_blocks)


def admit_kernel(spans, first_ref, order_ref, source_ref, density_ref, received_ref, *refs):
    part_refs, own, sems = refs[: len(spans)], refs[len(spans)], refs[len(spans) + 1]

    def add(j, total):
        return total + received_ref[order_ref[j]].astype(jnp.float32)

    def place(p, carry):
        t = source_ref[p]
        total = lax.fori_loop(
            first_ref[t], first_ref[t + 1], add, density_ref[t].astype(jnp.float32)
        )
        own[p] = total.astype(own.dtype)
        return carry

    copies = []
    done = 0
    for i, (low, high) in enumerate(spans):
        if high > done:
            lax.fori_loop(done, high, place, 0)
            done = high
        copies.append(pltpu.make_async_copy(own.at[pl.ds(low, high - low)], part_refs[i], sems.at[i]))
        copies[-1].start()
    for copy in copies:
        copy.wait()


def admit(density, received, first, order, source, spans):
    return pl.pallas_call(
        functools.partial(admit_kernel, spans),
        out_shape=[
            jax.ShapeDtypeStruct((high - low,) + density.shape[1:], density.dtype)
            for low, high in spans
        ],
        in_specs=[pl.BlockSpec(memory_space=pltpu.SMEM)] * 3
        + [pl.BlockSpec(memory_space=pltpu.VMEM)] * 2,
        out_specs=[pl.BlockSpec(memory_space=pl.ANY)] * len(spans),
        scratch_shapes=[
            pltpu.VMEM(density.shape, density.dtype),
            pltpu.SemaphoreType.DMA((len(spans),)),
        ],
        name="admit",
    )(first, order, source, density, received)


def reach(part):
    wide, narrow = divmod(part, 3)
    wides = (0, 1, 2) if wide == 0 else (0, wide)
    narrows = (0, 1, 2) if narrow == 0 else (0, narrow)
    return [w * 3 + n for w in wides for n in narrows]


NEAR_PARTS = 6


def near_count(part):
    return len([q for q in reach(part) if q < NEAR_PARTS])


def far_count(part):
    return len(reach(part)) - near_count(part)


def load_pieces(pieces, piece_starts, table, sems):
    copies = []
    for i, (piece, start) in enumerate(zip(pieces, piece_starts)):
        copies.append(
            pltpu.make_async_copy(piece, table.at[pl.ds(start, piece.shape[0])], sems.at[i])
        )
        copies[-1].start()
    return copies


def lanes_of(ref, parts, group):
    return jnp.concatenate([ref[:, q * group:(q + 1) * group] for q in parts], axis=1)


def near_kernel(row_count, width, piece_starts, table_size, pos_ref, *refs):
    pieces = refs[: len(piece_starts)]
    outs = refs[len(piece_starts):]
    grids, (square, left_far, table, left, sems) = outs[:9], outs[9:]
    near = 9 * row_count
    group = row_count * width
    copies = load_pieces(pieces, piece_starts, table, sems)
    table[table_size] = jnp.zeros((width, width), table.dtype)
    for copy in copies:
        copy.wait()

    def block(m, k):
        return table[jnp.minimum(pos_ref[m * near + k], table_size)]

    for r in range(row_count):
        for k in range(near):
            left[r * width:(r + 1) * width, k * width:(k + 1) * width] = block(r, k)
    left_far[...] = left[:, NEAR_PARTS * group:]
    for part in range(9):
        parts = [q for q in reach(part) if q < NEAR_PARTS]
        for i, q in enumerate(parts):
            for r in range(row_count):
                for k in range(row_count):
                    low = (i * row_count + r) * width
                    grids[part][low:low + width, k * width:(k + 1) * width] = block(
                        q * row_count + r, part * row_count + k
                    )
        square[part] = jnp.dot(
            lanes_of(left, parts, group), grids[part][...], preferred_element_type=jnp.float32
        )


def square_near(positions, pieces, piece_starts, table_size, row_count, width):
    group = row_count * width
    span = 9 * group
    return pl.pallas_call(
        functools.partial(near_kernel, row_count, width, piece_starts, table_size),
        out_shape=[
            pltpu.VMEM((near_count(part) * group, group), jnp.bfloat16) for part in range(9)
        ] + [
            pltpu.VMEM((9, group, group), jnp.float32),
            pltpu.VMEM((group, (9 - NEAR_PARTS) * group), jnp.bfloat16),
        ],
        in_specs=[pl.BlockSpec(memory_space=pltpu.SMEM)]
        + [pl.BlockSpec(memory_space=pl.ANY)] * len(pieces),
        out_specs=[pl.BlockSpec(memory_space=pltpu.VMEM)] * 11,
        scratch_shapes=[
            pltpu.VMEM((table_size + 1, width, width), jnp.bfloat16),
            pltpu.VMEM((group, span), jnp.bfloat16),
            pltpu.SemaphoreType.DMA((len(pieces),)),
        ],
        compiler_params=pltpu.CompilerParams(vmem_limit_bytes=20 << 20),
        name="square_near",
    )(positions, *pieces)


def far_kernel(row_count, width, piece_starts, table_start, table_size, pos_ref, slot_ref, *refs):
    pieces = refs[: len(piece_starts)]
    outs = refs[len(piece_starts):]
    near_grids = outs[:9]
    square_in, left, out_ref, table, grid, square, square_b, staged, sems, out_sem = outs[9:]
    near = 9 * row_count
    group = row_count * width
    zero_at = table_start + table_size
    copies = load_pieces(pieces, piece_starts, table, sems)
    table[table_size] = jnp.zeros((width, width), table.dtype)
    for copy in copies:
        copy.wait()

    for part in range(9):
        parts = reach(part)
        base = near_count(part)
        far_base = sum(far_count(q) for q in range(part)) * group
        for i, q in enumerate(parts[base:]):
            for r in range(row_count):
                for k in range(row_count):
                    low = far_base + (i * row_count + r) * width
                    grid[low:low + width, k * width:(k + 1) * width] = table[
                        pos_ref[(q * row_count + r) * near + part * row_count + k] - table_start
                    ]
        product = square_in[part]
        if base < len(parts):
            product = product + jnp.dot(
                lanes_of(left, [q - NEAR_PARTS for q in parts[base:]], group),
                grid[far_base:far_base + far_count(part) * group],
                preferred_element_type=jnp.float32,
            )
        square[part] = product
        for r in range(row_count):
            for k in range(row_count):
                listed = pos_ref[r * near + part * row_count + k] != zero_at
                low = part * group + k * width
                square_b[r * width:(r + 1) * width, low:low + width] = jnp.where(
                    listed, product[r * width:(r + 1) * width, k * width:(k + 1) * width], 0.0
                ).astype(jnp.bfloat16)

    blocks = out_ref.shape[0]
    for part in range(9):
        parts = reach(part)
        base = near_count(part)
        far_base = sum(far_count(q) for q in range(part)) * group
        product = jnp.dot(
            lanes_of(square_b, parts[:base], group), near_grids[part][...],
            preferred_element_type=jnp.float32,
        )
        if base < len(parts):
            product = product + jnp.dot(
                lanes_of(square_b, parts[base:], group),
                grid[far_base:far_base + far_count(part) * group],
                preferred_element_type=jnp.float32,
            )
        result = 3.0 * square[part] - 2.0 * product
        for r in range(row_count):
            for k in range(row_count):
                slot = slot_ref[r * near + part * row_count + k]
                staged[slot] = result[r * width:(r + 1) * width, k * width:(k + 1) * width]

                @pl.when(slot < blocks)
                def _():
                    pltpu.make_async_copy(staged.at[slot], out_ref.at[slot], out_sem).start()

    pltpu.make_async_copy(staged.at[pl.ds(0, blocks)], out_ref, out_sem).wait()


def purify_far(
    positions, out_slots, pieces, piece_starts, carried, table_start, table_size,
    row_count, slot_count, width,
):
    group = row_count * width
    span = 9 * group
    blocks = row_count * slot_count
    return pl.pallas_call(
        functools.partial(
            far_kernel, row_count, width, piece_starts, table_start, table_size
        ),
        out_shape=jax.ShapeDtypeStruct((blocks, width, width), jnp.float32),
        in_specs=[pl.BlockSpec(memory_space=pltpu.SMEM)] * 2
        + [pl.BlockSpec(memory_space=pl.ANY)] * len(pieces)
        + [pl.BlockSpec(memory_space=pltpu.VMEM)] * len(carried),
        out_specs=pl.BlockSpec(memory_space=pl.ANY),
        scratch_shapes=[
            pltpu.VMEM((table_size + 1, width, width), jnp.bfloat16),
            pltpu.VMEM((sum(far_count(part) for part in range(9)) * group, group), jnp.bfloat16),
            pltpu.VMEM((9, group, group), jnp.float32),
            pltpu.VMEM((group, span), jnp.bfloat16),
            pltpu.VMEM((blocks + 1, width, width), jnp.float32),
            pltpu.SemaphoreType.DMA((len(pieces),)),
            pltpu.SemaphoreType.DMA,
        ],
        compiler_params=pltpu.CompilerParams(vmem_limit_bytes=28 << 20),
        name="purify_far",
    )(
        positions, out_slots, *pieces,
        *[pltpu.with_memory_space_constraint(array, pltpu.VMEM) for array in carried],
    )


def block_positions(neighbours, here_x, here_y, starts, zero_at):
    wide_count, narrow_count, row_count, slot_count = neighbours.shape
    total_rows = wide_count * narrow_count * row_count
    listing = neighbours.reshape(total_rows, slot_count)
    ids = jnp.arange(9 * row_count, dtype=jnp.int32)
    wide, narrow, inner = ids // (3 * row_count), ids // row_count % 3, ids % row_count
    beyond = jnp.where(here_x % 2 == 0, here_x + wide_count - 1, here_x + 1) % wide_count
    near_x = jnp.where(wide == 0, here_x, jnp.where(wide == 1, here_x ^ 1, beyond))
    near_y = jnp.where(
        narrow == 0, here_y, jnp.where(narrow == 1, here_y ^ 1, narrow_count - 1 - here_y)
    )
    rows = (near_x * narrow_count + near_y) * row_count + inner
    lists = jnp.take(listing, rows, axis=0)
    list_x = lists // (narrow_count * row_count)
    list_y = lists // row_count % narrow_count
    kind = jnp.where(
        list_x == (near_x ^ 1)[:, None], 2, jnp.where(list_y == (near_y ^ 1)[:, None], 1, 0)
    )
    slot_ids = jnp.arange(slot_count, dtype=jnp.int32)
    key = kind * slot_count + slot_ids
    place = jnp.sum((key[:, :, None] > key[:, None, :]).astype(jnp.int32), axis=2)
    part = wide * 3 + narrow
    start = jnp.zeros_like(part)
    for i, value in enumerate(starts):
        start = jnp.where(part == i, value, start)
    held_at = (start + inner)[:, None] + place * row_count
    matches = lists[:, None, :] == rows[None, :, None]
    positions = jnp.min(jnp.where(matches, held_at[:, None, :], zero_at), axis=2)
    own_matches = matches[:row_count]
    own_slots = slot_ids + slot_count * jnp.arange(row_count, dtype=jnp.int32)[:, None, None]
    out_slots = jnp.min(jnp.where(own_matches, own_slots, row_count * slot_count), axis=2)
    order = (place[:row_count] * row_count + inner[:row_count, None]).reshape(-1)
    flat_ids = jnp.arange(row_count * slot_count, dtype=jnp.int32)
    source = jnp.sum(jnp.where(order[None, :] == flat_ids[:, None], flat_ids[None, :], 0), axis=1)
    return (
        positions.astype(jnp.int32).reshape(-1),
        out_slots.astype(jnp.int32).reshape(-1),
        source.astype(jnp.int32),
    )


def per_device(density, neighbours, ent_blocks, ent_owner, ent_place):
    wide_count = lax.axis_size("gx")
    narrow_count = lax.axis_size("gy")
    device_count = wide_count * narrow_count
    here_x = lax.axis_index("gx")
    here_y = lax.axis_index("gy")
    self_index = here_x * narrow_count + here_y
    row_count = density.shape[2]
    slot_count = density.shape[3]
    width = density.shape[4]
    blocks = row_count * slot_count
    held = ent_blocks.shape[0]
    owners = ent_owner.reshape(device_count, held)
    places = ent_place.reshape(device_count, held)

    my_owners = lax.dynamic_index_in_dim(owners, self_index, 0, False)
    entry_ids = jnp.arange(held, dtype=jnp.int32)
    same = my_owners[:, None] == my_owners[None, :]
    my_ranks = jnp.sum(same & (entry_ids[None, :] < entry_ids[:, None]), axis=1)
    slots = (my_owners * C + my_ranks).astype(jnp.int32)
    outgoing = pack(ent_blocks, slots, device_count * C)
    received = lax.all_to_all(
        outgoing.reshape(device_count, C, width, width),
        ("gx", "gy"), split_axis=0, concat_axis=0, tiled=True,
    ).reshape(device_count * C, width, width)

    for_me = (owners == self_index).astype(jnp.int32)
    rank = jnp.cumsum(for_me, axis=1) - for_me
    picked = (for_me[:, :, None] == 1) & (
        rank[:, :, None] == jnp.arange(C, dtype=jnp.int32)[None, None, :]
    )
    slot_place = jnp.sum(jnp.where(picked, places[:, :, None], 0), axis=1).reshape(-1)
    slot_used = jnp.any(picked, axis=1).reshape(-1)
    slot_place = jnp.where(slot_used, slot_place, blocks)
    slot_ids = jnp.arange(device_count * C, dtype=jnp.int32)
    ahead = (slot_place[:, None] > slot_place[None, :]) | (
        (slot_place[:, None] == slot_place[None, :]) & (slot_ids[:, None] > slot_ids[None, :])
    )
    sorted_at = jnp.sum(ahead, axis=1)
    order = jnp.sum(
        jnp.where(sorted_at[None, :] == slot_ids[:, None], slot_ids[None, :], 0), axis=1
    ).astype(jnp.int32)
    target_ids = jnp.arange(blocks + 1, dtype=jnp.int32)
    first = jnp.sum(slot_place[None, :] < target_ids[:, None], axis=1).astype(jnp.int32)

    near_blocks = row_count * min(slot_count, 6 * row_count)
    corner_blocks = row_count * min(slot_count, 4 * row_count)
    sizes = [blocks] * 6 + [near_blocks, near_blocks, corner_blocks]
    starts = [sum(sizes[:i]) for i in range(9)]
    zero_at = sum(sizes)
    positions, out_slots, source = block_positions(neighbours, here_x, here_y, starts, zero_at)

    cut = corner_blocks // 2
    spans = ((0, cut), (cut, 2 * cut), (0, 2 * cut), (2 * cut, blocks))
    received, first, order, source, positions, out_slots = lax.optimization_barrier(
        (received, first, order, source, positions, out_slots)
    )
    own_1, own_2, own_12, own_3 = admit(
        density.reshape(blocks, width, width), received, first, order, source, spans
    )

    axes = ("gx", "gy")
    devices = [(x, y) for x in range(wide_count) for y in range(narrow_count)]

    def send(array, target):
        pairs = []
        for x, y in devices:
            to_x, to_y = target(x, y)
            pairs.append((x * narrow_count + y, to_x % wide_count * narrow_count + to_y))
        return lax.ppermute(array, axes, pairs)

    def across(x, y):
        return x, narrow_count - 1 - y

    def chip(x, y):
        return x, y ^ 1

    def ring(x, y):
        return x ^ 1, narrow_count - 1 - y

    def onward(x, y):
        return (x + 2 if x % 2 == 0 else x - 2), y

    ring_across_1 = send(own_1, ring)
    own_across_3 = send(own_3, across)
    ring_across_2 = send(own_2, ring)
    own_chip_12 = send(own_12, chip)
    own_chip_3 = send(own_3, chip)
    far_across_1 = send(ring_across_1, onward)
    ring_same_1 = send(ring_across_1, across)
    ring_same_3 = send(own_across_3, ring)
    far_across_2 = send(ring_across_2, onward)
    ring_same_2 = send(ring_across_2, across)
    ring_across_3 = send(own_3, ring)
    own_across_12 = send(own_12, across)
    far_same_1 = send(ring_same_1, onward)
    ring_chip_1 = send(ring_same_1, chip)
    far_same_2 = send(ring_same_2, onward)
    ring_chip_2 = send(ring_same_2, chip)
    far_same_3 = send(ring_same_3[:near_blocks - 2 * cut], onward)
    ring_chip_3 = send(ring_same_3, chip)
    far_chip_1 = send(far_same_1, chip)
    far_chip_2 = send(far_same_2, chip)
    far_chip_3 = send(far_same_3, chip)

    near_pieces = [
        (own_12, 0, 0), (own_3, 0, 2 * cut), (own_chip_12, 1, 0), (own_chip_3, 1, 2 * cut),
        (own_across_12, 2, 0), (own_across_3, 2, 2 * cut),
        (ring_same_1, 3, 0), (ring_same_2, 3, cut), (ring_same_3, 3, 2 * cut),
        (ring_chip_1, 4, 0), (ring_chip_2, 4, cut), (ring_chip_3, 4, 2 * cut),
        (ring_across_1, 5, 0), (ring_across_2, 5, cut), (ring_across_3, 5, 2 * cut),
    ]
    far_pieces = [
        (far_same_1, 6, 0), (far_same_2, 6, cut), (far_same_3, 6, 2 * cut),
        (far_chip_1, 7, 0), (far_chip_2, 7, cut), (far_chip_3, 7, 2 * cut),
        (far_across_1, 8, 0), (far_across_2, 8, cut),
    ]
    far_start = starts[NEAR_PARTS]
    carried = square_near(
        positions, [piece for piece, _, _ in near_pieces],
        [starts[part] + offset for _, part, offset in near_pieces],
        far_start, row_count, width,
    )
    purified = purify_far(
        positions, out_slots, [piece for piece, _, _ in far_pieces],
        [starts[part] + offset - far_start for _, part, offset in far_pieces],
        carried, far_start, zero_at - far_start, row_count, slot_count, width,
    )
    return purified.reshape(density.shape)


def solution(mesh):
    in_specs = (P("gx", "gy", None, None, None, None), P(), P(("gx", "gy"), None, None), P(), P())
    out_specs = P("gx", "gy", None, None, None, None)
    return jax.shard_map(
        per_device, mesh=mesh, in_specs=in_specs, out_specs=out_specs, check_vma=False
    )
```

profile of v0, /device:TPU:1, one launch (start us, length us, event | category | flops | bytes accessed | tf_op | source)
XLA Modules:
  0.0 292.5 jit_solution(3209147326442700866)
XLA Ops:
  0.0 0.9 reshape.486
  1.1 0.5 multiply_add_fusion.3.slots_ref
  1.6 3.5 %pack.1 = bf16[256,128,128]{2,1,0:T(8,128)(2,1)} custom-call(s32[96]{0:T(128)} %multiply_add_fusion.3.slots_ref, bf16[96,128,128]{2,1,0:T(8,128)(2,1)} %ent_ref.1), custom_call_target="tpu_custom_call" | custom-call | tf_op jit(solution)/shard_map/pack/pallas_call | solution.py:34
  5.2 12.1 %all-to-all-start = ((bf16[128,2,128,128]{3,2,1,0:T(8,128)(2,1)}), bf16[128,2,128,128]{3,2,1,0:T(8,128)(2,1)}, u32[]{:S(2)}, u32[]{:S(2)}) async-start(bf16[128,2,128,128]{3,2,1,0:T(8,128)(2,1)} %bitcast.12), calls=%async_computation | async-start | bytes 16777216 | tf_op jit(solution)/shard_map/all_to_all | solution.py:346
  17.7 0.6 gather_fusion
  19.2 0.3 select_reduce_fusion
  20.5 0.7 select_reduce_fusion.4.source_ref
  21.2 0.7 convert_reduce_fusion.2.first_ref
  22.0 0.7 select_reduce_fusion.1.order_ref
  22.7 93.8 %all-to-all-done = bf16[128,2,128,128]{3,2,1,0:T(8,128)(2,1)} async-done(((bf16[128,2,128,128]{3,2,1,0:T(8,128)(2,1)}), bf16[128,2,128,128]{3,2,1,0:T(8,128)(2,1)}, u32[]{:S(2)}, u32[]{:S(2)}) %all-to-all-start) | async-done | bytes 8388640 | tf_op jit(solution)/shard_map/all_to_all | solution.py:346
  116.6 7.1 %admit.1 = (bf16[18,128,128]{2,1,0:T(8,128)(2,1)}, bf16[18,128,128]{2,1,0:T(8,128)(2,1)}, bf16[36,128,128]{2,1,0:T(8,128)(2,1)}, bf16[24,128,128]{2,1,0:T(8,128)(2,1)}) custom-call(s32[61]{0:T(128)} %convert_reduce_fusion.2.first_ref, s32[256]{0:T(256)} %select_reduce_fusion.1.order_ref, s32[60]{0:T(128)} %select_reduce_fusion.4.source_ref, ...), custom_call_target="tpu_custom_call" | custom-call | tf_op jit(solution)/shard_map/admit/pallas_call | solution.py:78
  123.7 6.1 %collective-permute-start.6 = (bf16[24,128,128]{2,1,0:T(8,128)(2,1)}, bf16[24,128,128]{2,1,0:T(8,128)(2,1)S(1)}, u32[]{:S(2)}, u32[]{:S(2)}) collective-permute-start(bf16[24,128,128]{2,1,0:T(8,128)(2,1)} %get-tuple-element.34.refs_1_), channel_id=1, source_target_pairs={{0,3},{1,2},{2,1},{3,0},{4,7},{5,6},{6,5},{7,4},{8,11},{9,10},{10,... | collective-permute-start | bytes 2359304 | tf_op jit(solution)/shard_map/ppermute | solution.py:394
  129.9 3.0 %collective-permute-start.3 = (bf16[18,128,128]{2,1,0:T(8,128)(2,1)}, bf16[18,128,128]{2,1,0:T(8,128)(2,1)S(1)}, u32[]{:S(2)}, u32[]{:S(2)}) collective-permute-start(bf16[18,128,128]{2,1,0:T(8,128)(2,1)} %get-tuple-element.33), channel_id=1, source_target_pairs={{0,7},{1,6},{2,5},{3,4},{4,3},{5,2},{6,1},{7,0},{8,15},{9,14},{10,... | collective-permute-start | bytes 1769480 | tf_op jit(solution)/shard_map/ppermute | solution.py:394
  132.9 14.3 %collective-permute-done.refs_12_ = bf16[18,128,128]{2,1,0:T(8,128)(2,1)S(1)} collective-permute-done((bf16[18,128,128]{2,1,0:T(8,128)(2,1)}, bf16[18,128,128]{2,1,0:T(8,128)(2,1)S(1)}, u32[]{:S(2)}, u32[]{:S(2)}) %collective-permute-start) | collective-permute-done | bytes 589856 | tf_op jit(solution)/shard_map/ppermute | solution.py:394
  147.2 12.6 %collective-permute-done.3.refs_13_ = bf16[18,128,128]{2,1,0:T(8,128)(2,1)S(1)} collective-permute-done((bf16[18,128,128]{2,1,0:T(8,128)(2,1)}, bf16[18,128,128]{2,1,0:T(8,128)(2,1)S(1)}, u32[]{:S(2)}, u32[]{:S(2)}) %collective-permute-start.3) | collective-permute-done | bytes 589856 | tf_op jit(solution)/shard_map/ppermute | solution.py:394
  159.8 1.7 collective-permute-start.1
  161.6 15.1 %collective-permute-done.20.refs_14_ = bf16[24,128,128]{2,1,0:T(8,128)(2,1)S(1)} collective-permute-done((bf16[24,128,128]{2,1,0:T(8,128)(2,1)}, bf16[24,128,128]{2,1,0:T(8,128)(2,1)S(1)}, u32[]{:S(2)}, u32[]{:S(2)}) %collective-permute-start.20) | collective-permute-done | bytes 786464 | tf_op jit(solution)/shard_map/ppermute | solution.py:394
  176.7 24.6 %collective-permute-done.1.refs_6_ = bf16[18,128,128]{2,1,0:T(8,128)(2,1)S(1)} collective-permute-done((bf16[18,128,128]{2,1,0:T(8,128)(2,1)S(1)}, bf16[18,128,128]{2,1,0:T(8,128)(2,1)S(1)}, u32[]{:S(2)}, u32[]{:S(2)}) %collective-permute-start.1) | collective-permute-done | bytes 589856 | tf_op jit(solution)/shard_map/ppermute | solution.py:394
  201.3 0.5 collective-permute-start.19
  201.8 9.0 %collective-permute-done.4.refs_7_ = bf16[18,128,128]{2,1,0:T(8,128)(2,1)S(1)} collective-permute-done((bf16[18,128,128]{2,1,0:T(8,128)(2,1)S(1)}, bf16[18,128,128]{2,1,0:T(8,128)(2,1)S(1)}, u32[]{:S(2)}, u32[]{:S(2)}) %collective-permute-start.4) | collective-permute-done | bytes 589856 | tf_op jit(solution)/shard_map/ppermute | solution.py:394
  210.9 1.5 collective-permute-start.5
  212.5 1.1 collective-permute-start.8
  213.6 2.8 collective-permute-start.12
  216.4 12.2 %collective-permute-done.5.refs_1_ = bf16[18,128,128]{2,1,0:T(8,128)(2,1)S(1)} collective-permute-done((bf16[18,128,128]{2,1,0:T(8,128)(2,1)S(1)}, bf16[18,128,128]{2,1,0:T(8,128)(2,1)S(1)}, u32[]{:S(2)}, u32[]{:S(2)}) %collective-permute-start.5) | collective-permute-done | bytes 589856 | tf_op jit(solution)/shard_map/ppermute | solution.py:394
  228.6 12.6 %collective-permute-done.2.refs_0_ = bf16[18,128,128]{2,1,0:T(8,128)(2,1)S(1)} collective-permute-done((bf16[18,128,128]{2,1,0:T(8,128)(2,1)S(1)}, bf16[18,128,128]{2,1,0:T(8,128)(2,1)S(1)}, u32[]{:S(2)}, u32[]{:S(2)}) %collective-permute-start.2) | collective-permute-done | bytes 589856 | tf_op jit(solution)/shard_map/ppermute | solution.py:394
  241.2 2.3 collective-permute-start.10
  243.5 10.3 %collective-permute-done.8.refs_2_ = bf16[18,128,128]{2,1,0:T(8,128)(2,1)S(1)} collective-permute-done((bf16[18,128,128]{2,1,0:T(8,128)(2,1)S(1)}, bf16[18,128,128]{2,1,0:T(8,128)(2,1)S(1)}, u32[]{:S(2)}, u32[]{:S(2)}) %collective-permute-start.8) | collective-permute-done | bytes 589856 | tf_op jit(solution)/shard_map/ppermute | solution.py:394
  253.8 2.3 collective-permute-start.9
  256.2 1.1 copy-done.1
  257.3 9.0 %square_near.1 = (bf16[2304,384]{1,0:T(8,128)(2,1)S(1)}, bf16[1536,384]{1,0:T(8,128)(2,1)S(1)}, bf16[1536,384]{1,0:T(8,128)(2,1)S(1)}, bf16[2304,384]{1,0:T(8,12...) custom-call(s32[729]{0:T(1024)S(1)} %reshape.490.pos_ref, ...), custom_call_target="tpu_custom_call" | custom-call | tf_op jit(solution)/shard_map/square_near/pallas_call | solution.py:162
  266.5 12.6 %collective-permute-done.13.refs_7_ = bf16[18,128,128]{2,1,0:T(8,128)(2,1)S(1)} collective-permute-done((bf16[18,128,128]{2,1,0:T(8,128)(2,1)S(1)}, bf16[18,128,128]{2,1,0:T(8,128)(2,1)S(1)}, u32[]{:S(2)}, u32[]{:S(2)}) %collective-permute-start.13) | collective-permute-done | bytes 589856 | tf_op jit(solution)/shard_map/ppermute | solution.py:394
  279.1 13.2 %purify_far.1 = f32[60,128,128]{2,1,0:T(8,128)} custom-call(s32[729]{0:T(1024)S(1)} %reshape.490.pos_ref, s32[81]{0:T(128)S(1)} %reshape.491.slot_ref, bf16[18,128,128]{2,1,0:T(8,128)(2,1)S(1)} %collective-permute-done.2.refs_0_, bf16[18,128,128]{2,1,0:T(8,128)(2,1)S(1)} %collective-permute-done.5.refs_1_, ...), custom_call_target="tpu_custom_call" | custom-call | tf_op jit(solution)/shard_map/purify_far/pallas_call | solution.py:258
  (69 shorter events, 3.0 us)
Async XLA Ops:
  5.1 12.2 %copy-start.2 = (s32[32,4,3,20]{0,1,3,2:T(4,128)S(1)}, s32[32,4,3,20]{0,1,3,2:T(4,128)}, u32[]{:S(2)}) copy-start(s32[32,4,3,20]{0,1,3,2:T(4,128)} %param.6) | copy-start | bytes 92164
  5.2 111.4 %all-to-all-start = ((bf16[128,2,128,128]{3,2,1,0:T(8,128)(2,1)}), bf16[128,2,128,128]{3,2,1,0:T(8,128)(2,1)}, u32[]{:S(2)}, u32[]{:S(2)}) async-start(bf16[128,2,128,128]{3,2,1,0:T(8,128)(2,1)} %bitcast.12), calls=%async_computation | async-start | bytes 16777216 | tf_op jit(solution)/shard_map/all_to_all | solution.py:346
  17.2 2.8 copy-start.3
  123.7 132.5 %copy-start = (bf16[36,128,128]{2,1,0:T(8,128)(2,1)S(1)}, bf16[36,128,128]{2,1,0:T(8,128)(2,1)}, u32[]{:S(2)}) copy-start(bf16[36,128,128]{2,1,0:T(8,128)(2,1)} %get-tuple-element.35.refs_0_) | copy-start | bytes 3538948
  123.7 36.1 %collective-permute-start.6 = (bf16[24,128,128]{2,1,0:T(8,128)(2,1)}, bf16[24,128,128]{2,1,0:T(8,128)(2,1)S(1)}, u32[]{:S(2)}, u32[]{:S(2)}) collective-permute-start(bf16[24,128,128]{2,1,0:T(8,128)(2,1)} %get-tuple-element.34.refs_1_), channel_id=1, source_target_pairs={{0,3},{1,2},{2,1},{3,0},{4,7},{5,6},{6,5},{7,4},{8,11},{9,10},{10,... | collective-permute-start | bytes 2359304 | tf_op jit(solution)/shard_map/ppermute | solution.py:394
  129.9 17.3 %collective-permute-start = (bf16[18,128,128]{2,1,0:T(8,128)(2,1)}, bf16[18,128,128]{2,1,0:T(8,128)(2,1)S(1)}, u32[]{:S(2)}, u32[]{:S(2)}) collective-permute-start(bf16[18,128,128]{2,1,0:T(8,128)(2,1)} %get-tuple-element.32), channel_id=1, source_target_pairs={{0,7},{1,6},{2,5},{3,4},{4,3},{5,2},{6,1},{7,0},{8,15},{9,14},{10,... | collective-permute-start | bytes 1769480 | tf_op jit(solution)/shard_map/ppermute | solution.py:394
  129.9 30.0 %collective-permute-start.3 = (bf16[18,128,128]{2,1,0:T(8,128)(2,1)}, bf16[18,128,128]{2,1,0:T(8,128)(2,1)S(1)}, u32[]{:S(2)}, u32[]{:S(2)}) collective-permute-start(bf16[18,128,128]{2,1,0:T(8,128)(2,1)} %get-tuple-element.33), channel_id=1, source_target_pairs={{0,7},{1,6},{2,5},{3,4},{4,3},{5,2},{6,1},{7,0},{8,15},{9,14},{10,... | collective-permute-start | bytes 1769480 | tf_op jit(solution)/shard_map/ppermute | solution.py:394
  132.8 28.8 %collective-permute-start.15 = (bf16[24,128,128]{2,1,0:T(8,128)(2,1)}, bf16[24,128,128]{2,1,0:T(8,128)(2,1)S(1)}, u32[]{:S(2)}, u32[]{:S(2)}) collective-permute-start(bf16[24,128,128]{2,1,0:T(8,128)(2,1)} %get-tuple-element.34.refs_1_), channel_id=1, source_target_pairs={{0,1},{1,0},{2,3},{3,2},{4,5},{5,4},{6,7},{7,6},{8,9},{9,8},{10,11... | collective-permute-start | bytes 2359304 | tf_op jit(solution)/shard_map/ppermute | solution.py:394
  132.8 43.9 %collective-permute-start.20 = (bf16[24,128,128]{2,1,0:T(8,128)(2,1)}, bf16[24,128,128]{2,1,0:T(8,128)(2,1)S(1)}, u32[]{:S(2)}, u32[]{:S(2)}) collective-permute-start(bf16[24,128,128]{2,1,0:T(8,128)(2,1)} %get-tuple-element.34.refs_1_), channel_id=1, source_target_pairs={{0,7},{1,6},{2,5},{3,4},{4,3},{5,2},{6,1},{7,0},{8,15},{9,14},{10,... | collective-permute-start | bytes 2359304 | tf_op jit(solution)/shard_map/ppermute | solution.py:394
  147.2 63.7 %collective-permute-start.14 = (bf16[36,128,128]{2,1,0:T(8,128)(2,1)}, bf16[36,128,128]{2,1,0:T(8,128)(2,1)S(1)}, u32[]{:S(2)}, u32[]{:S(2)}) collective-permute-start(bf16[36,128,128]{2,1,0:T(8,128)(2,1)} %get-tuple-element.35.refs_0_), channel_id=1, source_target_pairs={{0,1},{1,0},{2,3},{3,2},{4,5},{5,4},{6,7},{7,6},{8,9},{9,8},{10,11... | collective-permute-start | bytes 3538952 | tf_op jit(solution)/shard_map/ppermute | solution.py:394
  159.8 52.5 %collective-permute-start.16 = (bf16[36,128,128]{2,1,0:T(8,128)(2,1)}, bf16[36,128,128]{2,1,0:T(8,128)(2,1)S(1)}, u32[]{:S(2)}, u32[]{:S(2)}) collective-permute-start(bf16[36,128,128]{2,1,0:T(8,128)(2,1)} %get-tuple-element.35.refs_0_), channel_id=1, source_target_pairs={{0,3},{1,2},{2,1},{3,0},{4,7},{5,6},{6,5},{7,4},{8,11},{9,10},{10,... | collective-permute-start | bytes 3538952 | tf_op jit(solution)/shard_map/ppermute | solution.py:394
  159.8 41.4 %collective-permute-start.1 = (bf16[18,128,128]{2,1,0:T(8,128)(2,1)S(1)}, bf16[18,128,128]{2,1,0:T(8,128)(2,1)S(1)}, u32[]{:S(2)}, u32[]{:S(2)}) collective-permute-start(bf16[18,128,128]{2,1,0:T(8,128)(2,1)S(1)} %collective-permute-done.refs_12_), channel_id=1, source_target_pairs={{0,3},{1,2},{2,1},{3,0},{4,7},{5,6},{6,5},{7,4},{8,11},{9,10},{10,... | collective-permute-start | bytes 1769480 | tf_op jit(solution)/shard_map/ppermute | solution.py:394
  161.6 39.7 %collective-permute-start.7 = (bf16[24,128,128]{2,1,0:T(8,128)(2,1)S(1)}, bf16[24,128,128]{2,1,0:T(8,128)(2,1)S(1)}, u32[]{:S(2)}, u32[]{:S(2)}) collective-permute-start(bf16[24,128,128]{2,1,0:T(8,128)(2,1)S(1)} %collective-permute-done.6.refs_5_), channel_id=1, source_target_pairs={{0,7},{1,6},{2,5},{3,4},{4,3},{5,2},{6,1},{7,0},{8,15},{9,14},{10,... | collective-permute-start | bytes 2359304 | tf_op jit(solution)/shard_map/ppermute | solution.py:394
  176.7 34.2 %collective-permute-start.4 = (bf16[18,128,128]{2,1,0:T(8,128)(2,1)S(1)}, bf16[18,128,128]{2,1,0:T(8,128)(2,1)S(1)}, u32[]{:S(2)}, u32[]{:S(2)}) collective-permute-start(bf16[18,128,128]{2,1,0:T(8,128)(2,1)S(1)} %collective-permute-done.3.refs_13_), channel_id=1, source_target_pairs={{0,3},{1,2},{2,1},{3,0},{4,7},{5,6},{6,5},{7,4},{8,11},{9,10},{10,... | collective-permute-start | bytes 1769480 | tf_op jit(solution)/shard_map/ppermute | solution.py:394
  201.2 11.2 %collective-permute-start.17 = (bf16[18,128,128]{2,1,0:T(8,128)(2,1)S(1)}, bf16[18,128,128]{2,1,0:T(8,128)(2,1)S(1)}, u32[]{:S(2)}, u32[]{:S(2)}) collective-permute-start(bf16[18,128,128]{2,1,0:T(8,128)(2,1)S(1)} %collective-permute-done.1.refs_6_), channel_id=1, source_target_pairs={{0,1},{1,0},{2,3},{3,2},{4,5},{5,4},{6,7},{7,6},{8,9},{9,8},{10,11... | collective-permute-start | bytes 1769480 | tf_op jit(solution)/shard_map/ppermute | solution.py:394
  201.3 54.9 %collective-permute-start.19 = (bf16[24,128,128]{2,1,0:T(8,128)(2,1)S(1)}, bf16[24,128,128]{2,1,0:T(8,128)(2,1)S(1)}, u32[]{:S(2)}, u32[]{:S(2)}) collective-permute-start(bf16[24,128,128]{2,1,0:T(8,128)(2,1)S(1)} %collective-permute-done.7.refs_8_), channel_id=1, source_target_pairs={{0,1},{1,0},{2,3},{3,2},{4,5},{5,4},{6,7},{7,6},{8,9},{9,8},{10,11... | collective-permute-start | bytes 2359304 | tf_op jit(solution)/shard_map/ppermute | solution.py:394
  210.9 2.7 collective-permute-start.18
  210.9 17.7 %collective-permute-start.5 = (bf16[18,128,128]{2,1,0:T(8,128)(2,1)S(1)}, bf16[18,128,128]{2,1,0:T(8,128)(2,1)S(1)}, u32[]{:S(2)}, u32[]{:S(2)}) collective-permute-start(bf16[18,128,128]{2,1,0:T(8,128)(2,1)S(1)} %collective-permute-done.4.refs_7_), channel_id=1, source_target_pairs={{0,8},{1,9},{2,10},{3,11},{4,124},{5,125},{6,126},{7,127},{8,16},{... | collective-permute-start | bytes 1769480 | tf_op jit(solution)/shard_map/ppermute | solution.py:394
  212.4 28.8 %collective-permute-start.2 = (bf16[18,128,128]{2,1,0:T(8,128)(2,1)S(1)}, bf16[18,128,128]{2,1,0:T(8,128)(2,1)S(1)}, u32[]{:S(2)}, u32[]{:S(2)}) collective-permute-start(bf16[18,128,128]{2,1,0:T(8,128)(2,1)S(1)} %collective-permute-done.1.refs_6_), channel_id=1, source_target_pairs={{0,8},{1,9},{2,10},{3,11},{4,124},{5,125},{6,126},{7,127},{8,16},{... | collective-permute-start | bytes 1769480 | tf_op jit(solution)/shard_map/ppermute | solution.py:394
  212.5 41.4 %collective-permute-start.8 = (bf16[18,128,128]{2,1,0:T(8,128)(2,1)S(1)}, bf16[18,128,128]{2,1,0:T(8,128)(2,1)S(1)}, u32[]{:S(2)}, u32[]{:S(2)}) collective-permute-start(bf16[18,128,128]{2,1,0:T(8,128)(2,1)S(1)} %slice.20), channel_id=1, source_target_pairs={{0,8},{1,9},{2,10},{3,11},{4,124},{5,125},{6,126},{7,127},{8,16},{... | collective-permute-start | bytes 1769480 | tf_op jit(solution)/shard_map/ppermute | solution.py:394
  213.6 52.9 %collective-permute-start.12 = (bf16[18,128,128]{2,1,0:T(8,128)(2,1)S(1)}, bf16[18,128,128]{2,1,0:T(8,128)(2,1)S(1)}, u32[]{:S(2)}, u32[]{:S(2)}) collective-permute-start(bf16[18,128,128]{2,1,0:T(8,128)(2,1)S(1)} %collective-permute-done.refs_12_), channel_id=1, source_target_pairs={{0,8},{1,9},{2,10},{3,11},{4,124},{5,125},{6,126},{7,127},{8,16},{... | collective-permute-start | bytes 1769480 | tf_op jit(solution)/shard_map/ppermute | solution.py:394
  228.6 50.6 %collective-permute-start.13 = (bf16[18,128,128]{2,1,0:T(8,128)(2,1)S(1)}, bf16[18,128,128]{2,1,0:T(8,128)(2,1)S(1)}, u32[]{:S(2)}, u32[]{:S(2)}) collective-permute-start(bf16[18,128,128]{2,1,0:T(8,128)(2,1)S(1)} %collective-permute-done.3.refs_13_), channel_id=1, source_target_pairs={{0,8},{1,9},{2,10},{3,11},{4,124},{5,125},{6,126},{7,127},{8,16},{... | collective-permute-start | bytes 1769480 | tf_op jit(solution)/shard_map/ppermute | solution.py:394
  241.2 37.9 %collective-permute-start.10 = (bf16[18,128,128]{2,1,0:T(8,128)(2,1)S(1)}, bf16[18,128,128]{2,1,0:T(8,128)(2,1)S(1)}, u32[]{:S(2)}, u32[]{:S(2)}) collective-permute-start(bf16[18,128,128]{2,1,0:T(8,128)(2,1)S(1)} %collective-permute-done.5.refs_1_), channel_id=1, source_target_pairs={{0,1},{1,0},{2,3},{3,2},{4,5},{5,4},{6,7},{7,6},{8,9},{9,8},{10,11... | collective-permute-start | bytes 1769480 | tf_op jit(solution)/shard_map/ppermute | solution.py:394
  253.8 25.3 %collective-permute-start.9 = (bf16[18,128,128]{2,1,0:T(8,128)(2,1)S(1)}, bf16[18,128,128]{2,1,0:T(8,128)(2,1)S(1)}, u32[]{:S(2)}, u32[]{:S(2)}) collective-permute-start(bf16[18,128,128]{2,1,0:T(8,128)(2,1)S(1)} %collective-permute-done.2.refs_0_), channel_id=1, source_target_pairs={{0,1},{1,0},{2,3},{3,2},{4,5},{5,4},{6,7},{7,6},{8,9},{9,8},{10,11... | collective-permute-start | bytes 1769480 | tf_op jit(solution)/shard_map/ppermute | solution.py:394
  256.2 23.0 %collective-permute-start.11 = (bf16[18,128,128]{2,1,0:T(8,128)(2,1)S(1)}, bf16[18,128,128]{2,1,0:T(8,128)(2,1)S(1)}, u32[]{:S(2)}, u32[]{:S(2)}) collective-permute-start(bf16[18,128,128]{2,1,0:T(8,128)(2,1)S(1)} %collective-permute-done.8.refs_2_), channel_id=1, source_target_pairs={{0,1},{1,0},{2,3},{3,2},{4,5},{5,4},{6,7},{7,6},{8,9},{9,8},{10,11... | collective-permute-start | bytes 1769480 | tf_op jit(solution)/shard_map/ppermute | solution.py:394
  256.2 1.1 copy-start.1
where the time goes:
time: 293 us; the launch traced here: 292 us
  waiting for transfers between devices  217 us (74%)
  starting transfers between devices  33.7 us (12%)
  Pallas kernels  32.8 us (11%)
  local copies, waits for them, and re-layouts  4.07 us (1%)
  other arithmetic  4.03 us (1%)
    ppermute x21, waiting for transfers between devices, send(): return lax.ppermute(array, axes, pairs)  124 us
    all_to_all x1, waiting for transfers between devices, per_device(): lax.all_to_all(outgoing.reshape(device_count, C, width, width), ('gx', 'g...  93.8 us
    ppermute x21, starting transfers between devices, send(): return lax.ppermute(array, axes, pairs)  21.6 us
    pallas_call x1, Pallas kernels, purify_far(): pl.pallas_call(functools.partial(far_kernel, row_count, width, piece_star...  13.2 us
    all_to_all x1, starting transfers between devices, per_device(): lax.all_to_all(outgoing.reshape(device_count, C, width, width), ('gx', 'g...  12.1 us
    pallas_call x1, Pallas kernels, square_near(): pl.pallas_call(functools.partial(near_kernel, row_count, width, piece_sta...  9.01 us
    pallas_call x1, Pallas kernels, admit(): pl.pallas_call(functools.partial(admit_kernel, spans), out_shape=[jax.Sha...  7.09 us
  transfers between devices with their start and end apart: 22, of which 11 were waited for; matrix products, arithmetic and copies ran while one was open for 2% of the time, Pallas kernels for 3%

commit v1 on v0

--- a/solution.py
+++ b/solution.py
@@ -68,8 +68,9 @@
         if high > done:
             lax.fori_loop(done, high, place, 0)
             done = high
-        copies.append(pltpu.make_async_copy(own.at[pl.ds(low, high - low)], part_refs[i], sems.at[i]))
-        copies[-1].start()
+        copy = pltpu.make_async_copy(own.at[pl.ds(low, high - low)], part_refs[i], sems.at[i])
+        copy.start()
+        copies.append(copy)
     for copy in copies:
         copy.wait()
 
@@ -99,15 +100,15 @@
     return [w * 3 + n for w in wides for n in narrows]
 
 
-NEAR_PARTS = 6
-
-
-def near_count(part):
-    return len([q for q in reach(part) if q < NEAR_PARTS])
-
-
-def far_count(part):
-    return len(reach(part)) - near_count(part)
+FAR_PARTS = (6, 7)
+
+
+def near_of(part):
+    return [q for q in reach(part) if q not in FAR_PARTS]
+
+
+def far_of(part):
+    return [q for q in reach(part) if q in FAR_PARTS]
 
 
 def load_pieces(pieces, piece_starts, table, sems):
@@ -141,9 +142,9 @@
     for r in range(row_count):
         for k in range(near):
             left[r * width:(r + 1) * width, k * width:(k + 1) * width] = block(r, k)
-    left_far[...] = left[:, NEAR_PARTS * group:]
+    left_far[...] = lanes_of(left, FAR_PARTS, group)
     for part in range(9):
-        parts = [q for q in reach(part) if q < NEAR_PARTS]
+        parts = near_of(part)
         for i, q in enumerate(parts):
             for r in range(row_count):
                 for k in range(row_count):
@@ -162,10 +163,10 @@
     return pl.pallas_call(
         functools.partial(near_kernel, row_count, width, piece_starts, table_size),
         out_shape=[
-            pltpu.VMEM((near_count(part) * group, group), jnp.bfloat16) for part in range(9)
+            pltpu.VMEM((len(near_of(part)) * group, group), jnp.bfloat16) for part in range(9)
         ] + [
             pltpu.VMEM((9, group, group), jnp.float32),
-            pltpu.VMEM((group, (9 - NEAR_PARTS) * group), jnp.bfloat16),
+            pltpu.VMEM((group, len(FAR_PARTS) * group), jnp.bfloat16),
         ],
         in_specs=[pl.BlockSpec(memory_space=pltpu.SMEM)]
         + [pl.BlockSpec(memory_space=pl.ANY)] * len(pieces),
@@ -194,10 +195,9 @@
         copy.wait()
 
     for part in range(9):
-        parts = reach(part)
-        base = near_count(part)
-        far_base = sum(far_count(q) for q in range(part)) * group
-        for i, q in enumerate(parts[base:]):
+        parts = far_of(part)
+        far_base = sum(len(far_of(q)) for q in range(part)) * group
+        for i, q in enumerate(parts):
             for r in range(row_count):
                 for k in range(row_count):
                     low = far_base + (i * row_count + r) * width
@@ -205,10 +205,10 @@
                         pos_ref[(q * row_count + r) * near + part * row_count + k] - table_start
                     ]
         product = square_in[part]
-        if base < len(parts):
+        if parts:
             product = product + jnp.dot(
-                lanes_of(left, [q - NEAR_PARTS for q in parts[base:]], group),
-                grid[far_base:far_base + far_count(part) * group],
+                lanes_of(left, [FAR_PARTS.index(q) for q in parts], group),
+                grid[far_base:far_base + len(parts) * group],
                 preferred_element_type=jnp.float32,
             )
         square[part] = product
@@ -222,17 +222,16 @@
 
     blocks = out_ref.shape[0]
     for part in range(9):
-        parts = reach(part)
-        base = near_count(part)
-        far_base = sum(far_count(q) for q in range(part)) * group
+        parts = far_of(part)
+        far_base = sum(len(far_of(q)) for q in range(part)) * group
         product = jnp.dot(
-            lanes_of(square_b, parts[:base], group), near_grids[part][...],
+            lanes_of(square_b, near_of(part), group), near_grids[part][...],
             preferred_element_type=jnp.float32,
         )
-        if base < len(parts):
+        if parts:
             product = product + jnp.dot(
-                lanes_of(square_b, parts[base:], group),
-                grid[far_base:far_base + far_count(part) * group],
+                lanes_of(square_b, parts, group),
+                grid[far_base:far_base + len(parts) * group],
                 preferred_element_type=jnp.float32,
             )
         result = 3.0 * square[part] - 2.0 * product
@@ -266,7 +265,7 @@
         out_specs=pl.BlockSpec(memory_space=pl.ANY),
         scratch_shapes=[
             pltpu.VMEM((table_size + 1, width, width), jnp.bfloat16),
-            pltpu.VMEM((sum(far_count(part) for part in range(9)) * group, group), jnp.bfloat16),
+            pltpu.VMEM((sum(len(far_of(part)) for part in range(9)) * group, group), jnp.bfloat16),
             pltpu.VMEM((9, group, group), jnp.float32),
             pltpu.VMEM((group, span), jnp.bfloat16),
             pltpu.VMEM((blocks + 1, width, width), jnp.float32),
@@ -296,8 +295,9 @@
     lists = jnp.take(listing, rows, axis=0)
     list_x = lists // (narrow_count * row_count)
     list_y = lists // row_count % narrow_count
+    aside = list_y == (near_y ^ 1)[:, None]
     kind = jnp.where(
-        list_x == (near_x ^ 1)[:, None], 2, jnp.where(list_y == (near_y ^ 1)[:, None], 1, 0)
+        list_x == (near_x ^ 1)[:, None], jnp.where(aside, 2, 3), jnp.where(aside, 1, 0)
     )
     slot_ids = jnp.arange(slot_count, dtype=jnp.int32)
     key = kind * slot_count + slot_ids
@@ -337,7 +337,7 @@
     owners = ent_owner.reshape(device_count, held)
     places = ent_place.reshape(device_count, held)
 
-    my_owners = lax.dynamic_index_in_dim(owners, self_index, 0, False)
+    my_owners = lax.dynamic_slice(ent_owner, (self_index * held,), (held,))
     entry_ids = jnp.arange(held, dtype=jnp.int32)
     same = my_owners[:, None] == my_owners[None, :]
     my_ranks = jnp.sum(same & (entry_ids[None, :] < entry_ids[:, None]), axis=1)
@@ -369,17 +369,23 @@
 
     near_blocks = row_count * min(slot_count, 6 * row_count)
     corner_blocks = row_count * min(slot_count, 4 * row_count)
-    sizes = [blocks] * 6 + [near_blocks, near_blocks, corner_blocks]
-    starts = [sum(sizes[:i]) for i in range(9)]
-    zero_at = sum(sizes)
+    layout = [(part, blocks) for part in range(6)]
+    layout += [(8, corner_blocks), (6, near_blocks), (7, near_blocks)]
+    starts, zero_at = [0] * 9, 0
+    for part, size in layout:
+        starts[part], zero_at = zero_at, zero_at + size
+    far_start = starts[6]
     positions, out_slots, source = block_positions(neighbours, here_x, here_y, starts, zero_at)
 
-    cut = corner_blocks // 2
-    spans = ((0, cut), (cut, 2 * cut), (0, 2 * cut), (2 * cut, blocks))
+    cut = corner_blocks // 3
+    tail = blocks - 6 * row_count
+    spans = (
+        (0, cut), (cut, 2 * cut), (0, 2 * cut), (2 * cut, 3 * cut), (2 * cut, blocks), (tail, blocks)
+    )
     received, first, order, source, positions, out_slots = lax.optimization_barrier(
         (received, first, order, source, positions, out_slots)
     )
-    own_1, own_2, own_12, own_3 = admit(
+    own_1, own_2, own_12, own_3, own_34, own_4 = admit(
         density.reshape(blocks, width, width), received, first, order, source, spans
     )
 
@@ -406,17 +412,19 @@
         return (x + 2 if x % 2 == 0 else x - 2), y
 
     ring_across_1 = send(own_1, ring)
-    own_across_3 = send(own_3, across)
+    own_across_34 = send(own_34, across)
     ring_across_2 = send(own_2, ring)
-    own_chip_12 = send(own_12, chip)
-    own_chip_3 = send(own_3, chip)
+    ring_across_3 = send(own_3, ring)
     far_across_1 = send(ring_across_1, onward)
     ring_same_1 = send(ring_across_1, across)
-    ring_same_3 = send(own_across_3, ring)
     far_across_2 = send(ring_across_2, onward)
     ring_same_2 = send(ring_across_2, across)
-    ring_across_3 = send(own_3, ring)
+    ring_same_3 = send(own_across_34, ring)
+    far_across_3 = send(ring_across_3, onward)
+    ring_across_4 = send(own_4, ring)
     own_across_12 = send(own_12, across)
+    own_chip_12 = send(own_12, chip)
+    own_chip_34 = send(own_34, chip)
     far_same_1 = send(ring_same_1, onward)
     ring_chip_1 = send(ring_same_1, chip)
     far_same_2 = send(ring_same_2, onward)
@@ -428,18 +436,18 @@
     far_chip_3 = send(far_same_3, chip)
 
     near_pieces = [
-        (own_12, 0, 0), (own_3, 0, 2 * cut), (own_chip_12, 1, 0), (own_chip_3, 1, 2 * cut),
-        (own_across_12, 2, 0), (own_across_3, 2, 2 * cut),
+        (own_12, 0, 0), (own_34, 0, 2 * cut), (own_chip_12, 1, 0), (own_chip_34, 1, 2 * cut),
+        (own_across_12, 2, 0), (own_across_34, 2, 2 * cut),
         (ring_same_1, 3, 0), (ring_same_2, 3, cut), (ring_same_3, 3, 2 * cut),
         (ring_chip_1, 4, 0), (ring_chip_2, 4, cut), (ring_chip_3, 4, 2 * cut),
         (ring_across_1, 5, 0), (ring_across_2, 5, cut), (ring_across_3, 5, 2 * cut),
+        (ring_across_4, 5, tail),
+        (far_across_1, 8, 0), (far_across_2, 8, cut), (far_across_3, 8, 2 * cut),
     ]
     far_pieces = [
         (far_same_1, 6, 0), (far_same_2, 6, cut), (far_same_3, 6, 2 * cut),
         (far_chip_1, 7, 0), (far_chip_2, 7, cut), (far_chip_3, 7, 2 * cut),
-        (far_across_1, 8, 0), (far_across_2, 8, cut),
     ]
-    far_start = starts[NEAR_PARTS]
     carried = square_near(
         positions, [piece for piece, _, _ in near_pieces],
         [starts[part] + offset for _, part, offset in near_pieces],

time: 293 us -> 325 us (1.11)
  waiting for transfers between devices: 217 us -> 245 us
    ppermute x21 -> x23, waiting for transfers between devices: 124 us -> 152 us  [send(): return lax.ppermute(array, axes, pairs)]
    ppermute x21 -> x23, starting transfers between devices: 21.6 us -> 23.5 us  [send(): return lax.ppermute(array, axes, pairs)]
  transfers between devices with their start and end apart: 22 -> 24, of which waited for: 11 -> 12; matrix products, arithmetic and copies ran while one was open for 2% -> 2% of each run, Pallas kernels for 3% -> 4%
where the time goes in v1:
time: 325 us; the launch traced here: 324 us
  waiting for transfers between devices  245 us (75%)
  Pallas kernels  35.4 us (11%)
  starting transfers between devices  35.4 us (11%)
  other arithmetic  4.76 us (1%)
    ppermute x23, waiting for transfers between devices, send(): return lax.ppermute(array, axes, pairs)  152 us
    all_to_all x1, waiting for transfers between devices, per_device(): lax.all_to_all(outgoing.reshape(device_count, C, width, width), ('gx', 'g...  93.7 us
    ppermute x23, starting transfers between devices, send(): return lax.ppermute(array, axes, pairs)  23.5 us
    pallas_call x1, Pallas kernels, purify_far(): pl.pallas_call(functools.partial(far_kernel, row_count, width, piece_star...  12.9 us
    all_to_all x1, starting transfers between devices, per_device(): lax.all_to_all(outgoing.reshape(device_count, C, width, width), ('gx', 'g...  11.8 us
    pallas_call x1, Pallas kernels, square_near(): pl.pallas_call(functools.partial(near_kernel, row_count, width, piece_sta...  11.4 us
    pallas_call x1, Pallas kernels, admit(): pl.pallas_call(functools.partial(admit_kernel, spans), out_shape=[jax.Sha...  7.4 us
  transfers between devices with their start and end apart: 24, of which 12 were waited for; matrix products, arithmetic and copies ran while one was open for 2% of the time, Pallas kernels for 4%

profile of v1, /device:TPU:1, one launch (start us, length us, event | category | flops | bytes accessed | tf_op | source)
XLA Modules:
  0.0 324.3 jit_solution(11062933514314654082)
XLA Ops:
  0.0 0.8 dynamic_slice.3
  0.9 1.3 multiply_add_fusion.3.slots_ref
  2.2 3.6 %pack.1 = bf16[256,128,128]{2,1,0:T(8,128)(2,1)} custom-call(s32[96]{0:T(128)} %multiply_add_fusion.3.slots_ref, bf16[96,128,128]{2,1,0:T(8,128)(2,1)} %ent_ref.1), custom_call_target="tpu_custom_call" | custom-call | tf_op jit(solution)/shard_map/pack/pallas_call | solution.py:34
  5.9 11.8 %all-to-all-start = ((bf16[128,2,128,128]{3,2,1,0:T(8,128)(2,1)}), bf16[128,2,128,128]{3,2,1,0:T(8,128)(2,1)}, u32[]{:S(2)}, u32[]{:S(2)}) async-start(bf16[128,2,128,128]{3,2,1,0:T(8,128)(2,1)} %bitcast.8), calls=%async_computation | async-start | bytes 16777216 | tf_op jit(solution)/shard_map/all_to_all | solution.py:346
  18.2 0.6 gather_fusion
  21.3 0.7 select_reduce_fusion.4.source_ref
  21.9 0.6 convert_reduce_fusion.2.first_ref
  22.7 0.7 select_reduce_fusion.1.order_ref
  23.4 93.7 %all-to-all-done = bf16[128,2,128,128]{3,2,1,0:T(8,128)(2,1)} async-done(((bf16[128,2,128,128]{3,2,1,0:T(8,128)(2,1)}), bf16[128,2,128,128]{3,2,1,0:T(8,128)(2,1)}, u32[]{:S(2)}, u32[]{:S(2)}) %all-to-all-start) | async-done | bytes 8388640 | tf_op jit(solution)/shard_map/all_to_all | solution.py:346
  117.1 7.4 %admit.1 = (bf16[12,128,128]{2,1,0:T(8,128)(2,1)}, bf16[12,128,128]{2,1,0:T(8,128)(2,1)}, bf16[24,128,128]{2,1,0:T(8,128)(2,1)}, bf16[12,128,128]{2,1,0:T(8,128)...) custom-call(s32[61]{0:T(128)} %convert_reduce_fusion.2.first_ref, s32[256]{0:T(256)} %select_reduce_fusion.1.order_ref, ...), custom_call_target="tpu_custom_call" | custom-call | tf_op jit(solution)/shard_map/admit/pallas_call | solution.py:79
  124.5 6.1 %collective-permute-start.6 = (bf16[36,128,128]{2,1,0:T(8,128)(2,1)}, bf16[36,128,128]{2,1,0:T(8,128)(2,1)S(1)}, u32[]{:S(2)}, u32[]{:S(2)}) collective-permute-start(bf16[36,128,128]{2,1,0:T(8,128)(2,1)} %get-tuple-element.36.refs_1_), channel_id=1, source_target_pairs={{0,3},{1,2},{2,1},{3,0},{4,7},{5,6},{6,5},{7,4},{8,11},{9,10},{10,... | collective-permute-start | bytes 3538952 | tf_op jit(solution)/shard_map/ppermute | solution.py:400
  130.7 25.8 %collective-permute-done.6.refs_5_ = bf16[36,128,128]{2,1,0:T(8,128)(2,1)S(1)} collective-permute-done((bf16[36,128,128]{2,1,0:T(8,128)(2,1)}, bf16[36,128,128]{2,1,0:T(8,128)(2,1)S(1)}, u32[]{:S(2)}, u32[]{:S(2)}) %collective-permute-start.6) | collective-permute-done | bytes 1179680 | tf_op jit(solution)/shard_map/ppermute | solution.py:400
  156.4 3.0 collective-permute-start
  159.4 2.9 collective-permute-start.3
  162.4 32.2 %collective-permute-done.refs_12_ = bf16[12,128,128]{2,1,0:T(8,128)(2,1)S(1)} collective-permute-done((bf16[12,128,128]{2,1,0:T(8,128)(2,1)}, bf16[12,128,128]{2,1,0:T(8,128)(2,1)S(1)}, u32[]{:S(2)}, u32[]{:S(2)}) %collective-permute-start) | collective-permute-done | bytes 393248 | tf_op jit(solution)/shard_map/ppermute | solution.py:400
  194.6 0.9 collective-permute-start.1
  195.5 20.2 %collective-permute-done.3.refs_13_ = bf16[12,128,128]{2,1,0:T(8,128)(2,1)S(1)} collective-permute-done((bf16[12,128,128]{2,1,0:T(8,128)(2,1)}, bf16[12,128,128]{2,1,0:T(8,128)(2,1)S(1)}, u32[]{:S(2)}, u32[]{:S(2)}) %collective-permute-start.3) | collective-permute-done | bytes 393248 | tf_op jit(solution)/shard_map/ppermute | solution.py:400
  215.7 0.9 collective-permute-start.4
  216.6 6.6 %collective-permute-done.18.refs_14_ = bf16[12,128,128]{2,1,0:T(8,128)(2,1)S(1)} collective-permute-done((bf16[12,128,128]{2,1,0:T(8,128)(2,1)}, bf16[12,128,128]{2,1,0:T(8,128)(2,1)S(1)}, u32[]{:S(2)}, u32[]{:S(2)}) %collective-permute-start.18) | collective-permute-done | bytes 393248 | tf_op jit(solution)/shard_map/ppermute | solution.py:400
  223.2 1.5 collective-permute-start.20
  225.9 11.2 %collective-permute-done.20.refs_16_ = bf16[12,128,128]{2,1,0:T(8,128)(2,1)S(1)} collective-permute-done((bf16[12,128,128]{2,1,0:T(8,128)(2,1)S(1)}, bf16[12,128,128]{2,1,0:T(8,128)(2,1)S(1)}, u32[]{:S(2)}, u32[]{:S(2)}) %collective-permute-start.20) | collective-permute-done | bytes 393248 | tf_op jit(solution)/shard_map/ppermute | solution.py:400
  237.1 8.4 %collective-permute-done.21.refs_17_ = bf16[12,128,128]{2,1,0:T(8,128)(2,1)S(1)} collective-permute-done((bf16[12,128,128]{2,1,0:T(8,128)(2,1)S(1)}, bf16[12,128,128]{2,1,0:T(8,128)(2,1)S(1)}, u32[]{:S(2)}, u32[]{:S(2)}) %collective-permute-start.21) | collective-permute-done | bytes 393248 | tf_op jit(solution)/shard_map/ppermute | solution.py:400
  245.6 3.1 collective-permute-start.14
  248.7 26.4 %collective-permute-done.22.refs_18_ = bf16[12,128,128]{2,1,0:T(8,128)(2,1)S(1)} collective-permute-done((bf16[12,128,128]{2,1,0:T(8,128)(2,1)S(1)}, bf16[12,128,128]{2,1,0:T(8,128)(2,1)S(1)}, u32[]{:S(2)}, u32[]{:S(2)}) %collective-permute-start.22) | collective-permute-done | bytes 393248 | tf_op jit(solution)/shard_map/ppermute | solution.py:400
  275.0 0.9 collective-permute-start.17
  276.6 3.8 %collective-permute-done.15.refs_9_ = bf16[12,128,128]{2,1,0:T(8,128)(2,1)S(1)} collective-permute-done((bf16[12,128,128]{2,1,0:T(8,128)(2,1)S(1)}, bf16[12,128,128]{2,1,0:T(8,128)(2,1)S(1)}, u32[]{:S(2)}, u32[]{:S(2)}) %collective-permute-start.15) | collective-permute-done | bytes 393248 | tf_op jit(solution)/shard_map/ppermute | solution.py:400
  280.8 9.6 %collective-permute-done.5.refs_1_ = bf16[12,128,128]{2,1,0:T(8,128)(2,1)S(1)} collective-permute-done((bf16[12,128,128]{2,1,0:T(8,128)(2,1)S(1)}, bf16[12,128,128]{2,1,0:T(8,128)(2,1)S(1)}, u32[]{:S(2)}, u32[]{:S(2)}) %collective-permute-start.5) | collective-permute-done | bytes 393248 | tf_op jit(solution)/shard_map/ppermute | solution.py:400
  290.4 1.5 collective-permute-start.10
  291.9 6.9 %collective-permute-done.2.refs_0_ = bf16[12,128,128]{2,1,0:T(8,128)(2,1)S(1)} collective-permute-done((bf16[12,128,128]{2,1,0:T(8,128)(2,1)S(1)}, bf16[12,128,128]{2,1,0:T(8,128)(2,1)S(1)}, u32[]{:S(2)}, u32[]{:S(2)}) %collective-permute-start.2) | collective-permute-done | bytes 393248 | tf_op jit(solution)/shard_map/ppermute | solution.py:400
  298.8 0.9 collective-permute-start.9
  299.7 11.4 %square_near.1 = (bf16[2688,384]{1,0:T(8,128)(2,1)S(1)}, bf16[1536,384]{1,0:T(8,128)(2,1)S(1)}, bf16[1920,384]{1,0:T(8,128)(2,1)S(1)}, bf16[2304,384]{1,0:T(8,12...) custom-call(s32[729]{0:T(1024)S(1)} %reshape.493.pos_ref, ...), custom_call_target="tpu_custom_call" | custom-call | tf_op jit(solution)/shard_map/square_near/pallas_call | solution.py:163
  311.2 12.9 %purify_far.1 = f32[60,128,128]{2,1,0:T(8,128)} custom-call(s32[729]{0:T(1024)S(1)} %reshape.493.pos_ref, s32[81]{0:T(128)S(1)} %reshape.494.slot_ref, bf16[12,128,128]{2,1,0:T(8,128)(2,1)S(1)} %collective-permute-done.2.refs_0_, bf16[12,128,128]{2,1,0:T(8,128)(2,1)S(1)} %collective-permute-done.5.refs_1_, ...), custom_call_target="tpu_custom_call" | custom-call | tf_op jit(solution)/shard_map/purify_far/pallas_call | solution.py:257
  (77 shorter events, 5.4 us)
Async XLA Ops:
  5.9 11.9 %copy-start.2 = (s32[32,4,3,20]{0,1,3,2:T(4,128)S(1)}, s32[32,4,3,20]{0,1,3,2:T(4,128)}, u32[]{:S(2)}) copy-start(s32[32,4,3,20]{0,1,3,2:T(4,128)} %param.6) | copy-start | bytes 92164
  5.9 111.2 %all-to-all-start = ((bf16[128,2,128,128]{3,2,1,0:T(8,128)(2,1)}), bf16[128,2,128,128]{3,2,1,0:T(8,128)(2,1)}, u32[]{:S(2)}, u32[]{:S(2)}) async-start(bf16[128,2,128,128]{3,2,1,0:T(8,128)(2,1)} %bitcast.8), calls=%async_computation | async-start | bytes 16777216 | tf_op jit(solution)/shard_map/all_to_all | solution.py:346
  17.7 2.5 copy-start.3
  17.7 3.0 copy-start.4
  124.5 100.3 %copy-start = (bf16[36,128,128]{2,1,0:T(8,128)(2,1)S(1)}, bf16[36,128,128]{2,1,0:T(8,128)(2,1)}, u32[]{:S(2)}) copy-start(bf16[36,128,128]{2,1,0:T(8,128)(2,1)} %get-tuple-element.36.refs_1_) | copy-start | bytes 3538948
  124.5 101.0 %copy-start.1 = (bf16[24,128,128]{2,1,0:T(8,128)(2,1)S(1)}, bf16[24,128,128]{2,1,0:T(8,128)(2,1)}, u32[]{:S(2)}) copy-start(bf16[24,128,128]{2,1,0:T(8,128)(2,1)} %get-tuple-element.37.refs_0_) | copy-start | bytes 2359300
  124.5 31.9 %collective-permute-start.6 = (bf16[36,128,128]{2,1,0:T(8,128)(2,1)}, bf16[36,128,128]{2,1,0:T(8,128)(2,1)S(1)}, u32[]{:S(2)}, u32[]{:S(2)}) collective-permute-start(bf16[36,128,128]{2,1,0:T(8,128)(2,1)} %get-tuple-element.36.refs_1_), channel_id=1, source_target_pairs={{0,3},{1,2},{2,1},{3,0},{4,7},{5,6},{6,5},{7,4},{8,11},{9,10},{10,... | collective-permute-start | bytes 3538952 | tf_op jit(solution)/shard_map/ppermute | solution.py:400
  156.4 68.3 %collective-permute-start.7 = (bf16[36,128,128]{2,1,0:T(8,128)(2,1)S(1)}, bf16[36,128,128]{2,1,0:T(8,128)(2,1)S(1)}, u32[]{:S(2)}, u32[]{:S(2)}) collective-permute-start(bf16[36,128,128]{2,1,0:T(8,128)(2,1)S(1)} %collective-permute-done.6.refs_5_), channel_id=1, source_target_pairs={{0,7},{1,6},{2,5},{3,4},{4,3},{5,2},{6,1},{7,0},{8,15},{9,14},{10,... | collective-permute-start | bytes 3538952 | tf_op jit(solution)/shard_map/ppermute | solution.py:400
  156.4 38.2 %collective-permute-start = (bf16[12,128,128]{2,1,0:T(8,128)(2,1)}, bf16[12,128,128]{2,1,0:T(8,128)(2,1)S(1)}, u32[]{:S(2)}, u32[]{:S(2)}) collective-permute-start(bf16[12,128,128]{2,1,0:T(8,128)(2,1)} %get-tuple-element.34), channel_id=1, source_target_pairs={{0,7},{1,6},{2,5},{3,4},{4,3},{5,2},{6,1},{7,0},{8,15},{9,14},{10,... | collective-permute-start | bytes 1179656 | tf_op jit(solution)/shard_map/ppermute | solution.py:400
  159.4 65.4 %collective-permute-start.19 = (bf16[18,128,128]{2,1,0:T(8,128)(2,1)}, bf16[18,128,128]{2,1,0:T(8,128)(2,1)S(1)}, u32[]{:S(2)}, u32[]{:S(2)}) collective-permute-start(bf16[18,128,128]{2,1,0:T(8,128)(2,1)} %get-tuple-element.39), channel_id=1, source_target_pairs={{0,7},{1,6},{2,5},{3,4},{4,3},{5,2},{6,1},{7,0},{8,15},{9,14},{10,... | collective-permute-start | bytes 1769480 | tf_op jit(solution)/shard_map/ppermute | solution.py:400
  159.4 56.3 %collective-permute-start.3 = (bf16[12,128,128]{2,1,0:T(8,128)(2,1)}, bf16[12,128,128]{2,1,0:T(8,128)(2,1)S(1)}, u32[]{:S(2)}, u32[]{:S(2)}) collective-permute-start(bf16[12,128,128]{2,1,0:T(8,128)(2,1)} %get-tuple-element.35), channel_id=1, source_target_pairs={{0,7},{1,6},{2,5},{3,4},{4,3},{5,2},{6,1},{7,0},{8,15},{9,14},{10,... | collective-permute-start | bytes 1179656 | tf_op jit(solution)/shard_map/ppermute | solution.py:400
  162.3 60.8 %collective-permute-start.18 = (bf16[12,128,128]{2,1,0:T(8,128)(2,1)}, bf16[12,128,128]{2,1,0:T(8,128)(2,1)S(1)}, u32[]{:S(2)}, u32[]{:S(2)}) collective-permute-start(bf16[12,128,128]{2,1,0:T(8,128)(2,1)} %get-tuple-element.38), channel_id=1, source_target_pairs={{0,7},{1,6},{2,5},{3,4},{4,3},{5,2},{6,1},{7,0},{8,15},{9,14},{10,... | collective-permute-start | bytes 1179656 | tf_op jit(solution)/shard_map/ppermute | solution.py:400
  194.6 30.6 %collective-permute-start.1 = (bf16[12,128,128]{2,1,0:T(8,128)(2,1)S(1)}, bf16[12,128,128]{2,1,0:T(8,128)(2,1)S(1)}, u32[]{:S(2)}, u32[]{:S(2)}) collective-permute-start(bf16[12,128,128]{2,1,0:T(8,128)(2,1)S(1)} %collective-permute-done.refs_12_), channel_id=1, source_target_pairs={{0,3},{1,2},{2,1},{3,0},{4,7},{5,6},{6,5},{7,4},{8,11},{9,10},{10,... | collective-permute-start | bytes 1179656 | tf_op jit(solution)/shard_map/ppermute | solution.py:400
  215.7 9.8 %collective-permute-start.4 = (bf16[12,128,128]{2,1,0:T(8,128)(2,1)S(1)}, bf16[12,128,128]{2,1,0:T(8,128)(2,1)S(1)}, u32[]{:S(2)}, u32[]{:S(2)}) collective-permute-start(bf16[12,128,128]{2,1,0:T(8,128)(2,1)S(1)} %collective-permute-done.3.refs_13_), channel_id=1, source_target_pairs={{0,3},{1,2},{2,1},{3,0},{4,7},{5,6},{6,5},{7,4},{8,11},{9,10},{10,... | collective-permute-start | bytes 1179656 | tf_op jit(solution)/shard_map/ppermute | solution.py:400
  223.2 14.0 %collective-permute-start.20 = (bf16[12,128,128]{2,1,0:T(8,128)(2,1)S(1)}, bf16[12,128,128]{2,1,0:T(8,128)(2,1)S(1)}, u32[]{:S(2)}, u32[]{:S(2)}) collective-permute-start(bf16[12,128,128]{2,1,0:T(8,128)(2,1)S(1)} %collective-permute-done.refs_12_), channel_id=1, source_target_pairs={{0,8},{1,9},{2,10},{3,11},{4,124},{5,125},{6,126},{7,127},{8,16},{... | collective-permute-start | bytes 1179656 | tf_op jit(solution)/shard_map/ppermute | solution.py:400
  224.7 20.9 %collective-permute-start.21 = (bf16[12,128,128]{2,1,0:T(8,128)(2,1)S(1)}, bf16[12,128,128]{2,1,0:T(8,128)(2,1)S(1)}, u32[]{:S(2)}, u32[]{:S(2)}) collective-permute-start(bf16[12,128,128]{2,1,0:T(8,128)(2,1)S(1)} %collective-permute-done.3.refs_13_), channel_id=1, source_target_pairs={{0,8},{1,9},{2,10},{3,11},{4,124},{5,125},{6,126},{7,127},{8,16},{... | collective-permute-start | bytes 1179656 | tf_op jit(solution)/shard_map/ppermute | solution.py:400
  224.8 51.6 %collective-permute-start.13 = (bf16[36,128,128]{2,1,0:T(8,128)(2,1)S(1)}, bf16[36,128,128]{2,1,0:T(8,128)(2,1)S(1)}, u32[]{:S(2)}, u32[]{:S(2)}) collective-permute-start(bf16[36,128,128]{2,1,0:T(8,128)(2,1)S(1)} %copy-done), channel_id=1, source_target_pairs={{0,1},{1,0},{2,3},{3,2},{4,5},{5,4},{6,7},{7,6},{8,9},{9,8},{10,11... | collective-permute-start | bytes 3538952 | tf_op jit(solution)/shard_map/ppermute | solution.py:400
  225.2 50.7 %collective-permute-start.8 = (bf16[30,128,128]{2,1,0:T(8,128)(2,1)S(1)}, bf16[30,128,128]{2,1,0:T(8,128)(2,1)S(1)}, u32[]{:S(2)}, u32[]{:S(2)}) collective-permute-start(bf16[30,128,128]{2,1,0:T(8,128)(2,1)S(1)} %slice.20), channel_id=1, source_target_pairs={{0,8},{1,9},{2,10},{3,11},{4,124},{5,125},{6,126},{7,127},{8,16},{... | collective-permute-start | bytes 2949128 | tf_op jit(solution)/shard_map/ppermute | solution.py:400
  225.5 50.4 %collective-permute-start.12 = (bf16[24,128,128]{2,1,0:T(8,128)(2,1)S(1)}, bf16[24,128,128]{2,1,0:T(8,128)(2,1)S(1)}, u32[]{:S(2)}, u32[]{:S(2)}) collective-permute-start(bf16[24,128,128]{2,1,0:T(8,128)(2,1)S(1)} %copy-done.1), channel_id=1, source_target_pairs={{0,1},{1,0},{2,3},{3,2},{4,5},{5,4},{6,7},{7,6},{8,9},{9,8},{10,11... | collective-permute-start | bytes 2359304 | tf_op jit(solution)/shard_map/ppermute | solution.py:400
  237.1 37.9 %collective-permute-start.22 = (bf16[12,128,128]{2,1,0:T(8,128)(2,1)S(1)}, bf16[12,128,128]{2,1,0:T(8,128)(2,1)S(1)}, u32[]{:S(2)}, u32[]{:S(2)}) collective-permute-start(bf16[12,128,128]{2,1,0:T(8,128)(2,1)S(1)} %collective-permute-done.18.refs_14_), channel_id=1, source_target_pairs={{0,8},{1,9},{2,10},{3,11},{4,124},{5,125},{6,126},{7,127},{8,16},{... | collective-permute-start | bytes 1179656 | tf_op jit(solution)/shard_map/ppermute | solution.py:400
  245.6 30.9 %collective-permute-start.14 = (bf16[24,128,128]{2,1,0:T(8,128)(2,1)S(1)}, bf16[24,128,128]{2,1,0:T(8,128)(2,1)S(1)}, u32[]{:S(2)}, u32[]{:S(2)}) collective-permute-start(bf16[24,128,128]{2,1,0:T(8,128)(2,1)S(1)} %copy-done.1), channel_id=1, source_target_pairs={{0,3},{1,2},{2,1},{3,0},{4,7},{5,6},{6,5},{7,4},{8,11},{9,10},{10,... | collective-permute-start | bytes 2359304 | tf_op jit(solution)/shard_map/ppermute | solution.py:400
  275.0 24.7 %collective-permute-start.17 = (bf16[36,128,128]{2,1,0:T(8,128)(2,1)S(1)}, bf16[36,128,128]{2,1,0:T(8,128)(2,1)S(1)}, u32[]{:S(2)}, u32[]{:S(2)}) collective-permute-start(bf16[36,128,128]{2,1,0:T(8,128)(2,1)S(1)} %collective-permute-done.7.refs_8_), channel_id=1, source_target_pairs={{0,1},{1,0},{2,3},{3,2},{4,5},{5,4},{6,7},{7,6},{8,9},{9,8},{10,11... | collective-permute-start | bytes 3538952 | tf_op jit(solution)/shard_map/ppermute | solution.py:400
  275.9 35.3 %collective-permute-start.11 = (bf16[30,128,128]{2,1,0:T(8,128)(2,1)S(1)}, bf16[30,128,128]{2,1,0:T(8,128)(2,1)S(1)}, u32[]{:S(2)}, u32[]{:S(2)}) collective-permute-start(bf16[30,128,128]{2,1,0:T(8,128)(2,1)S(1)} %collective-permute-done.8.refs_2_), channel_id=1, source_target_pairs={{0,1},{1,0},{2,3},{3,2},{4,5},{5,4},{6,7},{7,6},{8,9},{9,8},{10,11... | collective-permute-start | bytes 2949128 | tf_op jit(solution)/shard_map/ppermute | solution.py:400
  276.0 4.4 %collective-permute-start.15 = (bf16[12,128,128]{2,1,0:T(8,128)(2,1)S(1)}, bf16[12,128,128]{2,1,0:T(8,128)(2,1)S(1)}, u32[]{:S(2)}, u32[]{:S(2)}) collective-permute-start(bf16[12,128,128]{2,1,0:T(8,128)(2,1)S(1)} %collective-permute-done.1.refs_6_), channel_id=1, source_target_pairs={{0,1},{1,0},{2,3},{3,2},{4,5},{5,4},{6,7},{7,6},{8,9},{9,8},{10,11... | collective-permute-start | bytes 1179656 | tf_op jit(solution)/shard_map/ppermute | solution.py:400
  276.5 13.9 %collective-permute-start.5 = (bf16[12,128,128]{2,1,0:T(8,128)(2,1)S(1)}, bf16[12,128,128]{2,1,0:T(8,128)(2,1)S(1)}, u32[]{:S(2)}, u32[]{:S(2)}) collective-permute-start(bf16[12,128,128]{2,1,0:T(8,128)(2,1)S(1)} %collective-permute-done.4.refs_7_), channel_id=1, source_target_pairs={{0,8},{1,9},{2,10},{3,11},{4,124},{5,125},{6,126},{7,127},{8,16},{... | collective-permute-start | bytes 1179656 | tf_op jit(solution)/shard_map/ppermute | solution.py:400
  276.5 22.3 %collective-permute-start.2 = (bf16[12,128,128]{2,1,0:T(8,128)(2,1)S(1)}, bf16[12,128,128]{2,1,0:T(8,128)(2,1)S(1)}, u32[]{:S(2)}, u32[]{:S(2)}) collective-permute-start(bf16[12,128,128]{2,1,0:T(8,128)(2,1)S(1)} %collective-permute-done.1.refs_6_), channel_id=1, source_target_pairs={{0,8},{1,9},{2,10},{3,11},{4,124},{5,125},{6,126},{7,127},{8,16},{... | collective-permute-start | bytes 1179656 | tf_op jit(solution)/shard_map/ppermute | solution.py:400
  280.4 19.4 %collective-permute-start.16 = (bf16[12,128,128]{2,1,0:T(8,128)(2,1)S(1)}, bf16[12,128,128]{2,1,0:T(8,128)(2,1)S(1)}, u32[]{:S(2)}, u32[]{:S(2)}) collective-permute-start(bf16[12,128,128]{2,1,0:T(8,128)(2,1)S(1)} %collective-permute-done.4.refs_7_), channel_id=1, source_target_pairs={{0,1},{1,0},{2,3},{3,2},{4,5},{5,4},{6,7},{7,6},{8,9},{9,8},{10,11... | collective-permute-start | bytes 1179656 | tf_op jit(solution)/shard_map/ppermute | solution.py:400
  290.4 20.8 %collective-permute-start.10 = (bf16[12,128,128]{2,1,0:T(8,128)(2,1)S(1)}, bf16[12,128,128]{2,1,0:T(8,128)(2,1)S(1)}, u32[]{:S(2)}, u32[]{:S(2)}) collective-permute-start(bf16[12,128,128]{2,1,0:T(8,128)(2,1)S(1)} %collective-permute-done.5.refs_1_), channel_id=1, source_target_pairs={{0,1},{1,0},{2,3},{3,2},{4,5},{5,4},{6,7},{7,6},{8,9},{9,8},{10,11... | collective-permute-start | bytes 1179656 | tf_op jit(solution)/shard_map/ppermute | solution.py:400
  298.8 12.4 %collective-permute-start.9 = (bf16[12,128,128]{2,1,0:T(8,128)(2,1)S(1)}, bf16[12,128,128]{2,1,0:T(8,128)(2,1)S(1)}, u32[]{:S(2)}, u32[]{:S(2)}) collective-permute-start(bf16[12,128,128]{2,1,0:T(8,128)(2,1)S(1)} %collective-permute-done.2.refs_0_), channel_id=1, source_target_pairs={{0,1},{1,0},{2,3},{3,2},{4,5},{5,4},{6,7},{7,6},{8,9},{9,8},{10,11... | collective-permute-start | bytes 1179656 | tf_op jit(solution)/shard_map/ppermute | solution.py:400

commit v2 on v1

--- a/solution.py
+++ b/solution.py
@@ -48,25 +48,45 @@
     )(slots, ent_blocks)
 
 
-def admit_kernel(spans, first_ref, order_ref, source_ref, density_ref, received_ref, *refs):
-    part_refs, own, sems = refs[: len(spans)], refs[len(spans)], refs[len(spans) + 1]
-
-    def add(j, total):
-        return total + received_ref[order_ref[j]].astype(jnp.float32)
-
-    def place(p, carry):
-        t = source_ref[p]
-        total = lax.fori_loop(
-            first_ref[t], first_ref[t + 1], add, density_ref[t].astype(jnp.float32)
-        )
-        own[p] = total.astype(own.dtype)
+def admit_kernel(spans, first_ref, order_ref, target_ref, source_ref, density_ref, received_ref, *refs):
+    part_refs = refs[: len(spans)]
+    density, received, total, own, load_sem, chunk_sems, sems = refs[len(spans):]
+    chunks = chunk_sems.shape[0]
+    size = received.shape[0] // chunks
+    density_load = pltpu.make_async_copy(density_ref, density, load_sem)
+    density_load.start()
+    loads = []
+    for c in range(chunks):
+        rows = pl.ds(c * size, size)
+        load = pltpu.make_async_copy(received_ref.at[rows], received.at[rows], chunk_sems.at[c])
+        load.start()
+        loads.append(load)
+    density_load.wait()
+
+    def begin(p, carry):
+        total[p] = density[source_ref[p]].astype(jnp.float32)
+        return carry
+
+    lax.fori_loop(0, own.shape[0], begin, 0)
+
+    def add(j, carry):
+        p = target_ref[j]
+        total[p] = total[p] + received[order_ref[j]].astype(jnp.float32)
+        return carry
+
+    for c in range(chunks):
+        loads[c].wait()
+        lax.fori_loop(first_ref[c], first_ref[c + 1], add, 0)
+
+    def finish(p, carry):
+        own[p] = total[p].astype(own.dtype)
         return carry
 
     copies = []
     done = 0
     for i, (low, high) in enumerate(spans):
         if high > done:
-            lax.fori_loop(done, high, place, 0)
+            lax.fori_loop(done, high, finish, 0)
             done = high
         copy = pltpu.make_async_copy(own.at[pl.ds(low, high - low)], part_refs[i], sems.at[i])
         copy.start()
@@ -75,22 +95,30 @@
         copy.wait()
 
 
-def admit(density, received, first, order, source, spans):
+RECEIVE_CHUNKS = 4
+
+
+def admit(density, received, first, order, target, source, spans):
     return pl.pallas_call(
         functools.partial(admit_kernel, spans),
         out_shape=[
             jax.ShapeDtypeStruct((high - low,) + density.shape[1:], density.dtype)
             for low, high in spans
         ],
-        in_specs=[pl.BlockSpec(memory_space=pltpu.SMEM)] * 3
-        + [pl.BlockSpec(memory_space=pltpu.VMEM)] * 2,
+        in_specs=[pl.BlockSpec(memory_space=pltpu.SMEM)] * 4
+        + [pl.BlockSpec(memory_space=pl.ANY)] * 2,
         out_specs=[pl.BlockSpec(memory_space=pl.ANY)] * len(spans),
         scratch_shapes=[
             pltpu.VMEM(density.shape, density.dtype),
+            pltpu.VMEM(received.shape, received.dtype),
+            pltpu.VMEM(density.shape, jnp.float32),
+            pltpu.VMEM(density.shape, density.dtype),
+            pltpu.SemaphoreType.DMA,
+            pltpu.SemaphoreType.DMA((RECEIVE_CHUNKS,)),
             pltpu.SemaphoreType.DMA((len(spans),)),
         ],
         name="admit",
-    )(first, order, source, density, received)
+    )(first, order, target, source, density, received)
 
 
 def reach(part):
@@ -100,11 +128,32 @@
     return [w * 3 + n for w in wides for n in narrows]
 
 
-FAR_PARTS = (6, 7)
+FAR_PARTS = (6, 7, 8)
 
 
 def near_of(part):
     return [q for q in reach(part) if q not in FAR_PARTS]
+
+
+def middle_of(part):
+    return [q for q in reach(part) if q // 3 == 1]
+
+
+def inner_of(part):
+    return [q for q in reach(part) if q // 3 == 0]
+
+
+def masked(product, pos_ref, row_count, width, part, zero_at):
+    near = 9 * row_count
+    rows = []
+    for r in range(row_count):
+        row = []
+        for k in range(row_count):
+            listed = pos_ref[r * near + part * row_count + k] != zero_at
+            block = product[r * width:(r + 1) * width, k * width:(k + 1) * width]
+            row.append(jnp.where(listed, block, 0.0).astype(jnp.bfloat16))
+        rows.append(jnp.concatenate(row, axis=1))
+    return jnp.concatenate(rows, axis=0)
 
 
 def far_of(part):
@@ -125,10 +174,11 @@
     return jnp.concatenate([ref[:, q * group:(q + 1) * group] for q in parts], axis=1)
 
 
-def near_kernel(row_count, width, piece_starts, table_size, pos_ref, *refs):
+def near_kernel(row_count, width, piece_starts, table_size, zero_at, pos_ref, *refs):
     pieces = refs[: len(piece_starts)]
     outs = refs[len(piece_starts):]
-    grids, (square, left_far, table, left, sems) = outs[:9], outs[9:]
+    inner_grids, (square, cube, left_far, table, left, square_b, sems) = outs[:9], outs[9:16]
+    outer_grids = outs[16:]
     near = 9 * row_count
     group = row_count * width
     copies = load_pieces(pieces, piece_starts, table, sems)
@@ -146,37 +196,62 @@
     for part in range(9):
         parts = near_of(part)
         for i, q in enumerate(parts):
+            count = len(inner_of(part))
+            ref, at = (inner_grids[part], i) if i < count else (outer_grids[part], i - count)
             for r in range(row_count):
                 for k in range(row_count):
-                    low = (i * row_count + r) * width
-                    grids[part][low:low + width, k * width:(k + 1) * width] = block(
+                    low = (at * row_count + r) * width
+                    ref[low:low + width, k * width:(k + 1) * width] = block(
                         q * row_count + r, part * row_count + k
                     )
-        square[part] = jnp.dot(
-            lanes_of(left, parts, group), grids[part][...], preferred_element_type=jnp.float32
+        product = jnp.dot(
+            lanes_of(left, inner_of(part), group), inner_grids[part][...],
+            preferred_element_type=jnp.float32,
         )
-
-
-def square_near(positions, pieces, piece_starts, table_size, row_count, width):
+        if middle_of(part):
+            product = product + jnp.dot(
+                lanes_of(left, middle_of(part), group), outer_grids[part][...],
+                preferred_element_type=jnp.float32,
+            )
+        square[part] = product
+        if part // 3 == 1:
+            lanes = slice((part - 3) * group, (part - 2) * group)
+            square_b[:, lanes] = masked(product, pos_ref, row_count, width, part, zero_at)
+    for part in range(6):
+        product = jnp.dot(
+            lanes_of(square_b, [q - 3 for q in middle_of(part)], group), outer_grids[part][...],
+            preferred_element_type=jnp.float32,
+        )
+        if part < 3:
+            cube[part] = product
+        else:
+            square[part] = 3.0 * square[part] - 2.0 * product
+
+
+def square_near(positions, pieces, piece_starts, table_size, zero_at, row_count, width):
     group = row_count * width
     span = 9 * group
     return pl.pallas_call(
-        functools.partial(near_kernel, row_count, width, piece_starts, table_size),
+        functools.partial(near_kernel, row_count, width, piece_starts, table_size, zero_at),
         out_shape=[
-            pltpu.VMEM((len(near_of(part)) * group, group), jnp.bfloat16) for part in range(9)
+            pltpu.VMEM((len(inner_of(part)) * group, group), jnp.bfloat16) for part in range(9)
         ] + [
             pltpu.VMEM((9, group, group), jnp.float32),
+            pltpu.VMEM((3, group, group), jnp.float32),
             pltpu.VMEM((group, len(FAR_PARTS) * group), jnp.bfloat16),
         ],
         in_specs=[pl.BlockSpec(memory_space=pltpu.SMEM)]
         + [pl.BlockSpec(memory_space=pl.ANY)] * len(pieces),
-        out_specs=[pl.BlockSpec(memory_space=pltpu.VMEM)] * 11,
+        out_specs=[pl.BlockSpec(memory_space=pltpu.VMEM)] * 12,
         scratch_shapes=[
             pltpu.VMEM((table_size + 1, width, width), jnp.bfloat16),
             pltpu.VMEM((group, span), jnp.bfloat16),
+            pltpu.VMEM((group, 3 * group), jnp.bfloat16),
             pltpu.SemaphoreType.DMA((len(pieces),)),
-        ],
-        compiler_params=pltpu.CompilerParams(vmem_limit_bytes=20 << 20),
+        ] + [
+            pltpu.VMEM((len(middle_of(part)) * group, group), jnp.bfloat16) for part in range(6)
+        ],
+        compiler_params=pltpu.CompilerParams(vmem_limit_bytes=24 << 20),
         name="square_near",
     )(positions, *pieces)
 
@@ -184,8 +259,8 @@
 def far_kernel(row_count, width, piece_starts, table_start, table_size, pos_ref, slot_ref, *refs):
     pieces = refs[: len(piece_starts)]
     outs = refs[len(piece_starts):]
-    near_grids = outs[:9]
-    square_in, left, out_ref, table, grid, square, square_b, staged, sems, out_sem = outs[9:]
+    inner_grids = outs[:9]
+    square_in, cube_in, left, out_ref, table, grid, square, square_b, staged, sems, out_sem = outs[9:]
     near = 9 * row_count
     group = row_count * width
     zero_at = table_start + table_size
@@ -194,7 +269,8 @@
     for copy in copies:
         copy.wait()
 
-    for part in range(9):
+    outer = [0, 1, 2, 6, 7, 8]
+    for index, part in enumerate(outer):
         parts = far_of(part)
         far_base = sum(len(far_of(q)) for q in range(part)) * group
         for i, q in enumerate(parts):
@@ -204,37 +280,35 @@
                     grid[low:low + width, k * width:(k + 1) * width] = table[
                         pos_ref[(q * row_count + r) * near + part * row_count + k] - table_start
                     ]
-        product = square_in[part]
-        if parts:
-            product = product + jnp.dot(
-                lanes_of(left, [FAR_PARTS.index(q) for q in parts], group),
-                grid[far_base:far_base + len(parts) * group],
-                preferred_element_type=jnp.float32,
-            )
-        square[part] = product
-        for r in range(row_count):
-            for k in range(row_count):
-                listed = pos_ref[r * near + part * row_count + k] != zero_at
-                low = part * group + k * width
-                square_b[r * width:(r + 1) * width, low:low + width] = jnp.where(
-                    listed, product[r * width:(r + 1) * width, k * width:(k + 1) * width], 0.0
-                ).astype(jnp.bfloat16)
+        product = square_in[part] + jnp.dot(
+            lanes_of(left, [FAR_PARTS.index(q) for q in parts], group),
+            grid[far_base:far_base + len(parts) * group],
+            preferred_element_type=jnp.float32,
+        )
+        square[index] = product
+        square_b[:, index * group:(index + 1) * group] = masked(
+            product, pos_ref, row_count, width, part, zero_at
+        )
 
     blocks = out_ref.shape[0]
     for part in range(9):
         parts = far_of(part)
         far_base = sum(len(far_of(q)) for q in range(part)) * group
         product = jnp.dot(
-            lanes_of(square_b, near_of(part), group), near_grids[part][...],
-            preferred_element_type=jnp.float32,
+            lanes_of(square_b, [outer.index(q) for q in inner_of(part)], group),
+            inner_grids[part][...], preferred_element_type=jnp.float32,
         )
         if parts:
             product = product + jnp.dot(
-                lanes_of(square_b, parts, group),
+                lanes_of(square_b, [outer.index(q) for q in parts], group),
                 grid[far_base:far_base + len(parts) * group],
                 preferred_element_type=jnp.float32,
             )
-        result = 3.0 * square[part] - 2.0 * product
+            if part < 3:
+                product = product + cube_in[part]
+            result = 3.0 * square[outer.index(part)] - 2.0 * product
+        else:
+            result = square_in[part] - 2.0 * product
         for r in range(row_count):
             for k in range(row_count):
                 slot = slot_ref[r * near + part * row_count + k]
@@ -252,7 +326,6 @@
     row_count, slot_count, width,
 ):
     group = row_count * width
-    span = 9 * group
     blocks = row_count * slot_count
     return pl.pallas_call(
         functools.partial(
@@ -266,8 +339,8 @@
         scratch_shapes=[
             pltpu.VMEM((table_size + 1, width, width), jnp.bfloat16),
             pltpu.VMEM((sum(len(far_of(part)) for part in range(9)) * group, group), jnp.bfloat16),
-            pltpu.VMEM((9, group, group), jnp.float32),
-            pltpu.VMEM((group, span), jnp.bfloat16),
+            pltpu.VMEM((6, group, group), jnp.float32),
+            pltpu.VMEM((group, 6 * group), jnp.bfloat16),
             pltpu.VMEM((blocks + 1, width, width), jnp.float32),
             pltpu.SemaphoreType.DMA((len(pieces),)),
             pltpu.SemaphoreType.DMA,
@@ -337,7 +410,7 @@
     owners = ent_owner.reshape(device_count, held)
     places = ent_place.reshape(device_count, held)
 
-    my_owners = lax.dynamic_slice(ent_owner, (self_index * held,), (held,))
+    my_owners = lax.dynamic_index_in_dim(owners, self_index, 0, False)
     entry_ids = jnp.arange(held, dtype=jnp.int32)
     same = my_owners[:, None] == my_owners[None, :]
     my_ranks = jnp.sum(same & (entry_ids[None, :] < entry_ids[:, None]), axis=1)
@@ -355,38 +428,43 @@
     )
     slot_place = jnp.sum(jnp.where(picked, places[:, :, None], 0), axis=1).reshape(-1)
     slot_used = jnp.any(picked, axis=1).reshape(-1)
-    slot_place = jnp.where(slot_used, slot_place, blocks)
     slot_ids = jnp.arange(device_count * C, dtype=jnp.int32)
-    ahead = (slot_place[:, None] > slot_place[None, :]) | (
-        (slot_place[:, None] == slot_place[None, :]) & (slot_ids[:, None] > slot_ids[None, :])
-    )
-    sorted_at = jnp.sum(ahead, axis=1)
-    order = jnp.sum(
-        jnp.where(sorted_at[None, :] == slot_ids[:, None], slot_ids[None, :], 0), axis=1
+    used = slot_used.astype(jnp.int32)
+    ahead = jnp.sum(
+        jnp.where(slot_ids[None, :] < slot_ids[:, None], used[None, :], 0), axis=1
+    )
+    chosen = slot_used[None, :] & (ahead[None, :] == slot_ids[:, None])
+    order = jnp.sum(jnp.where(chosen, slot_ids[None, :], 0), axis=1).astype(jnp.int32)
+    bounds = jnp.arange(RECEIVE_CHUNKS + 1, dtype=jnp.int32) * (device_count * C // RECEIVE_CHUNKS)
+    first = jnp.sum(
+        jnp.where(slot_ids[None, :] < bounds[:, None], used[None, :], 0), axis=1
     ).astype(jnp.int32)
-    target_ids = jnp.arange(blocks + 1, dtype=jnp.int32)
-    first = jnp.sum(slot_place[None, :] < target_ids[:, None], axis=1).astype(jnp.int32)
 
     near_blocks = row_count * min(slot_count, 6 * row_count)
     corner_blocks = row_count * min(slot_count, 4 * row_count)
     layout = [(part, blocks) for part in range(6)]
-    layout += [(8, corner_blocks), (6, near_blocks), (7, near_blocks)]
+    layout += [(6, near_blocks), (7, near_blocks), (8, corner_blocks)]
     starts, zero_at = [0] * 9, 0
     for part, size in layout:
         starts[part], zero_at = zero_at, zero_at + size
     far_start = starts[6]
     positions, out_slots, source = block_positions(neighbours, here_x, here_y, starts, zero_at)
+    targets = jnp.arange(blocks, dtype=jnp.int32)
+    slot_target = jnp.sum(
+        jnp.where(source[None, :] == slot_place[:, None], targets[None, :], 0), axis=1
+    )
+    target = jnp.sum(jnp.where(chosen, slot_target[None, :], 0), axis=1).astype(jnp.int32)
 
     cut = corner_blocks // 3
     tail = blocks - 6 * row_count
     spans = (
-        (0, cut), (cut, 2 * cut), (0, 2 * cut), (2 * cut, 3 * cut), (2 * cut, blocks), (tail, blocks)
-    )
-    received, first, order, source, positions, out_slots = lax.optimization_barrier(
-        (received, first, order, source, positions, out_slots)
-    )
-    own_1, own_2, own_12, own_3, own_34, own_4 = admit(
-        density.reshape(blocks, width, width), received, first, order, source, spans
+        (0, cut), (cut, 2 * cut), (0, 2 * cut), (2 * cut, 3 * cut), (2 * cut, tail), (tail, blocks)
+    )
+    received, first, order, target, source, positions, out_slots = lax.optimization_barrier(
+        (received, first, order, target, source, positions, out_slots)
+    )
+    own_1, own_2, own_12, own_3, own_34a, own_34b = admit(
+        density.reshape(blocks, width, width), received, first, order, target, source, spans
     )
 
     axes = ("gx", "gy")
@@ -412,46 +490,53 @@
         return (x + 2 if x % 2 == 0 else x - 2), y
 
     ring_across_1 = send(own_1, ring)
-    own_across_34 = send(own_34, across)
+    own_across_a = send(own_34a, across)
+    own_across_b = send(own_34b, across)
     ring_across_2 = send(own_2, ring)
     ring_across_3 = send(own_3, ring)
     far_across_1 = send(ring_across_1, onward)
     ring_same_1 = send(ring_across_1, across)
     far_across_2 = send(ring_across_2, onward)
     ring_same_2 = send(ring_across_2, across)
-    ring_same_3 = send(own_across_34, ring)
+    ring_same_a = send(own_across_a, ring)
+    ring_same_b = send(own_across_b, ring)
     far_across_3 = send(ring_across_3, onward)
-    ring_across_4 = send(own_4, ring)
+    ring_across_4 = send(own_34b, ring)
     own_across_12 = send(own_12, across)
     own_chip_12 = send(own_12, chip)
-    own_chip_34 = send(own_34, chip)
+    own_chip_a = send(own_34a, chip)
+    own_chip_b = send(own_34b, chip)
     far_same_1 = send(ring_same_1, onward)
     ring_chip_1 = send(ring_same_1, chip)
     far_same_2 = send(ring_same_2, onward)
     ring_chip_2 = send(ring_same_2, chip)
-    far_same_3 = send(ring_same_3[:near_blocks - 2 * cut], onward)
-    ring_chip_3 = send(ring_same_3, chip)
+    far_same_a = send(ring_same_a, onward)
+    ring_chip_a = send(ring_same_a, chip)
+    far_same_b = send(ring_same_b[:near_blocks - tail], onward)
+    ring_chip_b = send(ring_same_b, chip)
     far_chip_1 = send(far_same_1, chip)
     far_chip_2 = send(far_same_2, chip)
-    far_chip_3 = send(far_same_3, chip)
+    far_chip_a = send(far_same_a, chip)
+    far_chip_b = send(far_same_b, chip)
 
     near_pieces = [
-        (own_12, 0, 0), (own_34, 0, 2 * cut), (own_chip_12, 1, 0), (own_chip_34, 1, 2 * cut),
-        (own_across_12, 2, 0), (own_across_34, 2, 2 * cut),
-        (ring_same_1, 3, 0), (ring_same_2, 3, cut), (ring_same_3, 3, 2 * cut),
-        (ring_chip_1, 4, 0), (ring_chip_2, 4, cut), (ring_chip_3, 4, 2 * cut),
+        (own_12, 0, 0), (own_34a, 0, 2 * cut), (own_34b, 0, tail),
+        (own_chip_12, 1, 0), (own_chip_a, 1, 2 * cut), (own_chip_b, 1, tail),
+        (own_across_12, 2, 0), (own_across_a, 2, 2 * cut), (own_across_b, 2, tail),
+        (ring_same_1, 3, 0), (ring_same_2, 3, cut), (ring_same_a, 3, 2 * cut), (ring_same_b, 3, tail),
+        (ring_chip_1, 4, 0), (ring_chip_2, 4, cut), (ring_chip_a, 4, 2 * cut), (ring_chip_b, 4, tail),
         (ring_across_1, 5, 0), (ring_across_2, 5, cut), (ring_across_3, 5, 2 * cut),
         (ring_across_4, 5, tail),
-        (far_across_1, 8, 0), (far_across_2, 8, cut), (far_across_3, 8, 2 * cut),
     ]
     far_pieces = [
-        (far_same_1, 6, 0), (far_same_2, 6, cut), (far_same_3, 6, 2 * cut),
-        (far_chip_1, 7, 0), (far_chip_2, 7, cut), (far_chip_3, 7, 2 * cut),
+        (far_same_1, 6, 0), (far_same_2, 6, cut), (far_same_a, 6, 2 * cut), (far_same_b, 6, tail),
+        (far_chip_1, 7, 0), (far_chip_2, 7, cut), (far_chip_a, 7, 2 * cut), (far_chip_b, 7, tail),
+        (far_across_1, 8, 0), (far_across_2, 8, cut), (far_across_3, 8, 2 * cut),
     ]
     carried = square_near(
         positions, [piece for piece, _, _ in near_pieces],
         [starts[part] + offset for _, part, offset in near_pieces],
-        far_start, row_count, width,
+        far_start, zero_at, row_count, width,
     )
     purified = purify_far(
         positions, out_slots, [piece for piece, _, _ in far_pieces],

time: 325 us -> 284 us (0.87)
  waiting for transfers between devices: 245 us -> 194 us
  starting transfers between devices: 35.4 us -> 42.8 us
  local copies, waits for them, and re-layouts: 3.07 us -> 6.48 us
    ppermute x23 -> x29, waiting for transfers between devices: 152 us -> 100 us  [send(): return lax.ppermute(array, axes, pairs)]
    ppermute x23 -> x29, starting transfers between devices: 23.5 us -> 30.9 us  [send(): return lax.ppermute(array, axes, pairs)]
  transfers between devices with their start and end apart: 24 -> 30, of which waited for: 12 -> 15; matrix products, arithmetic and copies ran while one was open for 2% -> 2% of each run, Pallas kernels for 4% -> 4%
where the time goes in v2:
time: 284 us
  waiting for transfers between devices  194 us (68%)
  starting transfers between devices  42.8 us (15%)
  Pallas kernels  36.2 us (13%)
  local copies, waits for them, and re-layouts  6.48 us (2%)
  other arithmetic  3.67 us (1%)
    ppermute x29, waiting for transfers between devices, send(): return lax.ppermute(array, axes, pairs)  100 us
    all_to_all x1, waiting for transfers between devices, per_device(): lax.all_to_all(outgoing.reshape(device_count, C, width, width), ('gx', 'g...  93.9 us
    ppermute x29, starting transfers between devices, send(): return lax.ppermute(array, axes, pairs)  30.9 us
    pallas_call x1, Pallas kernels, square_near(): pl.pallas_call(functools.partial(near_kernel, row_count, width, piece_sta...  12.6 us
    pallas_call x1, Pallas kernels, purify_far(): pl.pallas_call(functools.partial(far_kernel, row_count, width, piece_star...  12.3 us
    all_to_all x1, starting transfers between devices, per_device(): lax.all_to_all(outgoing.reshape(device_count, C, width, width), ('gx', 'g...  11.9 us
    pallas_call x1, Pallas kernels, admit(): pl.pallas_call(functools.partial(admit_kernel, spans), out_shape=[jax.Sha...  7.81 us
  transfers between devices with their start and end apart: 30, of which 15 were waited for; matrix products, arithmetic and copies ran while one was open for 2% of the time, Pallas kernels for 4%

profile of v2, /device:TPU:1, one launch (start us, length us, event | category | flops | bytes accessed | tf_op | source)
XLA Modules:
  0.0 284.0 jit_solution(3810935260223368999)
XLA Ops:
  1.6 3.5 %pack.1 = bf16[256,128,128]{2,1,0:T(8,128)(2,1)} custom-call(s32[96]{0:T(128)} %multiply_add_fusion.3.slots_ref, bf16[96,128,128]{2,1,0:T(8,128)(2,1)} %ent_ref.1), custom_call_target="tpu_custom_call" | custom-call | tf_op jit(solution)/shard_map/pack/pallas_call | solution.py:34
  5.1 11.9 %all-to-all-start = ((bf16[128,2,128,128]{3,2,1,0:T(8,128)(2,1)}), bf16[128,2,128,128]{3,2,1,0:T(8,128)(2,1)}, u32[]{:S(2)}, u32[]{:S(2)}) async-start(bf16[128,2,128,128]{3,2,1,0:T(8,128)(2,1)} %bitcast.12), calls=%async_computation | async-start | bytes 16777216 | tf_op jit(solution)/shard_map/all_to_all | solution.py:419
  22.5 93.9 %all-to-all-done = bf16[128,2,128,128]{3,2,1,0:T(8,128)(2,1)} async-done(((bf16[128,2,128,128]{3,2,1,0:T(8,128)(2,1)}), bf16[128,2,128,128]{3,2,1,0:T(8,128)(2,1)}, u32[]{:S(2)}, u32[]{:S(2)}) %all-to-all-start) | async-done | bytes 8388640 | tf_op jit(solution)/shard_map/all_to_all | solution.py:419
  116.4 7.8 %admit.1 = (bf16[12,128,128]{2,1,0:T(8,128)(2,1)}, bf16[12,128,128]{2,1,0:T(8,128)(2,1)}, bf16[24,128,128]{2,1,0:T(8,128)(2,1)}, bf16[12,128,128]{2,1,0:T(8,128)...) custom-call(s32[5]{0:T(128)} %select_reduce_fusion.8.first_ref, s32[256]{0:T(256)} %get-tuple-element.33.order_ref, ...), custom_call_target="tpu_custom_call" | custom-call | tf_op jit(solution)/shard_map/admit/pallas_call | solution.py:102
  124.2 3.2 %collective-permute-start = (bf16[12,128,128]{2,1,0:T(8,128)(2,1)}, bf16[12,128,128]{2,1,0:T(8,128)(2,1)S(1)}, u32[]{:S(2)}, u32[]{:S(2)}) collective-permute-start(bf16[12,128,128]{2,1,0:T(8,128)(2,1)} %get-tuple-element.37), channel_id=1, source_target_pairs={{0,7},{1,6},{2,5},{3,4},{4,3},{5,2},{6,1},{7,0},{8,15},{9,14},{10,... | collective-permute-start | bytes 1179656 | tf_op jit(solution)/shard_map/ppermute | solution.py:478
  127.6 4.5 %collective-permute-start.6 = (bf16[18,128,128]{2,1,0:T(8,128)(2,1)}, bf16[18,128,128]{2,1,0:T(8,128)(2,1)S(1)}, u32[]{:S(2)}, u32[]{:S(2)}) collective-permute-start(bf16[18,128,128]{2,1,0:T(8,128)(2,1)} %get-tuple-element.39.refs_1_), channel_id=1, source_target_pairs={{0,3},{1,2},{2,1},{3,0},{4,7},{5,6},{6,5},{7,4},{8,11},{9,10},{10,... | collective-permute-start | bytes 1769480 | tf_op jit(solution)/shard_map/ppermute | solution.py:478
  132.8 4.6 %collective-permute-done.refs_17_ = bf16[12,128,128]{2,1,0:T(8,128)(2,1)S(1)} collective-permute-done((bf16[12,128,128]{2,1,0:T(8,128)(2,1)}, bf16[12,128,128]{2,1,0:T(8,128)(2,1)S(1)}, u32[]{:S(2)}, u32[]{:S(2)}) %collective-permute-start) | collective-permute-done | bytes 393248 | tf_op jit(solution)/shard_map/ppermute | solution.py:478
  138.3 7.5 %collective-permute-done.3.refs_18_ = bf16[12,128,128]{2,1,0:T(8,128)(2,1)S(1)} collective-permute-done((bf16[12,128,128]{2,1,0:T(8,128)(2,1)}, bf16[12,128,128]{2,1,0:T(8,128)(2,1)S(1)}, u32[]{:S(2)}, u32[]{:S(2)}) %collective-permute-start.3) | collective-permute-done | bytes 393248 | tf_op jit(solution)/shard_map/ppermute | solution.py:478
  146.7 7.5 %collective-permute-done.18.refs_19_ = bf16[12,128,128]{2,1,0:T(8,128)(2,1)S(1)} collective-permute-done((bf16[12,128,128]{2,1,0:T(8,128)(2,1)}, bf16[12,128,128]{2,1,0:T(8,128)(2,1)S(1)}, u32[]{:S(2)}, u32[]{:S(2)}) %collective-permute-start.18) | collective-permute-done | bytes 393248 | tf_op jit(solution)/shard_map/ppermute | solution.py:478
  154.9 2.1 collective-permute-start.28
  157.9 2.4 collective-permute-start.23
  160.3 1.7 collective-permute-start.4
  162.0 9.3 %collective-permute-done.28.refs_20_ = bf16[18,128,128]{2,1,0:T(8,128)(2,1)S(1)} collective-permute-done((bf16[18,128,128]{2,1,0:T(8,128)(2,1)}, bf16[18,128,128]{2,1,0:T(8,128)(2,1)S(1)}, u32[]{:S(2)}, u32[]{:S(2)}) %collective-permute-start.28) | collective-permute-done | bytes 589856 | tf_op jit(solution)/shard_map/ppermute | solution.py:478
  171.3 2.3 collective-permute-start.7
  173.6 13.6 %collective-permute-done.1.refs_9_ = bf16[12,128,128]{2,1,0:T(8,128)(2,1)S(1)} collective-permute-done((bf16[12,128,128]{2,1,0:T(8,128)(2,1)S(1)}, bf16[12,128,128]{2,1,0:T(8,128)(2,1)S(1)}, u32[]{:S(2)}, u32[]{:S(2)}) %collective-permute-start.1) | collective-permute-done | bytes 393248 | tf_op jit(solution)/shard_map/ppermute | solution.py:478
  187.3 1.5 collective-permute-start.16
  188.8 6.0 %collective-permute-done.4.refs_10_ = bf16[12,128,128]{2,1,0:T(8,128)(2,1)S(1)} collective-permute-done((bf16[12,128,128]{2,1,0:T(8,128)(2,1)S(1)}, bf16[12,128,128]{2,1,0:T(8,128)(2,1)S(1)}, u32[]{:S(2)}, u32[]{:S(2)}) %collective-permute-start.4) | collective-permute-done | bytes 393248 | tf_op jit(solution)/shard_map/ppermute | solution.py:478
  194.8 1.5 collective-permute-start.17
  196.3 2.3 collective-permute-start.10
  198.9 2.2 collective-permute-done.16.refs_8_
  201.5 8.3 %collective-permute-done.17.refs_9_ = bf16[12,128,128]{2,1,0:T(8,128)(2,1)S(1)} collective-permute-done((bf16[12,128,128]{2,1,0:T(8,128)(2,1)S(1)}, bf16[12,128,128]{2,1,0:T(8,128)(2,1)S(1)}, u32[]{:S(2)}, u32[]{:S(2)}) %collective-permute-start.17) | collective-permute-done | bytes 393248 | tf_op jit(solution)/shard_map/ppermute | solution.py:478
  209.9 3.1 %collective-permute-done.10.refs_12_ = bf16[18,128,128]{2,1,0:T(8,128)(2,1)S(1)} collective-permute-done((bf16[18,128,128]{2,1,0:T(8,128)(2,1)S(1)}, bf16[18,128,128]{2,1,0:T(8,128)(2,1)S(1)}, u32[]{:S(2)}, u32[]{:S(2)}) %collective-permute-start.10) | collective-permute-done | bytes 589856 | tf_op jit(solution)/shard_map/ppermute | solution.py:478
  213.6 9.8 %collective-permute-done.2.refs_0_ = bf16[12,128,128]{2,1,0:T(8,128)(2,1)S(1)} collective-permute-done((bf16[12,128,128]{2,1,0:T(8,128)(2,1)S(1)}, bf16[12,128,128]{2,1,0:T(8,128)(2,1)S(1)}, u32[]{:S(2)}, u32[]{:S(2)}) %collective-permute-start.2) | collective-permute-done | bytes 393248 | tf_op jit(solution)/shard_map/ppermute | solution.py:478
  223.5 12.6 %collective-permute-done.8.refs_2_ = bf16[18,128,128]{2,1,0:T(8,128)(2,1)S(1)} collective-permute-done((bf16[18,128,128]{2,1,0:T(8,128)(2,1)S(1)}, bf16[18,128,128]{2,1,0:T(8,128)(2,1)S(1)}, u32[]{:S(2)}, u32[]{:S(2)}) %collective-permute-start.8) | collective-permute-done | bytes 589856 | tf_op jit(solution)/shard_map/ppermute | solution.py:478
  236.1 2.1 collective-permute-start.14
  238.2 6.3 %collective-permute-done.5.refs_1_ = bf16[12,128,128]{2,1,0:T(8,128)(2,1)S(1)} collective-permute-done((bf16[12,128,128]{2,1,0:T(8,128)(2,1)S(1)}, bf16[12,128,128]{2,1,0:T(8,128)(2,1)S(1)}, u32[]{:S(2)}, u32[]{:S(2)}) %collective-permute-start.5) | collective-permute-done | bytes 393248 | tf_op jit(solution)/shard_map/ppermute | solution.py:478
  244.5 8.4 %collective-permute-done.11.refs_3_ = bf16[12,128,128]{2,1,0:T(8,128)(2,1)S(1)} collective-permute-done((bf16[12,128,128]{2,1,0:T(8,128)(2,1)S(1)}, bf16[12,128,128]{2,1,0:T(8,128)(2,1)S(1)}, u32[]{:S(2)}, u32[]{:S(2)}) %collective-permute-start.11) | collective-permute-done | bytes 393248 | tf_op jit(solution)/shard_map/ppermute | solution.py:478
  252.9 2.1 collective-permute-start.12
  255.6 1.1 copy-done
  256.7 1.1 copy-done.1
  258.8 12.6 %square_near.1 = (bf16[1152,384]{1,0:T(8,128)(2,1)S(1)}, bf16[768,384]{1,0:T(8,128)(2,1)S(1)}, bf16[768,384]{1,0:T(8,128)(2,1)S(1)}, bf16[1152,384]{1,0:T(8,128)...) custom-call(s32[729]{0:T(1024)S(1)} %reshape.487.pos_ref, ...), custom_call_target="tpu_custom_call" | custom-call | tf_op jit(solution)/shard_map/square_near/pallas_call | solution.py:234
  271.5 12.3 %purify_far.1 = f32[60,128,128]{2,1,0:T(8,128)} custom-call(s32[729]{0:T(1024)S(1)} %reshape.487.pos_ref, s32[81]{0:T(128)S(1)} %reshape.488.slot_ref, bf16[12,128,128]{2,1,0:T(8,128)(2,1)S(1)} %collective-permute-done.2.refs_0_, bf16[12,128,128]{2,1,0:T(8,128)(2,1)S(1)} %collective-permute-done.5.refs_1_, ...), custom_call_target="tpu_custom_call" | custom-call | tf_op jit(solution)/shard_map/purify_far/pallas_call | solution.py:330
  (93 shorter events, 13.9 us)
Async XLA Ops:
  5.1 14.7 %copy-start.4 = (s32[12288]{0:T(1024)S(1)}, s32[12288]{0:T(1024)}, u32[]{:S(2)}) copy-start(s32[12288]{0:T(1024)} %param.9) | copy-start | bytes 147460
  5.1 111.3 %all-to-all-start = ((bf16[128,2,128,128]{3,2,1,0:T(8,128)(2,1)}), bf16[128,2,128,128]{3,2,1,0:T(8,128)(2,1)}, u32[]{:S(2)}, u32[]{:S(2)}) async-start(bf16[128,2,128,128]{3,2,1,0:T(8,128)(2,1)} %bitcast.12), calls=%async_computation | async-start | bytes 16777216 | tf_op jit(solution)/shard_map/all_to_all | solution.py:419
  20.8 95.7 %copy-start.5 = (s32[60]{0:T(128)}, s32[60]{0:T(128)S(1)}, u32[]{:S(2)}) copy-start(s32[60]{0:T(128)S(1)} %select_reduce_fusion.7.source_ref) | copy-start | bytes 724
  124.2 13.2 %collective-permute-start = (bf16[12,128,128]{2,1,0:T(8,128)(2,1)}, bf16[12,128,128]{2,1,0:T(8,128)(2,1)S(1)}, u32[]{:S(2)}, u32[]{:S(2)}) collective-permute-start(bf16[12,128,128]{2,1,0:T(8,128)(2,1)} %get-tuple-element.37), channel_id=1, source_target_pairs={{0,7},{1,6},{2,5},{3,4},{4,3},{5,2},{6,1},{7,0},{8,15},{9,14},{10,... | collective-permute-start | bytes 1179656 | tf_op jit(solution)/shard_map/ppermute | solution.py:478
  127.5 18.4 %collective-permute-start.3 = (bf16[12,128,128]{2,1,0:T(8,128)(2,1)}, bf16[12,128,128]{2,1,0:T(8,128)(2,1)S(1)}, u32[]{:S(2)}, u32[]{:S(2)}) collective-permute-start(bf16[12,128,128]{2,1,0:T(8,128)(2,1)} %get-tuple-element.38), channel_id=1, source_target_pairs={{0,7},{1,6},{2,5},{3,4},{4,3},{5,2},{6,1},{7,0},{8,15},{9,14},{10,... | collective-permute-start | bytes 1179656 | tf_op jit(solution)/shard_map/ppermute | solution.py:478
  127.6 27.3 %collective-permute-start.6 = (bf16[18,128,128]{2,1,0:T(8,128)(2,1)}, bf16[18,128,128]{2,1,0:T(8,128)(2,1)S(1)}, u32[]{:S(2)}, u32[]{:S(2)}) collective-permute-start(bf16[18,128,128]{2,1,0:T(8,128)(2,1)} %get-tuple-element.39.refs_1_), channel_id=1, source_target_pairs={{0,3},{1,2},{2,1},{3,0},{4,7},{5,6},{6,5},{7,4},{8,11},{9,10},{10,... | collective-permute-start | bytes 1769480 | tf_op jit(solution)/shard_map/ppermute | solution.py:478
  132.1 22.1 %collective-permute-start.18 = (bf16[12,128,128]{2,1,0:T(8,128)(2,1)}, bf16[12,128,128]{2,1,0:T(8,128)(2,1)S(1)}, u32[]{:S(2)}, u32[]{:S(2)}) collective-permute-start(bf16[12,128,128]{2,1,0:T(8,128)(2,1)} %get-tuple-element.41), channel_id=1, source_target_pairs={{0,7},{1,6},{2,5},{3,4},{4,3},{5,2},{6,1},{7,0},{8,15},{9,14},{10,... | collective-permute-start | bytes 1179656 | tf_op jit(solution)/shard_map/ppermute | solution.py:478
  132.8 25.1 %collective-permute-start.9 = (bf16[18,128,128]{2,1,0:T(8,128)(2,1)}, bf16[18,128,128]{2,1,0:T(8,128)(2,1)S(1)}, u32[]{:S(2)}, u32[]{:S(2)}) collective-permute-start(bf16[18,128,128]{2,1,0:T(8,128)(2,1)} %get-tuple-element.40.refs_2_), channel_id=1, source_target_pairs={{0,3},{1,2},{2,1},{3,0},{4,7},{5,6},{6,5},{7,4},{8,11},{9,10},{10,... | collective-permute-start | bytes 1769480 | tf_op jit(solution)/shard_map/ppermute | solution.py:478
  137.4 22.8 %collective-permute-start.21 = (bf16[18,128,128]{2,1,0:T(8,128)(2,1)}, bf16[18,128,128]{2,1,0:T(8,128)(2,1)S(1)}, u32[]{:S(2)}, u32[]{:S(2)}) collective-permute-start(bf16[18,128,128]{2,1,0:T(8,128)(2,1)} %get-tuple-element.39.refs_1_), channel_id=1, source_target_pairs={{0,1},{1,0},{2,3},{3,2},{4,5},{5,4},{6,7},{7,6},{8,9},{9,8},{10,11... | collective-permute-start | bytes 1769480 | tf_op jit(solution)/shard_map/ppermute | solution.py:478
  145.8 14.4 %collective-permute-start.22 = (bf16[18,128,128]{2,1,0:T(8,128)(2,1)}, bf16[18,128,128]{2,1,0:T(8,128)(2,1)S(1)}, u32[]{:S(2)}, u32[]{:S(2)}) collective-permute-start(bf16[18,128,128]{2,1,0:T(8,128)(2,1)} %get-tuple-element.40.refs_2_), channel_id=1, source_target_pairs={{0,1},{1,0},{2,3},{3,2},{4,5},{5,4},{6,7},{7,6},{8,9},{9,8},{10,11... | collective-permute-start | bytes 1769480 | tf_op jit(solution)/shard_map/ppermute | solution.py:478
  154.3 42.0 %collective-permute-start.20 = (bf16[24,128,128]{2,1,0:T(8,128)(2,1)}, bf16[24,128,128]{2,1,0:T(8,128)(2,1)S(1)}, u32[]{:S(2)}, u32[]{:S(2)}) collective-permute-start(bf16[24,128,128]{2,1,0:T(8,128)(2,1)} %get-tuple-element.42.refs_0_), channel_id=1, source_target_pairs={{0,1},{1,0},{2,3},{3,2},{4,5},{5,4},{6,7},{7,6},{8,9},{9,8},{10,11... | collective-permute-start | bytes 2359304 | tf_op jit(solution)/shard_map/ppermute | solution.py:478
  154.9 16.4 %collective-permute-start.28 = (bf16[18,128,128]{2,1,0:T(8,128)(2,1)}, bf16[18,128,128]{2,1,0:T(8,128)(2,1)S(1)}, u32[]{:S(2)}, u32[]{:S(2)}) collective-permute-start(bf16[18,128,128]{2,1,0:T(8,128)(2,1)} %get-tuple-element.40.refs_2_), channel_id=1, source_target_pairs={{0,7},{1,6},{2,5},{3,4},{4,3},{5,2},{6,1},{7,0},{8,15},{9,14},{10,... | collective-permute-start | bytes 1769480 | tf_op jit(solution)/shard_map/ppermute | solution.py:478
  157.9 40.7 %collective-permute-start.23 = (bf16[24,128,128]{2,1,0:T(8,128)(2,1)}, bf16[24,128,128]{2,1,0:T(8,128)(2,1)S(1)}, u32[]{:S(2)}, u32[]{:S(2)}) collective-permute-start(bf16[24,128,128]{2,1,0:T(8,128)(2,1)} %get-tuple-element.42.refs_0_), channel_id=1, source_target_pairs={{0,3},{1,2},{2,1},{3,0},{4,7},{5,6},{6,5},{7,4},{8,11},{9,10},{10,... | collective-permute-start | bytes 2359304 | tf_op jit(solution)/shard_map/ppermute | solution.py:478
  160.3 27.0 %collective-permute-start.1 = (bf16[12,128,128]{2,1,0:T(8,128)(2,1)S(1)}, bf16[12,128,128]{2,1,0:T(8,128)(2,1)S(1)}, u32[]{:S(2)}, u32[]{:S(2)}) collective-permute-start(bf16[12,128,128]{2,1,0:T(8,128)(2,1)S(1)} %collective-permute-done.refs_17_), channel_id=1, source_target_pairs={{0,3},{1,2},{2,1},{3,0},{4,7},{5,6},{6,5},{7,4},{8,11},{9,10},{10,... | collective-permute-start | bytes 1179656 | tf_op jit(solution)/shard_map/ppermute | solution.py:478
  160.3 34.5 %collective-permute-start.4 = (bf16[12,128,128]{2,1,0:T(8,128)(2,1)S(1)}, bf16[12,128,128]{2,1,0:T(8,128)(2,1)S(1)}, u32[]{:S(2)}, u32[]{:S(2)}) collective-permute-start(bf16[12,128,128]{2,1,0:T(8,128)(2,1)S(1)} %collective-permute-done.3.refs_18_), channel_id=1, source_target_pairs={{0,3},{1,2},{2,1},{3,0},{4,7},{5,6},{6,5},{7,4},{8,11},{9,10},{10,... | collective-permute-start | bytes 1179656 | tf_op jit(solution)/shard_map/ppermute | solution.py:478
  171.3 38.6 %collective-permute-start.7 = (bf16[18,128,128]{2,1,0:T(8,128)(2,1)S(1)}, bf16[18,128,128]{2,1,0:T(8,128)(2,1)S(1)}, u32[]{:S(2)}, u32[]{:S(2)}) collective-permute-start(bf16[18,128,128]{2,1,0:T(8,128)(2,1)S(1)} %collective-permute-done.6.refs_7_), channel_id=1, source_target_pairs={{0,7},{1,6},{2,5},{3,4},{4,3},{5,2},{6,1},{7,0},{8,15},{9,14},{10,... | collective-permute-start | bytes 1769480 | tf_op jit(solution)/shard_map/ppermute | solution.py:478
  187.3 13.9 %collective-permute-start.16 = (bf16[12,128,128]{2,1,0:T(8,128)(2,1)S(1)}, bf16[12,128,128]{2,1,0:T(8,128)(2,1)S(1)}, u32[]{:S(2)}, u32[]{:S(2)}) collective-permute-start(bf16[12,128,128]{2,1,0:T(8,128)(2,1)S(1)} %collective-permute-done.refs_17_), channel_id=1, source_target_pairs={{0,8},{1,9},{2,10},{3,11},{4,124},{5,125},{6,126},{7,127},{8,16},{... | collective-permute-start | bytes 1179656 | tf_op jit(solution)/shard_map/ppermute | solution.py:478
  194.8 15.1 %collective-permute-start.17 = (bf16[12,128,128]{2,1,0:T(8,128)(2,1)S(1)}, bf16[12,128,128]{2,1,0:T(8,128)(2,1)S(1)}, u32[]{:S(2)}, u32[]{:S(2)}) collective-permute-start(bf16[12,128,128]{2,1,0:T(8,128)(2,1)S(1)} %collective-permute-done.3.refs_18_), channel_id=1, source_target_pairs={{0,8},{1,9},{2,10},{3,11},{4,124},{5,125},{6,126},{7,127},{8,16},{... | collective-permute-start | bytes 1179656 | tf_op jit(solution)/shard_map/ppermute | solution.py:478
  196.3 16.7 %collective-permute-start.10 = (bf16[18,128,128]{2,1,0:T(8,128)(2,1)S(1)}, bf16[18,128,128]{2,1,0:T(8,128)(2,1)S(1)}, u32[]{:S(2)}, u32[]{:S(2)}) collective-permute-start(bf16[18,128,128]{2,1,0:T(8,128)(2,1)S(1)} %collective-permute-done.9.refs_8_), channel_id=1, source_target_pairs={{0,7},{1,6},{2,5},{3,4},{4,3},{5,2},{6,1},{7,0},{8,15},{9,14},{10,... | collective-permute-start | bytes 1769480 | tf_op jit(solution)/shard_map/ppermute | solution.py:478
  198.6 14.7 %collective-permute-start.24 = (bf16[12,128,128]{2,1,0:T(8,128)(2,1)S(1)}, bf16[12,128,128]{2,1,0:T(8,128)(2,1)S(1)}, u32[]{:S(2)}, u32[]{:S(2)}) collective-permute-start(bf16[12,128,128]{2,1,0:T(8,128)(2,1)S(1)} %collective-permute-done.1.refs_9_), channel_id=1, source_target_pairs={{0,1},{1,0},{2,3},{3,2},{4,5},{5,4},{6,7},{7,6},{8,9},{9,8},{10,11... | collective-permute-start | bytes 1179656 | tf_op jit(solution)/shard_map/ppermute | solution.py:478
  201.1 12.4 %collective-permute-start.25 = (bf16[12,128,128]{2,1,0:T(8,128)(2,1)S(1)}, bf16[12,128,128]{2,1,0:T(8,128)(2,1)S(1)}, u32[]{:S(2)}, u32[]{:S(2)}) collective-permute-start(bf16[12,128,128]{2,1,0:T(8,128)(2,1)S(1)} %collective-permute-done.4.refs_10_), channel_id=1, source_target_pairs={{0,1},{1,0},{2,3},{3,2},{4,5},{5,4},{6,7},{7,6},{8,9},{9,8},{10,11... | collective-permute-start | bytes 1179656 | tf_op jit(solution)/shard_map/ppermute | solution.py:478
  209.9 13.6 %collective-permute-start.2 = (bf16[12,128,128]{2,1,0:T(8,128)(2,1)S(1)}, bf16[12,128,128]{2,1,0:T(8,128)(2,1)S(1)}, u32[]{:S(2)}, u32[]{:S(2)}) collective-permute-start(bf16[12,128,128]{2,1,0:T(8,128)(2,1)S(1)} %collective-permute-done.1.refs_9_), channel_id=1, source_target_pairs={{0,8},{1,9},{2,10},{3,11},{4,124},{5,125},{6,126},{7,127},{8,16},{... | collective-permute-start | bytes 1179656 | tf_op jit(solution)/shard_map/ppermute | solution.py:478
  209.9 26.2 %collective-permute-start.8 = (bf16[18,128,128]{2,1,0:T(8,128)(2,1)S(1)}, bf16[18,128,128]{2,1,0:T(8,128)(2,1)S(1)}, u32[]{:S(2)}, u32[]{:S(2)}) collective-permute-start(bf16[18,128,128]{2,1,0:T(8,128)(2,1)S(1)} %collective-permute-done.7.refs_11_), channel_id=1, source_target_pairs={{0,8},{1,9},{2,10},{3,11},{4,124},{5,125},{6,126},{7,127},{8,16},{... | collective-permute-start | bytes 1769480 | tf_op jit(solution)/shard_map/ppermute | solution.py:478
  213.0 42.1 %collective-permute-start.26 = (bf16[18,128,128]{2,1,0:T(8,128)(2,1)S(1)}, bf16[18,128,128]{2,1,0:T(8,128)(2,1)S(1)}, u32[]{:S(2)}, u32[]{:S(2)}) collective-permute-start(bf16[18,128,128]{2,1,0:T(8,128)(2,1)S(1)} %collective-permute-done.7.refs_11_), channel_id=1, source_target_pairs={{0,1},{1,0},{2,3},{3,2},{4,5},{5,4},{6,7},{7,6},{8,9},{9,8},{10,11... | collective-permute-start | bytes 1769480 | tf_op jit(solution)/shard_map/ppermute | solution.py:478
  213.4 41.7 %collective-permute-start.27 = (bf16[18,128,128]{2,1,0:T(8,128)(2,1)S(1)}, bf16[18,128,128]{2,1,0:T(8,128)(2,1)S(1)}, u32[]{:S(2)}, u32[]{:S(2)}) collective-permute-start(bf16[18,128,128]{2,1,0:T(8,128)(2,1)S(1)} %collective-permute-done.10.refs_12_), channel_id=1, source_target_pairs={{0,1},{1,0},{2,3},{3,2},{4,5},{5,4},{6,7},{7,6},{8,9},{9,8},{10,11... | collective-permute-start | bytes 1769480 | tf_op jit(solution)/shard_map/ppermute | solution.py:478
  213.5 31.0 %collective-permute-start.5 = (bf16[12,128,128]{2,1,0:T(8,128)(2,1)S(1)}, bf16[12,128,128]{2,1,0:T(8,128)(2,1)S(1)}, u32[]{:S(2)}, u32[]{:S(2)}) collective-permute-start(bf16[12,128,128]{2,1,0:T(8,128)(2,1)S(1)} %collective-permute-done.4.refs_10_), channel_id=1, source_target_pairs={{0,8},{1,9},{2,10},{3,11},{4,124},{5,125},{6,126},{7,127},{8,16},{... | collective-permute-start | bytes 1179656 | tf_op jit(solution)/shard_map/ppermute | solution.py:478
  223.5 29.5 %collective-permute-start.11 = (bf16[12,128,128]{2,1,0:T(8,128)(2,1)S(1)}, bf16[12,128,128]{2,1,0:T(8,128)(2,1)S(1)}, u32[]{:S(2)}, u32[]{:S(2)}) collective-permute-start(bf16[12,128,128]{2,1,0:T(8,128)(2,1)S(1)} %slice.20), channel_id=1, source_target_pairs={{0,8},{1,9},{2,10},{3,11},{4,124},{5,125},{6,126},{7,127},{8,16},{... | collective-permute-start | bytes 1179656 | tf_op jit(solution)/shard_map/ppermute | solution.py:478
  236.1 35.4 %collective-permute-start.14 = (bf16[18,128,128]{2,1,0:T(8,128)(2,1)S(1)}, bf16[18,128,128]{2,1,0:T(8,128)(2,1)S(1)}, u32[]{:S(2)}, u32[]{:S(2)}) collective-permute-start(bf16[18,128,128]{2,1,0:T(8,128)(2,1)S(1)} %collective-permute-done.8.refs_2_), channel_id=1, source_target_pairs={{0,1},{1,0},{2,3},{3,2},{4,5},{5,4},{6,7},{7,6},{8,9},{9,8},{10,11... | collective-permute-start | bytes 1769480 | tf_op jit(solution)/shard_map/ppermute | solution.py:478
  244.5 26.9 %collective-permute-start.19 = (bf16[12,128,128]{2,1,0:T(8,128)(2,1)S(1)}, bf16[12,128,128]{2,1,0:T(8,128)(2,1)S(1)}, u32[]{:S(2)}, u32[]{:S(2)}) collective-permute-start(bf16[12,128,128]{2,1,0:T(8,128)(2,1)S(1)} %collective-permute-done.18.refs_19_), channel_id=1, source_target_pairs={{0,8},{1,9},{2,10},{3,11},{4,124},{5,125},{6,126},{7,127},{8,16},{... | collective-permute-start | bytes 1179656 | tf_op jit(solution)/shard_map/ppermute | solution.py:478
  252.9 18.5 %collective-permute-start.12 = (bf16[12,128,128]{2,1,0:T(8,128)(2,1)S(1)}, bf16[12,128,128]{2,1,0:T(8,128)(2,1)S(1)}, u32[]{:S(2)}, u32[]{:S(2)}) collective-permute-start(bf16[12,128,128]{2,1,0:T(8,128)(2,1)S(1)} %collective-permute-done.2.refs_0_), channel_id=1, source_target_pairs={{0,1},{1,0},{2,3},{3,2},{4,5},{5,4},{6,7},{7,6},{8,9},{9,8},{10,11... | collective-permute-start | bytes 1179656 | tf_op jit(solution)/shard_map/ppermute | solution.py:478
  255.1 16.4 %collective-permute-start.13 = (bf16[12,128,128]{2,1,0:T(8,128)(2,1)S(1)}, bf16[12,128,128]{2,1,0:T(8,128)(2,1)S(1)}, u32[]{:S(2)}, u32[]{:S(2)}) collective-permute-start(bf16[12,128,128]{2,1,0:T(8,128)(2,1)S(1)} %collective-permute-done.5.refs_1_), channel_id=1, source_target_pairs={{0,1},{1,0},{2,3},{3,2},{4,5},{5,4},{6,7},{7,6},{8,9},{9,8},{10,11... | collective-permute-start | bytes 1179656 | tf_op jit(solution)/shard_map/ppermute | solution.py:478
  255.1 16.4 %collective-permute-start.15 = (bf16[12,128,128]{2,1,0:T(8,128)(2,1)S(1)}, bf16[12,128,128]{2,1,0:T(8,128)(2,1)S(1)}, u32[]{:S(2)}, u32[]{:S(2)}) collective-permute-start(bf16[12,128,128]{2,1,0:T(8,128)(2,1)S(1)} %collective-permute-done.11.refs_3_), channel_id=1, source_target_pairs={{0,1},{1,0},{2,3},{3,2},{4,5},{5,4},{6,7},{7,6},{8,9},{9,8},{10,11... | collective-permute-start | bytes 1179656 | tf_op jit(solution)/shard_map/ppermute | solution.py:478
  (4 other events, 15.3 us)

commit v3 on v0

--- a/solution.py
+++ b/solution.py
@@ -10,7 +10,7 @@
 C = 2
 
 
-def pack_kernel(slots_ref, ent_ref, out_ref, staged, load_sems, store_sem):
+def pack_kernel(base_ref, owner_ref, ent_ref, out_ref, staged, seen, load_sems, store_sem):
     count = ent_ref.shape[0]
     parts = load_sems.shape[0]
     size = count // parts
@@ -20,32 +20,45 @@
         loads.append(pltpu.make_async_copy(ent_ref.at[rows], staged.at[rows], load_sems.at[p]))
         loads[-1].start()
 
+    def clear(i, carry):
+        seen[i] = 0
+        return carry
+
     def issue(i, carry):
-        pltpu.make_async_copy(staged.at[i], out_ref.at[slots_ref[i]], store_sem).start()
+        owner = owner_ref[base_ref[0] + i]
+        rank = seen[owner]
+        seen[owner] = rank + 1
+        slot = owner * C + rank
+        pltpu.make_async_copy(staged.at[i], out_ref.at[slot], store_sem).start()
         return carry
 
+    lax.fori_loop(0, seen.shape[0], clear, 0, unroll=8)
     for p in range(parts):
         loads[p].wait()
         lax.fori_loop(p * size, (p + 1) * size, issue, 0)
     pltpu.make_async_copy(staged, out_ref.at[pl.ds(0, count)], store_sem).wait()
 
 
-def pack(ent_blocks, slots, total):
+def pack(ent_blocks, ent_owner, base, device_count):
     return pl.pallas_call(
         pack_kernel,
-        out_shape=jax.ShapeDtypeStruct((total,) + ent_blocks.shape[1:], ent_blocks.dtype),
+        out_shape=jax.ShapeDtypeStruct(
+            (device_count * C,) + ent_blocks.shape[1:], ent_blocks.dtype
+        ),
         in_specs=[
+            pl.BlockSpec(memory_space=pltpu.SMEM),
             pl.BlockSpec(memory_space=pltpu.SMEM),
             pl.BlockSpec(memory_space=pl.ANY),
         ],
         out_specs=pl.BlockSpec(memory_space=pl.ANY),
         scratch_shapes=[
             pltpu.VMEM(ent_blocks.shape, ent_blocks.dtype),
+            pltpu.SMEM((device_count,), jnp.int32),
             pltpu.SemaphoreType.DMA((4,)),
             pltpu.SemaphoreType.DMA,
         ],
         name="pack",
-    )(slots, ent_blocks)
+    )(base, ent_owner, ent_blocks)
 
 
 def admit_kernel(spans, first_ref, order_ref, source_ref, density_ref, received_ref, *refs):
@@ -63,7 +76,7 @@
         return carry
 
     copies = []
-    done = 0
+    done = spans[0][0]
     for i, (low, high) in enumerate(spans):
         if high > done:
             lax.fori_loop(done, high, place, 0)
@@ -296,8 +309,9 @@
     lists = jnp.take(listing, rows, axis=0)
     list_x = lists // (narrow_count * row_count)
     list_y = lists // row_count % narrow_count
+    aside = list_y == (near_y ^ 1)[:, None]
     kind = jnp.where(
-        list_x == (near_x ^ 1)[:, None], 2, jnp.where(list_y == (near_y ^ 1)[:, None], 1, 0)
+        list_x == (near_x ^ 1)[:, None], jnp.where(aside, 2, 3), jnp.where(aside, 1, 0)
     )
     slot_ids = jnp.arange(slot_count, dtype=jnp.int32)
     key = kind * slot_count + slot_ids
@@ -337,12 +351,8 @@
     owners = ent_owner.reshape(device_count, held)
     places = ent_place.reshape(device_count, held)
 
-    my_owners = lax.dynamic_index_in_dim(owners, self_index, 0, False)
-    entry_ids = jnp.arange(held, dtype=jnp.int32)
-    same = my_owners[:, None] == my_owners[None, :]
-    my_ranks = jnp.sum(same & (entry_ids[None, :] < entry_ids[:, None]), axis=1)
-    slots = (my_owners * C + my_ranks).astype(jnp.int32)
-    outgoing = pack(ent_blocks, slots, device_count * C)
+    base = (self_index * held).astype(jnp.int32).reshape(1)
+    outgoing = pack(ent_blocks, ent_owner, base, device_count)
     received = lax.all_to_all(
         outgoing.reshape(device_count, C, width, width),
         ("gx", "gy"), split_axis=0, concat_axis=0, tiled=True,
@@ -375,12 +385,15 @@
     positions, out_slots, source = block_positions(neighbours, here_x, here_y, starts, zero_at)
 
     cut = corner_blocks // 2
-    spans = ((0, cut), (cut, 2 * cut), (0, 2 * cut), (2 * cut, blocks))
+    tail = blocks - 6 * row_count
     received, first, order, source, positions, out_slots = lax.optimization_barrier(
         (received, first, order, source, positions, out_slots)
     )
-    own_1, own_2, own_12, own_3 = admit(
-        density.reshape(blocks, width, width), received, first, order, source, spans
+    flat_density = density.reshape(blocks, width, width)
+    (own_1,) = admit(flat_density, received, first, order, source, ((0, cut),))
+    own_2, own_3, own_t = admit(
+        flat_density, received, first, order, source,
+        ((cut, 2 * cut), (2 * cut, blocks), (tail, blocks)),
     )
 
     axes = ("gx", "gy")
@@ -406,33 +419,36 @@
         return (x + 2 if x % 2 == 0 else x - 2), y
 
     ring_across_1 = send(own_1, ring)
+    own_across_1 = send(own_1, across)
+    ring_across_2 = send(own_2, ring)
     own_across_3 = send(own_3, across)
-    ring_across_2 = send(own_2, ring)
-    own_chip_12 = send(own_12, chip)
-    own_chip_3 = send(own_3, chip)
     far_across_1 = send(ring_across_1, onward)
     ring_same_1 = send(ring_across_1, across)
-    ring_same_3 = send(own_across_3, ring)
+    own_chip_1 = send(own_1, chip)
     far_across_2 = send(ring_across_2, onward)
     ring_same_2 = send(ring_across_2, across)
-    ring_across_3 = send(own_3, ring)
-    own_across_12 = send(own_12, across)
+    ring_same_3 = send(own_across_3, ring)
+    ring_across_t = send(own_t, ring)
+    own_across_2 = send(own_2, across)
+    own_chip_2 = send(own_2, chip)
+    own_chip_3 = send(own_3, chip)
     far_same_1 = send(ring_same_1, onward)
     ring_chip_1 = send(ring_same_1, chip)
+    far_same_3 = send(ring_same_3[:near_blocks - 2 * cut], onward)
+    ring_chip_3 = send(ring_same_3, chip)
     far_same_2 = send(ring_same_2, onward)
     ring_chip_2 = send(ring_same_2, chip)
-    far_same_3 = send(ring_same_3[:near_blocks - 2 * cut], onward)
-    ring_chip_3 = send(ring_same_3, chip)
     far_chip_1 = send(far_same_1, chip)
+    far_chip_3 = send(far_same_3, chip)
     far_chip_2 = send(far_same_2, chip)
-    far_chip_3 = send(far_same_3, chip)
 
     near_pieces = [
-        (own_12, 0, 0), (own_3, 0, 2 * cut), (own_chip_12, 1, 0), (own_chip_3, 1, 2 * cut),
-        (own_across_12, 2, 0), (own_across_3, 2, 2 * cut),
+        (own_1, 0, 0), (own_2, 0, cut), (own_3, 0, 2 * cut),
+        (own_chip_1, 1, 0), (own_chip_2, 1, cut), (own_chip_3, 1, 2 * cut),
+        (own_across_1, 2, 0), (own_across_2, 2, cut), (own_across_3, 2, 2 * cut),
         (ring_same_1, 3, 0), (ring_same_2, 3, cut), (ring_same_3, 3, 2 * cut),
         (ring_chip_1, 4, 0), (ring_chip_2, 4, cut), (ring_chip_3, 4, 2 * cut),
-        (ring_across_1, 5, 0), (ring_across_2, 5, cut), (ring_across_3, 5, 2 * cut),
+        (ring_across_1, 5, 0), (ring_across_2, 5, cut), (ring_across_t, 5, tail),
     ]
     far_pieces = [
         (far_same_1, 6, 0), (far_same_2, 6, cut), (far_same_3, 6, 2 * cut),

time: 293 us -> 279 us (0.952)
  waiting for transfers between devices: 217 us -> 190 us
  starting transfers between devices: 33.7 us -> 43.1 us
  Pallas kernels: 32.8 us -> 39.1 us
    ppermute x21 -> x23, waiting for transfers between devices: 124 us -> 96 us  [send(): return lax.ppermute(array, axes, pairs)]
    ppermute x21 -> x23, starting transfers between devices: 21.6 us -> 31.1 us  [send(): return lax.ppermute(array, axes, pairs)]
    pallas_call x1 -> x2, Pallas kernels: 7.09 us -> 12.1 us  [admit(): pl.pallas_call(functools.partial(admit_kernel, spans), out_shape=[jax.Sha...]
  transfers between devices with their start and end apart: 22 -> 24, of which waited for: 11 -> 12; matrix products, arithmetic and copies ran while one was open for 2% -> 2% of each run, Pallas kernels for 3% -> 5%
where the time goes in v3:
time: 279 us
  waiting for transfers between devices  190 us (68%)
  starting transfers between devices  43.1 us (15%)
  Pallas kernels  39.1 us (14%)
  local copies, waits for them, and re-layouts  3.31 us (1%)
  other arithmetic  3.31 us (1%)
    ppermute x23, waiting for transfers between devices, send(): return lax.ppermute(array, axes, pairs)  96 us
    all_to_all x1, waiting for transfers between devices, per_device(): lax.all_to_all(outgoing.reshape(device_count, C, width, width), ('gx', 'g...  93.7 us
    ppermute x23, starting transfers between devices, send(): return lax.ppermute(array, axes, pairs)  31.1 us
    pallas_call x1, Pallas kernels, purify_far(): pl.pallas_call(functools.partial(far_kernel, row_count, width, piece_star...  13 us
    pallas_call x2, Pallas kernels, admit(): pl.pallas_call(functools.partial(admit_kernel, spans), out_shape=[jax.Sha...  12.1 us
    all_to_all x1, starting transfers between devices, per_device(): lax.all_to_all(outgoing.reshape(device_count, C, width, width), ('gx', 'g...  12 us
    pallas_call x1, Pallas kernels, square_near(): pl.pallas_call(functools.partial(near_kernel, row_count, width, piece_sta...  9.64 us
  transfers between devices with their start and end apart: 24, of which 12 were waited for; matrix products, arithmetic and copies ran while one was open for 2% of the time, Pallas kernels for 5%

profile of v3, /device:TPU:1, one launch (start us, length us, event | category | flops | bytes accessed | tf_op | source)
XLA Modules:
  0.0 278.9 jit_solution(15152694434886431598)
XLA Ops:
  0.0 4.4 %pack.1 = bf16[256,128,128]{2,1,0:T(8,128)(2,1)} custom-call(s32[1]{0:T(128)} %bitcast.base_ref, s32[12288]{0:T(1024)} %owner_ref.1, bf16[96,128,128]{2,1,0:T(8,128)(2,1)} %ent_ref.1), custom_call_target="tpu_custom_call" | custom-call | tf_op jit(solution)/shard_map/pack/pallas_call | solution.py:43
  4.4 12.0 %all-to-all-start = ((bf16[128,2,128,128]{3,2,1,0:T(8,128)(2,1)}), bf16[128,2,128,128]{3,2,1,0:T(8,128)(2,1)}, u32[]{:S(2)}, u32[]{:S(2)}) async-start(bf16[128,2,128,128]{3,2,1,0:T(8,128)(2,1)} %bitcast.9), calls=%async_computation | async-start | bytes 16777216 | tf_op jit(solution)/shard_map/all_to_all | solution.py:356
  22.1 93.7 %all-to-all-done = bf16[128,2,128,128]{3,2,1,0:T(8,128)(2,1)} async-done(((bf16[128,2,128,128]{3,2,1,0:T(8,128)(2,1)}), bf16[128,2,128,128]{3,2,1,0:T(8,128)(2,1)}, u32[]{:S(2)}, u32[]{:S(2)}) %all-to-all-start) | async-done | bytes 8388640 | tf_op jit(solution)/shard_map/all_to_all | solution.py:356
  115.8 6.5 %admit.3 = (bf16[18,128,128]{2,1,0:T(8,128)(2,1)}, bf16[24,128,128]{2,1,0:T(8,128)(2,1)}, bf16[18,128,128]{2,1,0:T(8,128)(2,1)}) custom-call(s32[61]{0:T(128)} %convert_reduce_fusion.2.first_ref, s32[256]{0:T(256)} %select_reduce_fusion.1.order_ref, s32[60]{0:T(128)} %select_reduce_fusion.4.source_ref, bf16[60,128,128]{2,1,0:T(8,128)(2,1)} %bitcast.10, ...), custom_call_target="tpu_custom_call" | custom-call | tf_op jit(solution)/shard_map/admit/pallas_call | solution.py:91
  122.3 3.4 %collective-permute-start.3 = (bf16[18,128,128]{2,1,0:T(8,128)(2,1)}, bf16[18,128,128]{2,1,0:T(8,128)(2,1)S(1)}, u32[]{:S(2)}, u32[]{:S(2)}) collective-permute-start(bf16[18,128,128]{2,1,0:T(8,128)(2,1)} %get-tuple-element.31.refs_1_), channel_id=1, source_target_pairs={{0,7},{1,6},{2,5},{3,4},{4,3},{5,2},{6,1},{7,0},{8,15},{9,14},{10,... | collective-permute-start | bytes 1769480 | tf_op jit(solution)/shard_map/ppermute | solution.py:407
  126.0 2.8 %collective-permute-start.18 = (bf16[18,128,128]{2,1,0:T(8,128)(2,1)}, bf16[18,128,128]{2,1,0:T(8,128)(2,1)}, u32[]{:S(2)}, u32[]{:S(2)}) collective-permute-start(bf16[18,128,128]{2,1,0:T(8,128)(2,1)} %get-tuple-element.31.refs_1_), channel_id=1, source_target_pairs={{0,3},{1,2},{2,1},{3,0},{4,7},{5,6},{6,5},{7,4},{8,11},{9,10},{10,... | collective-permute-start | bytes 1769480 | tf_op jit(solution)/shard_map/ppermute | solution.py:407
  128.9 2.1 collective-permute-start.22
  131.0 5.6 %admit.2.refs_0_ = bf16[18,128,128]{2,1,0:T(8,128)(2,1)} custom-call(s32[61]{0:T(128)} %convert_reduce_fusion.2.first_ref, s32[256]{0:T(256)} %select_reduce_fusion.1.order_ref, s32[60]{0:T(128)} %select_reduce_fusion.4.source_ref, bf16[60,128,128]{2,1,0:T(8,128)(2,1)} %bitcast.11, bf16[256,128,128]{2,1,0:T(8,128)(2,1)} %bitcast.2.received_ref), custom_call_target="tpu_custom_call" | custom-call | tf_op jit(solution)/shard_map/admit/pallas_call | solution.py:91
  136.5 3.3 %collective-permute-done.3.refs_16_ = bf16[18,128,128]{2,1,0:T(8,128)(2,1)S(1)} collective-permute-done((bf16[18,128,128]{2,1,0:T(8,128)(2,1)}, bf16[18,128,128]{2,1,0:T(8,128)(2,1)S(1)}, u32[]{:S(2)}, u32[]{:S(2)}) %collective-permute-start.3) | collective-permute-done | bytes 589856 | tf_op jit(solution)/shard_map/ppermute | solution.py:407
  139.8 2.5 collective-permute-start
  142.4 1.0 collective-permute-start.14
  143.4 1.5 collective-permute-start.4
  144.9 15.1 %collective-permute-done.6.refs_8_ = bf16[24,128,128]{2,1,0:T(8,128)(2,1)S(1)} collective-permute-done((bf16[24,128,128]{2,1,0:T(8,128)(2,1)}, bf16[24,128,128]{2,1,0:T(8,128)(2,1)S(1)}, u32[]{:S(2)}, u32[]{:S(2)}) %collective-permute-start.6) | collective-permute-done | bytes 786464 | tf_op jit(solution)/shard_map/ppermute | solution.py:407
  160.0 1.8 collective-permute-start.7
  162.7 2.4 collective-permute-done.refs_15_
  165.1 4.6 %collective-permute-start.1 = (bf16[18,128,128]{2,1,0:T(8,128)(2,1)S(1)}, bf16[18,128,128]{2,1,0:T(8,128)(2,1)S(1)}, u32[]{:S(2)}, u32[]{:S(2)}) collective-permute-start(bf16[18,128,128]{2,1,0:T(8,128)(2,1)S(1)} %collective-permute-done.refs_15_), channel_id=1, source_target_pairs={{0,3},{1,2},{2,1},{3,0},{4,7},{5,6},{6,5},{7,4},{8,11},{9,10},{10,... | collective-permute-start | bytes 1769480 | tf_op jit(solution)/shard_map/ppermute | solution.py:407
  169.7 2.9 %collective-permute-done.4.refs_10_ = bf16[18,128,128]{2,1,0:T(8,128)(2,1)S(1)} collective-permute-done((bf16[18,128,128]{2,1,0:T(8,128)(2,1)S(1)}, bf16[18,128,128]{2,1,0:T(8,128)(2,1)S(1)}, u32[]{:S(2)}, u32[]{:S(2)}) %collective-permute-start.4) | collective-permute-done | bytes 589856 | tf_op jit(solution)/shard_map/ppermute | solution.py:407
  172.7 9.3 %collective-permute-done.7.refs_11_ = bf16[24,128,128]{2,1,0:T(8,128)(2,1)S(1)} collective-permute-done((bf16[24,128,128]{2,1,0:T(8,128)(2,1)S(1)}, bf16[24,128,128]{2,1,0:T(8,128)(2,1)S(1)}, u32[]{:S(2)}, u32[]{:S(2)}) %collective-permute-start.7) | collective-permute-done | bytes 786464 | tf_op jit(solution)/shard_map/ppermute | solution.py:407
  182.7 2.6 collective-permute-done.1.refs_9_
  185.3 12.1 %collective-permute-done.17.refs_6_ = bf16[18,128,128]{2,1,0:T(8,128)(2,1)S(1)} collective-permute-done((bf16[18,128,128]{2,1,0:T(8,128)(2,1)}, bf16[18,128,128]{2,1,0:T(8,128)(2,1)S(1)}, u32[]{:S(2)}, u32[]{:S(2)}) %collective-permute-start.17) | collective-permute-done | bytes 589856 | tf_op jit(solution)/shard_map/ppermute | solution.py:407
  197.4 1.4 collective-permute-start.5
  198.8 1.3 collective-permute-start.8
  200.1 2.4 collective-permute-start.13
  202.6 12.6 %collective-permute-done.5.refs_1_ = bf16[18,128,128]{2,1,0:T(8,128)(2,1)S(1)} collective-permute-done((bf16[18,128,128]{2,1,0:T(8,128)(2,1)S(1)}, bf16[18,128,128]{2,1,0:T(8,128)(2,1)S(1)}, u32[]{:S(2)}, u32[]{:S(2)}) %collective-permute-start.5) | collective-permute-done | bytes 589856 | tf_op jit(solution)/shard_map/ppermute | solution.py:407
  215.2 12.6 %collective-permute-done.2.refs_0_ = bf16[18,128,128]{2,1,0:T(8,128)(2,1)S(1)} collective-permute-done((bf16[18,128,128]{2,1,0:T(8,128)(2,1)S(1)}, bf16[18,128,128]{2,1,0:T(8,128)(2,1)S(1)}, u32[]{:S(2)}, u32[]{:S(2)}) %collective-permute-start.2) | collective-permute-done | bytes 589856 | tf_op jit(solution)/shard_map/ppermute | solution.py:407
  227.8 2.1 collective-permute-start.10
  229.9 10.5 %collective-permute-done.8.refs_2_ = bf16[18,128,128]{2,1,0:T(8,128)(2,1)S(1)} collective-permute-done((bf16[18,128,128]{2,1,0:T(8,128)(2,1)S(1)}, bf16[18,128,128]{2,1,0:T(8,128)(2,1)S(1)}, u32[]{:S(2)}, u32[]{:S(2)}) %collective-permute-start.8) | collective-permute-done | bytes 589856 | tf_op jit(solution)/shard_map/ppermute | solution.py:407
  240.5 2.1 collective-permute-start.9
  242.6 1.1 copy-done
  243.7 9.6 %square_near.1 = (bf16[2304,384]{1,0:T(8,128)(2,1)S(1)}, bf16[1536,384]{1,0:T(8,128)(2,1)S(1)}, bf16[1536,384]{1,0:T(8,128)(2,1)S(1)}, bf16[2304,384]{1,0:T(8,12...) custom-call(s32[729]{0:T(1024)S(1)} %reshape.495.pos_ref, ...), custom_call_target="tpu_custom_call" | custom-call | tf_op jit(solution)/shard_map/square_near/pallas_call | solution.py:175
  253.3 12.4 %collective-permute-done.12.refs_6_ = bf16[18,128,128]{2,1,0:T(8,128)(2,1)S(1)} collective-permute-done((bf16[18,128,128]{2,1,0:T(8,128)(2,1)S(1)}, bf16[18,128,128]{2,1,0:T(8,128)(2,1)S(1)}, u32[]{:S(2)}, u32[]{:S(2)}) %collective-permute-start.12) | collective-permute-done | bytes 589856 | tf_op jit(solution)/shard_map/ppermute | solution.py:407
  265.8 13.0 %purify_far.1 = f32[60,128,128]{2,1,0:T(8,128)} custom-call(s32[729]{0:T(1024)S(1)} %reshape.495.pos_ref, s32[81]{0:T(128)S(1)} %reshape.496.slot_ref, bf16[18,128,128]{2,1,0:T(8,128)(2,1)S(1)} %collective-permute-done.2.refs_0_, bf16[18,128,128]{2,1,0:T(8,128)(2,1)S(1)} %collective-permute-done.5.refs_1_, ...), custom_call_target="tpu_custom_call" | custom-call | tf_op jit(solution)/shard_map/purify_far/pallas_call | solution.py:271
  (77 shorter events, 7.6 us)
Async XLA Ops:
  4.4 12.1 %copy-start.4 = (s32[32,4,3,20]{0,1,3,2:T(4,128)S(1)}, s32[32,4,3,20]{0,1,3,2:T(4,128)}, u32[]{:S(2)}) copy-start(s32[32,4,3,20]{0,1,3,2:T(4,128)} %param.6) | copy-start | bytes 92164
  4.4 14.6 %copy-start.3 = (s32[12288]{0:T(1024)S(1)}, s32[12288]{0:T(1024)}, u32[]{:S(2)}) copy-start(s32[12288]{0:T(1024)} %owner_ref.1) | copy-start | bytes 147460
  4.4 111.4 %all-to-all-start = ((bf16[128,2,128,128]{3,2,1,0:T(8,128)(2,1)}), bf16[128,2,128,128]{3,2,1,0:T(8,128)(2,1)}, u32[]{:S(2)}, u32[]{:S(2)}) async-start(bf16[128,2,128,128]{3,2,1,0:T(8,128)(2,1)} %bitcast.9), calls=%async_computation | async-start | bytes 16777216 | tf_op jit(solution)/shard_map/all_to_all | solution.py:356
  16.4 3.0 %copy-start.5 = (s32[12288]{0:T(1024)S(1)}, s32[12288]{0:T(1024)}, u32[]{:S(2)}) copy-start(s32[12288]{0:T(1024)} %param.9) | copy-start | bytes 147460
  122.3 17.5 %collective-permute-start.3 = (bf16[18,128,128]{2,1,0:T(8,128)(2,1)}, bf16[18,128,128]{2,1,0:T(8,128)(2,1)S(1)}, u32[]{:S(2)}, u32[]{:S(2)}) collective-permute-start(bf16[18,128,128]{2,1,0:T(8,128)(2,1)} %get-tuple-element.31.refs_1_), channel_id=1, source_target_pairs={{0,7},{1,6},{2,5},{3,4},{4,3},{5,2},{6,1},{7,0},{8,15},{9,14},{10,... | collective-permute-start | bytes 1769480 | tf_op jit(solution)/shard_map/ppermute | solution.py:407
  125.7 16.6 %collective-permute-start.15 = (bf16[18,128,128]{2,1,0:T(8,128)(2,1)}, bf16[18,128,128]{2,1,0:T(8,128)(2,1)S(1)}, u32[]{:S(2)}, u32[]{:S(2)}) collective-permute-start(bf16[18,128,128]{2,1,0:T(8,128)(2,1)} %get-tuple-element.31.refs_1_), channel_id=1, source_target_pairs={{0,1},{1,0},{2,3},{3,2},{4,5},{5,4},{6,7},{7,6},{8,9},{9,8},{10,11... | collective-permute-start | bytes 1769480 | tf_op jit(solution)/shard_map/ppermute | solution.py:407
  126.0 17.5 %collective-permute-start.18 = (bf16[18,128,128]{2,1,0:T(8,128)(2,1)}, bf16[18,128,128]{2,1,0:T(8,128)(2,1)}, u32[]{:S(2)}, u32[]{:S(2)}) collective-permute-start(bf16[18,128,128]{2,1,0:T(8,128)(2,1)} %get-tuple-element.31.refs_1_), channel_id=1, source_target_pairs={{0,3},{1,2},{2,1},{3,0},{4,7},{5,6},{6,5},{7,4},{8,11},{9,10},{10,... | collective-permute-start | bytes 1769480 | tf_op jit(solution)/shard_map/ppermute | solution.py:407
  128.8 31.2 %collective-permute-start.6 = (bf16[24,128,128]{2,1,0:T(8,128)(2,1)}, bf16[24,128,128]{2,1,0:T(8,128)(2,1)S(1)}, u32[]{:S(2)}, u32[]{:S(2)}) collective-permute-start(bf16[24,128,128]{2,1,0:T(8,128)(2,1)} %get-tuple-element.32.refs_2_), channel_id=1, source_target_pairs={{0,3},{1,2},{2,1},{3,0},{4,7},{5,6},{6,5},{7,4},{8,11},{9,10},{10,... | collective-permute-start | bytes 2359304 | tf_op jit(solution)/shard_map/ppermute | solution.py:407
  128.9 33.0 %copy-start.1 = (bf16[24,128,128]{2,1,0:T(8,128)(2,1)S(1)}, bf16[24,128,128]{2,1,0:T(8,128)(2,1)}, u32[]{:S(2)}) copy-start(bf16[24,128,128]{2,1,0:T(8,128)(2,1)} %get-tuple-element.32.refs_2_) | copy-start | bytes 2359300
  128.9 113.7 %copy-start.2 = (bf16[18,128,128]{2,1,0:T(8,128)(2,1)S(1)}, bf16[18,128,128]{2,1,0:T(8,128)(2,1)}, u32[]{:S(2)}) copy-start(bf16[18,128,128]{2,1,0:T(8,128)(2,1)} %get-tuple-element.31.refs_1_) | copy-start | bytes 1769476
  128.9 33.0 %collective-permute-start.22 = (bf16[18,128,128]{2,1,0:T(8,128)(2,1)}, bf16[18,128,128]{2,1,0:T(8,128)(2,1)}, u32[]{:S(2)}, u32[]{:S(2)}) collective-permute-start(bf16[18,128,128]{2,1,0:T(8,128)(2,1)} %get-tuple-element.33), channel_id=1, source_target_pairs={{0,7},{1,6},{2,5},{3,4},{4,3},{5,2},{6,1},{7,0},{8,15},{9,14},{10,... | collective-permute-start | bytes 1769480 | tf_op jit(solution)/shard_map/ppermute | solution.py:407
  139.8 25.3 %collective-permute-start = (bf16[18,128,128]{2,1,0:T(8,128)(2,1)}, bf16[18,128,128]{2,1,0:T(8,128)(2,1)S(1)}, u32[]{:S(2)}, u32[]{:S(2)}) collective-permute-start(bf16[18,128,128]{2,1,0:T(8,128)(2,1)} %admit.2.refs_0_), channel_id=1, source_target_pairs={{0,7},{1,6},{2,5},{3,4},{4,3},{5,2},{6,1},{7,0},{8,15},{9,14},{10,... | collective-permute-start | bytes 1769480 | tf_op jit(solution)/shard_map/ppermute | solution.py:407
  142.4 27.3 %collective-permute-start.14 = (bf16[18,128,128]{2,1,0:T(8,128)(2,1)}, bf16[18,128,128]{2,1,0:T(8,128)(2,1)S(1)}, u32[]{:S(2)}, u32[]{:S(2)}) collective-permute-start(bf16[18,128,128]{2,1,0:T(8,128)(2,1)} %admit.2.refs_0_), channel_id=1, source_target_pairs={{0,1},{1,0},{2,3},{3,2},{4,5},{5,4},{6,7},{7,6},{8,9},{9,8},{10,11... | collective-permute-start | bytes 1769480 | tf_op jit(solution)/shard_map/ppermute | solution.py:407
  143.4 29.2 %collective-permute-start.4 = (bf16[18,128,128]{2,1,0:T(8,128)(2,1)S(1)}, bf16[18,128,128]{2,1,0:T(8,128)(2,1)S(1)}, u32[]{:S(2)}, u32[]{:S(2)}) collective-permute-start(bf16[18,128,128]{2,1,0:T(8,128)(2,1)S(1)} %collective-permute-done.3.refs_16_), channel_id=1, source_target_pairs={{0,3},{1,2},{2,1},{3,0},{4,7},{5,6},{6,5},{7,4},{8,11},{9,10},{10,... | collective-permute-start | bytes 1769480 | tf_op jit(solution)/shard_map/ppermute | solution.py:407
  160.0 21.9 %collective-permute-start.7 = (bf16[24,128,128]{2,1,0:T(8,128)(2,1)S(1)}, bf16[24,128,128]{2,1,0:T(8,128)(2,1)S(1)}, u32[]{:S(2)}, u32[]{:S(2)}) collective-permute-start(bf16[24,128,128]{2,1,0:T(8,128)(2,1)S(1)} %collective-permute-done.6.refs_8_), channel_id=1, source_target_pairs={{0,7},{1,6},{2,5},{3,4},{4,3},{5,2},{6,1},{7,0},{8,15},{9,14},{10,... | collective-permute-start | bytes 2359304 | tf_op jit(solution)/shard_map/ppermute | solution.py:407
  161.8 36.9 %collective-permute-start.16 = (bf16[24,128,128]{2,1,0:T(8,128)(2,1)S(1)}, bf16[24,128,128]{2,1,0:T(8,128)(2,1)S(1)}, u32[]{:S(2)}, u32[]{:S(2)}) collective-permute-start(bf16[24,128,128]{2,1,0:T(8,128)(2,1)S(1)} %copy-done.1), channel_id=1, source_target_pairs={{0,1},{1,0},{2,3},{3,2},{4,5},{5,4},{6,7},{7,6},{8,9},{9,8},{10,11... | collective-permute-start | bytes 2359304 | tf_op jit(solution)/shard_map/ppermute | solution.py:407
  165.1 20.2 %collective-permute-start.1 = (bf16[18,128,128]{2,1,0:T(8,128)(2,1)S(1)}, bf16[18,128,128]{2,1,0:T(8,128)(2,1)S(1)}, u32[]{:S(2)}, u32[]{:S(2)}) collective-permute-start(bf16[18,128,128]{2,1,0:T(8,128)(2,1)S(1)} %collective-permute-done.refs_15_), channel_id=1, source_target_pairs={{0,3},{1,2},{2,1},{3,0},{4,7},{5,6},{6,5},{7,4},{8,11},{9,10},{10,... | collective-permute-start | bytes 1769480 | tf_op jit(solution)/shard_map/ppermute | solution.py:407
  169.7 27.7 %collective-permute-start.17 = (bf16[18,128,128]{2,1,0:T(8,128)(2,1)}, bf16[18,128,128]{2,1,0:T(8,128)(2,1)S(1)}, u32[]{:S(2)}, u32[]{:S(2)}) collective-permute-start(bf16[18,128,128]{2,1,0:T(8,128)(2,1)} %admit.2.refs_0_), channel_id=1, source_target_pairs={{0,3},{1,2},{2,1},{3,0},{4,7},{5,6},{6,5},{7,4},{8,11},{9,10},{10,... | collective-permute-start | bytes 1769480 | tf_op jit(solution)/shard_map/ppermute | solution.py:407
  172.7 26.2 %collective-permute-start.20 = (bf16[18,128,128]{2,1,0:T(8,128)(2,1)S(1)}, bf16[18,128,128]{2,1,0:T(8,128)(2,1)S(1)}, u32[]{:S(2)}, u32[]{:S(2)}) collective-permute-start(bf16[18,128,128]{2,1,0:T(8,128)(2,1)S(1)} %collective-permute-done.4.refs_10_), channel_id=1, source_target_pairs={{0,1},{1,0},{2,3},{3,2},{4,5},{5,4},{6,7},{7,6},{8,9},{9,8},{10,11... | collective-permute-start | bytes 1769480 | tf_op jit(solution)/shard_map/ppermute | solution.py:407
  181.9 60.6 %collective-permute-start.21 = (bf16[24,128,128]{2,1,0:T(8,128)(2,1)S(1)}, bf16[24,128,128]{2,1,0:T(8,128)(2,1)S(1)}, u32[]{:S(2)}, u32[]{:S(2)}) collective-permute-start(bf16[24,128,128]{2,1,0:T(8,128)(2,1)S(1)} %collective-permute-done.7.refs_11_), channel_id=1, source_target_pairs={{0,1},{1,0},{2,3},{3,2},{4,5},{5,4},{6,7},{7,6},{8,9},{9,8},{10,11... | collective-permute-start | bytes 2359304 | tf_op jit(solution)/shard_map/ppermute | solution.py:407
  185.3 14.8 %collective-permute-start.19 = (bf16[18,128,128]{2,1,0:T(8,128)(2,1)S(1)}, bf16[18,128,128]{2,1,0:T(8,128)(2,1)S(1)}, u32[]{:S(2)}, u32[]{:S(2)}) collective-permute-start(bf16[18,128,128]{2,1,0:T(8,128)(2,1)S(1)} %collective-permute-done.1.refs_9_), channel_id=1, source_target_pairs={{0,1},{1,0},{2,3},{3,2},{4,5},{5,4},{6,7},{7,6},{8,9},{9,8},{10,11... | collective-permute-start | bytes 1769480 | tf_op jit(solution)/shard_map/ppermute | solution.py:407
  197.4 17.8 %collective-permute-start.5 = (bf16[18,128,128]{2,1,0:T(8,128)(2,1)S(1)}, bf16[18,128,128]{2,1,0:T(8,128)(2,1)S(1)}, u32[]{:S(2)}, u32[]{:S(2)}) collective-permute-start(bf16[18,128,128]{2,1,0:T(8,128)(2,1)S(1)} %collective-permute-done.4.refs_10_), channel_id=1, source_target_pairs={{0,8},{1,9},{2,10},{3,11},{4,124},{5,125},{6,126},{7,127},{8,16},{... | collective-permute-start | bytes 1769480 | tf_op jit(solution)/shard_map/ppermute | solution.py:407
  198.7 29.1 %collective-permute-start.2 = (bf16[18,128,128]{2,1,0:T(8,128)(2,1)S(1)}, bf16[18,128,128]{2,1,0:T(8,128)(2,1)S(1)}, u32[]{:S(2)}, u32[]{:S(2)}) collective-permute-start(bf16[18,128,128]{2,1,0:T(8,128)(2,1)S(1)} %collective-permute-done.1.refs_9_), channel_id=1, source_target_pairs={{0,8},{1,9},{2,10},{3,11},{4,124},{5,125},{6,126},{7,127},{8,16},{... | collective-permute-start | bytes 1769480 | tf_op jit(solution)/shard_map/ppermute | solution.py:407
  198.8 41.6 %collective-permute-start.8 = (bf16[18,128,128]{2,1,0:T(8,128)(2,1)S(1)}, bf16[18,128,128]{2,1,0:T(8,128)(2,1)S(1)}, u32[]{:S(2)}, u32[]{:S(2)}) collective-permute-start(bf16[18,128,128]{2,1,0:T(8,128)(2,1)S(1)} %slice.20), channel_id=1, source_target_pairs={{0,8},{1,9},{2,10},{3,11},{4,124},{5,125},{6,126},{7,127},{8,16},{... | collective-permute-start | bytes 1769480 | tf_op jit(solution)/shard_map/ppermute | solution.py:407
  200.1 53.2 %collective-permute-start.13 = (bf16[18,128,128]{2,1,0:T(8,128)(2,1)S(1)}, bf16[18,128,128]{2,1,0:T(8,128)(2,1)S(1)}, u32[]{:S(2)}, u32[]{:S(2)}) collective-permute-start(bf16[18,128,128]{2,1,0:T(8,128)(2,1)S(1)} %collective-permute-done.3.refs_16_), channel_id=1, source_target_pairs={{0,8},{1,9},{2,10},{3,11},{4,124},{5,125},{6,126},{7,127},{8,16},{... | collective-permute-start | bytes 1769480 | tf_op jit(solution)/shard_map/ppermute | solution.py:407
  215.2 50.6 %collective-permute-start.12 = (bf16[18,128,128]{2,1,0:T(8,128)(2,1)S(1)}, bf16[18,128,128]{2,1,0:T(8,128)(2,1)S(1)}, u32[]{:S(2)}, u32[]{:S(2)}) collective-permute-start(bf16[18,128,128]{2,1,0:T(8,128)(2,1)S(1)} %collective-permute-done.refs_15_), channel_id=1, source_target_pairs={{0,8},{1,9},{2,10},{3,11},{4,124},{5,125},{6,126},{7,127},{8,16},{... | collective-permute-start | bytes 1769480 | tf_op jit(solution)/shard_map/ppermute | solution.py:407
  227.8 37.9 %collective-permute-start.10 = (bf16[18,128,128]{2,1,0:T(8,128)(2,1)S(1)}, bf16[18,128,128]{2,1,0:T(8,128)(2,1)S(1)}, u32[]{:S(2)}, u32[]{:S(2)}) collective-permute-start(bf16[18,128,128]{2,1,0:T(8,128)(2,1)S(1)} %collective-permute-done.5.refs_1_), channel_id=1, source_target_pairs={{0,1},{1,0},{2,3},{3,2},{4,5},{5,4},{6,7},{7,6},{8,9},{9,8},{10,11... | collective-permute-start | bytes 1769480 | tf_op jit(solution)/shard_map/ppermute | solution.py:407
  240.5 25.3 %collective-permute-start.9 = (bf16[18,128,128]{2,1,0:T(8,128)(2,1)S(1)}, bf16[18,128,128]{2,1,0:T(8,128)(2,1)S(1)}, u32[]{:S(2)}, u32[]{:S(2)}) collective-permute-start(bf16[18,128,128]{2,1,0:T(8,128)(2,1)S(1)} %collective-permute-done.2.refs_0_), channel_id=1, source_target_pairs={{0,1},{1,0},{2,3},{3,2},{4,5},{5,4},{6,7},{7,6},{8,9},{9,8},{10,11... | collective-permute-start | bytes 1769480 | tf_op jit(solution)/shard_map/ppermute | solution.py:407
  242.6 23.2 %collective-permute-start.11 = (bf16[18,128,128]{2,1,0:T(8,128)(2,1)S(1)}, bf16[18,128,128]{2,1,0:T(8,128)(2,1)S(1)}, u32[]{:S(2)}, u32[]{:S(2)}) collective-permute-start(bf16[18,128,128]{2,1,0:T(8,128)(2,1)S(1)} %collective-permute-done.8.refs_2_), channel_id=1, source_target_pairs={{0,1},{1,0},{2,3},{3,2},{4,5},{5,4},{6,7},{7,6},{8,9},{9,8},{10,11... | collective-permute-start | bytes 1769480 | tf_op jit(solution)/shard_map/ppermute | solution.py:407
  242.6 1.1 copy-start

commit v4 on v3

--- a/solution.py
+++ b/solution.py
@@ -76,10 +76,10 @@
         return carry
 
     copies = []
-    done = spans[0][0]
+    done = 0
     for i, (low, high) in enumerate(spans):
         if high > done:
-            lax.fori_loop(done, high, place, 0)
+            lax.fori_loop(max(low, done), high, place, 0)
             done = high
         copies.append(pltpu.make_async_copy(own.at[pl.ds(low, high - low)], part_refs[i], sems.at[i]))
         copies[-1].start()
@@ -390,11 +390,11 @@
         (received, first, order, source, positions, out_slots)
     )
     flat_density = density.reshape(blocks, width, width)
-    (own_1,) = admit(flat_density, received, first, order, source, ((0, cut),))
-    own_2, own_3, own_t = admit(
+    own_1, own_3, own_t = admit(
         flat_density, received, first, order, source,
-        ((cut, 2 * cut), (2 * cut, blocks), (tail, blocks)),
-    )
+        ((0, cut), (2 * cut, blocks), (tail, blocks)),
+    )
+    (own_2,) = admit(flat_density, received, first, order, source, ((cut, 2 * cut),))
 
     axes = ("gx", "gy")
     devices = [(x, y) for x in range(wide_count) for y in range(narrow_count)]

time: 279 us -> 279 us (level)
  starting transfers between devices: 43.1 us -> 40 us
    ppermute x23, starting transfers between devices: 31.1 us -> 28 us  [send(): return lax.ppermute(array, axes, pairs)]
  transfers between devices with their start and end apart: 24 -> 24, of which waited for: 12 -> 10; matrix products, arithmetic and copies ran while one was open for 2% -> 2% of each run, Pallas kernels for 5% -> 6%
where the time goes in v4:
time: 279 us
  waiting for transfers between devices  192 us (69%)
  starting transfers between devices  40 us (14%)
  Pallas kernels  38.3 us (14%)
  local copies, waits for them, and re-layouts  4.44 us (2%)
  other arithmetic  3.31 us (1%)
    ppermute x23, waiting for transfers between devices, send(): return lax.ppermute(array, axes, pairs)  98.3 us
    all_to_all x1, waiting for transfers between devices, per_device(): lax.all_to_all(outgoing.reshape(device_count, C, width, width), ('gx', 'g...  93.7 us
    ppermute x23, starting transfers between devices, send(): return lax.ppermute(array, axes, pairs)  28 us
    pallas_call x1, Pallas kernels, purify_far(): pl.pallas_call(functools.partial(far_kernel, row_count, width, piece_star...  13 us
    pallas_call x2, Pallas kernels, admit(): pl.pallas_call(functools.partial(admit_kernel, spans), out_shape=[jax.Sha...  12.1 us
    all_to_all x1, starting transfers between devices, per_device(): lax.all_to_all(outgoing.reshape(device_count, C, width, width), ('gx', 'g...  12 us
    pallas_call x1, Pallas kernels, square_near(): pl.pallas_call(functools.partial(near_kernel, row_count, width, piece_sta...  8.83 us
  transfers between devices with their start and end apart: 24, of which 10 were waited for; matrix products, arithmetic and copies ran while one was open for 2% of the time, Pallas kernels for 6%

profile of v4, /device:TPU:1, one launch (start us, length us, event | category | flops | bytes accessed | tf_op | source)
XLA Modules:
  0.0 278.5 jit_solution(3013486681444692647)
XLA Ops:
  0.0 4.4 %pack.1 = bf16[256,128,128]{2,1,0:T(8,128)(2,1)} custom-call(s32[1]{0:T(128)} %bitcast.base_ref, s32[12288]{0:T(1024)} %owner_ref.1, bf16[96,128,128]{2,1,0:T(8,128)(2,1)} %ent_ref.1), custom_call_target="tpu_custom_call" | custom-call | tf_op jit(solution)/shard_map/pack/pallas_call | solution.py:43
  4.4 12.0 %all-to-all-start = ((bf16[128,2,128,128]{3,2,1,0:T(8,128)(2,1)}), bf16[128,2,128,128]{3,2,1,0:T(8,128)(2,1)}, u32[]{:S(2)}, u32[]{:S(2)}) async-start(bf16[128,2,128,128]{3,2,1,0:T(8,128)(2,1)} %bitcast.9), calls=%async_computation | async-start | bytes 16777216 | tf_op jit(solution)/shard_map/all_to_all | solution.py:356
  22.1 93.7 %all-to-all-done = bf16[128,2,128,128]{3,2,1,0:T(8,128)(2,1)} async-done(((bf16[128,2,128,128]{3,2,1,0:T(8,128)(2,1)}), bf16[128,2,128,128]{3,2,1,0:T(8,128)(2,1)}, u32[]{:S(2)}, u32[]{:S(2)}) %all-to-all-start) | async-done | bytes 8388640 | tf_op jit(solution)/shard_map/all_to_all | solution.py:356
  115.8 5.5 %admit.3.refs_1_ = bf16[18,128,128]{2,1,0:T(8,128)(2,1)} custom-call(s32[61]{0:T(128)} %convert_reduce_fusion.2.first_ref, s32[256]{0:T(256)} %select_reduce_fusion.1.order_ref, s32[60]{0:T(128)} %select_reduce_fusion.4.source_ref, bf16[60,128,128]{2,1,0:T(8,128)(2,1)} %bitcast.10, bf16[256,128,128]{2,1,0:T(8,128)(2,1)} %bitcast.2.received_ref), custom_call_target="tpu_custom_call" | custom-call | tf_op jit(solution)/shard_map/admit/pallas_call | solution.py:91
  121.2 3.3 %collective-permute-start.3 = (bf16[18,128,128]{2,1,0:T(8,128)(2,1)}, bf16[18,128,128]{2,1,0:T(8,128)(2,1)S(1)}, u32[]{:S(2)}, u32[]{:S(2)}) collective-permute-start(bf16[18,128,128]{2,1,0:T(8,128)(2,1)} %admit.3.refs_1_), channel_id=1, source_target_pairs={{0,7},{1,6},{2,5},{3,4},{4,3},{5,2},{6,1},{7,0},{8,15},{9,14},{10,... | collective-permute-start | bytes 1769480 | tf_op jit(solution)/shard_map/ppermute | solution.py:407
  124.8 2.9 %collective-permute-start.18 = (bf16[18,128,128]{2,1,0:T(8,128)(2,1)}, bf16[18,128,128]{2,1,0:T(8,128)(2,1)S(1)}, u32[]{:S(2)}, u32[]{:S(2)}) collective-permute-start(bf16[18,128,128]{2,1,0:T(8,128)(2,1)} %admit.3.refs_1_), channel_id=1, source_target_pairs={{0,3},{1,2},{2,1},{3,0},{4,7},{5,6},{6,5},{7,4},{8,11},{9,10},{10,... | collective-permute-start | bytes 1769480 | tf_op jit(solution)/shard_map/ppermute | solution.py:407
  127.7 6.7 %admit.2 = (bf16[18,128,128]{2,1,0:T(8,128)(2,1)}, bf16[24,128,128]{2,1,0:T(8,128)(2,1)}, bf16[18,128,128]{2,1,0:T(8,128)(2,1)}) custom-call(s32[61]{0:T(128)} %convert_reduce_fusion.2.first_ref, s32[256]{0:T(256)} %select_reduce_fusion.1.order_ref, s32[60]{0:T(128)} %select_reduce_fusion.4.source_ref, bf16[60,128,128]{2,1,0:T(8,128)(2,1)} %bitcast.11, ...), custom_call_target="tpu_custom_call" | custom-call | tf_op jit(solution)/shard_map/admit/pallas_call | solution.py:91
  134.5 2.2 collective-permute-start
  136.6 1.8 collective-permute-done.3.refs_16_
  138.5 0.9 collective-permute-start.14
  139.4 4.0 %collective-permute-start.17 = (bf16[18,128,128]{2,1,0:T(8,128)(2,1)}, bf16[18,128,128]{2,1,0:T(8,128)(2,1)S(1)}, u32[]{:S(2)}, u32[]{:S(2)}) collective-permute-start(bf16[18,128,128]{2,1,0:T(8,128)(2,1)} %get-tuple-element.31.refs_0_), channel_id=1, source_target_pairs={{0,3},{1,2},{2,1},{3,0},{4,7},{5,6},{6,5},{7,4},{8,11},{9,10},{10,... | collective-permute-start | bytes 1769480 | tf_op jit(solution)/shard_map/ppermute | solution.py:407
  143.5 15.5 %collective-permute-done.6.refs_8_ = bf16[24,128,128]{2,1,0:T(8,128)(2,1)S(1)} collective-permute-done((bf16[24,128,128]{2,1,0:T(8,128)(2,1)}, bf16[24,128,128]{2,1,0:T(8,128)(2,1)S(1)}, u32[]{:S(2)}, u32[]{:S(2)}) %collective-permute-start.6) | collective-permute-done | bytes 786464 | tf_op jit(solution)/shard_map/ppermute | solution.py:407
  159.0 1.8 collective-permute-start.7
  160.8 0.9 collective-permute-start.16
  161.6 0.7 collective-permute-start.1
  162.4 9.2 %collective-permute-done.17.refs_6_ = bf16[18,128,128]{2,1,0:T(8,128)(2,1)S(1)} collective-permute-done((bf16[18,128,128]{2,1,0:T(8,128)(2,1)}, bf16[18,128,128]{2,1,0:T(8,128)(2,1)S(1)}, u32[]{:S(2)}, u32[]{:S(2)}) %collective-permute-start.17) | collective-permute-done | bytes 589856 | tf_op jit(solution)/shard_map/ppermute | solution.py:407
  171.6 1.8 collective-permute-start.22
  173.4 10.8 %collective-permute-done.4.refs_10_ = bf16[18,128,128]{2,1,0:T(8,128)(2,1)S(1)} collective-permute-done((bf16[18,128,128]{2,1,0:T(8,128)(2,1)S(1)}, bf16[18,128,128]{2,1,0:T(8,128)(2,1)S(1)}, u32[]{:S(2)}, u32[]{:S(2)}) %collective-permute-start.4) | collective-permute-done | bytes 589856 | tf_op jit(solution)/shard_map/ppermute | solution.py:407
  184.8 11.5 %collective-permute-done.1.refs_9_ = bf16[18,128,128]{2,1,0:T(8,128)(2,1)S(1)} collective-permute-done((bf16[18,128,128]{2,1,0:T(8,128)(2,1)S(1)}, bf16[18,128,128]{2,1,0:T(8,128)(2,1)S(1)}, u32[]{:S(2)}, u32[]{:S(2)}) %collective-permute-start.1) | collective-permute-done | bytes 589856 | tf_op jit(solution)/shard_map/ppermute | solution.py:407
  196.7 1.2 collective-permute-start.5
  198.1 1.3 collective-permute-start.8
  199.4 2.4 collective-permute-start.13
  201.8 13.0 %collective-permute-done.5.refs_1_ = bf16[18,128,128]{2,1,0:T(8,128)(2,1)S(1)} collective-permute-done((bf16[18,128,128]{2,1,0:T(8,128)(2,1)S(1)}, bf16[18,128,128]{2,1,0:T(8,128)(2,1)S(1)}, u32[]{:S(2)}, u32[]{:S(2)}) %collective-permute-start.5) | collective-permute-done | bytes 589856 | tf_op jit(solution)/shard_map/ppermute | solution.py:407
  214.8 12.6 %collective-permute-done.2.refs_0_ = bf16[18,128,128]{2,1,0:T(8,128)(2,1)S(1)} collective-permute-done((bf16[18,128,128]{2,1,0:T(8,128)(2,1)S(1)}, bf16[18,128,128]{2,1,0:T(8,128)(2,1)S(1)}, u32[]{:S(2)}, u32[]{:S(2)}) %collective-permute-start.2) | collective-permute-done | bytes 589856 | tf_op jit(solution)/shard_map/ppermute | solution.py:407
  227.5 1.5 collective-permute-start.10
  229.0 11.1 %collective-permute-done.8.refs_2_ = bf16[18,128,128]{2,1,0:T(8,128)(2,1)S(1)} collective-permute-done((bf16[18,128,128]{2,1,0:T(8,128)(2,1)S(1)}, bf16[18,128,128]{2,1,0:T(8,128)(2,1)S(1)}, u32[]{:S(2)}, u32[]{:S(2)}) %collective-permute-start.8) | collective-permute-done | bytes 589856 | tf_op jit(solution)/shard_map/ppermute | solution.py:407
  240.1 1.5 collective-permute-start.9
  241.7 1.1 copy-done.1
  242.8 1.1 copy-done.2
  243.9 8.8 %square_near.1 = (bf16[2304,384]{1,0:T(8,128)(2,1)S(1)}, bf16[1536,384]{1,0:T(8,128)(2,1)S(1)}, bf16[1536,384]{1,0:T(8,128)(2,1)S(1)}, bf16[2304,384]{1,0:T(8,12...) custom-call(s32[729]{0:T(1024)S(1)} %reshape.495.pos_ref, ...), custom_call_target="tpu_custom_call" | custom-call | tf_op jit(solution)/shard_map/square_near/pallas_call | solution.py:175
  252.7 12.6 %collective-permute-done.12.refs_6_ = bf16[18,128,128]{2,1,0:T(8,128)(2,1)S(1)} collective-permute-done((bf16[18,128,128]{2,1,0:T(8,128)(2,1)S(1)}, bf16[18,128,128]{2,1,0:T(8,128)(2,1)S(1)}, u32[]{:S(2)}, u32[]{:S(2)}) %collective-permute-start.12) | collective-permute-done | bytes 589856 | tf_op jit(solution)/shard_map/ppermute | solution.py:407
  265.4 13.0 %purify_far.1 = f32[60,128,128]{2,1,0:T(8,128)} custom-call(s32[729]{0:T(1024)S(1)} %reshape.495.pos_ref, s32[81]{0:T(128)S(1)} %reshape.496.slot_ref, bf16[18,128,128]{2,1,0:T(8,128)(2,1)S(1)} %collective-permute-done.2.refs_0_, bf16[18,128,128]{2,1,0:T(8,128)(2,1)S(1)} %collective-permute-done.5.refs_1_, ...), custom_call_target="tpu_custom_call" | custom-call | tf_op jit(solution)/shard_map/purify_far/pallas_call | solution.py:271
  (77 shorter events, 7.2 us)
Async XLA Ops:
  4.4 12.1 %copy-start.4 = (s32[32,4,3,20]{0,1,3,2:T(4,128)S(1)}, s32[32,4,3,20]{0,1,3,2:T(4,128)}, u32[]{:S(2)}) copy-start(s32[32,4,3,20]{0,1,3,2:T(4,128)} %param.6) | copy-start | bytes 92164
  4.4 14.6 %copy-start.3 = (s32[12288]{0:T(1024)S(1)}, s32[12288]{0:T(1024)}, u32[]{:S(2)}) copy-start(s32[12288]{0:T(1024)} %owner_ref.1) | copy-start | bytes 147460
  4.4 111.4 %all-to-all-start = ((bf16[128,2,128,128]{3,2,1,0:T(8,128)(2,1)}), bf16[128,2,128,128]{3,2,1,0:T(8,128)(2,1)}, u32[]{:S(2)}, u32[]{:S(2)}) async-start(bf16[128,2,128,128]{3,2,1,0:T(8,128)(2,1)} %bitcast.9), calls=%async_computation | async-start | bytes 16777216 | tf_op jit(solution)/shard_map/all_to_all | solution.py:356
  16.4 3.0 %copy-start.5 = (s32[12288]{0:T(1024)S(1)}, s32[12288]{0:T(1024)}, u32[]{:S(2)}) copy-start(s32[12288]{0:T(1024)} %param.9) | copy-start | bytes 147460
  121.2 120.4 %copy-start = (bf16[18,128,128]{2,1,0:T(8,128)(2,1)S(1)}, bf16[18,128,128]{2,1,0:T(8,128)(2,1)}, u32[]{:S(2)}) copy-start(bf16[18,128,128]{2,1,0:T(8,128)(2,1)} %admit.3.refs_1_) | copy-start | bytes 1769476
  121.2 17.2 %collective-permute-start.3 = (bf16[18,128,128]{2,1,0:T(8,128)(2,1)}, bf16[18,128,128]{2,1,0:T(8,128)(2,1)S(1)}, u32[]{:S(2)}, u32[]{:S(2)}) collective-permute-start(bf16[18,128,128]{2,1,0:T(8,128)(2,1)} %admit.3.refs_1_), channel_id=1, source_target_pairs={{0,7},{1,6},{2,5},{3,4},{4,3},{5,2},{6,1},{7,0},{8,15},{9,14},{10,... | collective-permute-start | bytes 1769480 | tf_op jit(solution)/shard_map/ppermute | solution.py:407
  124.6 14.8 %collective-permute-start.15 = (bf16[18,128,128]{2,1,0:T(8,128)(2,1)}, bf16[18,128,128]{2,1,0:T(8,128)(2,1)S(1)}, u32[]{:S(2)}, u32[]{:S(2)}) collective-permute-start(bf16[18,128,128]{2,1,0:T(8,128)(2,1)} %admit.3.refs_1_), channel_id=1, source_target_pairs={{0,1},{1,0},{2,3},{3,2},{4,5},{5,4},{6,7},{7,6},{8,9},{9,8},{10,11... | collective-permute-start | bytes 1769480 | tf_op jit(solution)/shard_map/ppermute | solution.py:407
  124.8 18.5 %collective-permute-start.18 = (bf16[18,128,128]{2,1,0:T(8,128)(2,1)}, bf16[18,128,128]{2,1,0:T(8,128)(2,1)S(1)}, u32[]{:S(2)}, u32[]{:S(2)}) collective-permute-start(bf16[18,128,128]{2,1,0:T(8,128)(2,1)} %admit.3.refs_1_), channel_id=1, source_target_pairs={{0,3},{1,2},{2,1},{3,0},{4,7},{5,6},{6,5},{7,4},{8,11},{9,10},{10,... | collective-permute-start | bytes 1769480 | tf_op jit(solution)/shard_map/ppermute | solution.py:407
  134.4 24.6 %collective-permute-start.6 = (bf16[24,128,128]{2,1,0:T(8,128)(2,1)}, bf16[24,128,128]{2,1,0:T(8,128)(2,1)S(1)}, u32[]{:S(2)}, u32[]{:S(2)}) collective-permute-start(bf16[24,128,128]{2,1,0:T(8,128)(2,1)} %get-tuple-element.32.refs_2_), channel_id=1, source_target_pairs={{0,3},{1,2},{2,1},{3,0},{4,7},{5,6},{6,5},{7,4},{8,11},{9,10},{10,... | collective-permute-start | bytes 2359304 | tf_op jit(solution)/shard_map/ppermute | solution.py:407
  134.5 26.3 %collective-permute-start = (bf16[18,128,128]{2,1,0:T(8,128)(2,1)}, bf16[18,128,128]{2,1,0:T(8,128)(2,1)S(1)}, u32[]{:S(2)}, u32[]{:S(2)}) collective-permute-start(bf16[18,128,128]{2,1,0:T(8,128)(2,1)} %get-tuple-element.31.refs_0_), channel_id=1, source_target_pairs={{0,7},{1,6},{2,5},{3,4},{4,3},{5,2},{6,1},{7,0},{8,15},{9,14},{10,... | collective-permute-start | bytes 1769480 | tf_op jit(solution)/shard_map/ppermute | solution.py:407
  138.5 23.2 %collective-permute-start.14 = (bf16[18,128,128]{2,1,0:T(8,128)(2,1)}, bf16[18,128,128]{2,1,0:T(8,128)(2,1)S(1)}, u32[]{:S(2)}, u32[]{:S(2)}) collective-permute-start(bf16[18,128,128]{2,1,0:T(8,128)(2,1)} %get-tuple-element.31.refs_0_), channel_id=1, source_target_pairs={{0,1},{1,0},{2,3},{3,2},{4,5},{5,4},{6,7},{7,6},{8,9},{9,8},{10,11... | collective-permute-start | bytes 1769480 | tf_op jit(solution)/shard_map/ppermute | solution.py:407
  139.4 32.2 %collective-permute-start.17 = (bf16[18,128,128]{2,1,0:T(8,128)(2,1)}, bf16[18,128,128]{2,1,0:T(8,128)(2,1)S(1)}, u32[]{:S(2)}, u32[]{:S(2)}) collective-permute-start(bf16[18,128,128]{2,1,0:T(8,128)(2,1)} %get-tuple-element.31.refs_0_), channel_id=1, source_target_pairs={{0,3},{1,2},{2,1},{3,0},{4,7},{5,6},{6,5},{7,4},{8,11},{9,10},{10,... | collective-permute-start | bytes 1769480 | tf_op jit(solution)/shard_map/ppermute | solution.py:407
  143.4 40.9 %collective-permute-start.4 = (bf16[18,128,128]{2,1,0:T(8,128)(2,1)S(1)}, bf16[18,128,128]{2,1,0:T(8,128)(2,1)S(1)}, u32[]{:S(2)}, u32[]{:S(2)}) collective-permute-start(bf16[18,128,128]{2,1,0:T(8,128)(2,1)S(1)} %collective-permute-done.3.refs_16_), channel_id=1, source_target_pairs={{0,3},{1,2},{2,1},{3,0},{4,7},{5,6},{6,5},{7,4},{8,11},{9,10},{10,... | collective-permute-start | bytes 1769480 | tf_op jit(solution)/shard_map/ppermute | solution.py:407
  159.0 25.3 %collective-permute-start.7 = (bf16[24,128,128]{2,1,0:T(8,128)(2,1)S(1)}, bf16[24,128,128]{2,1,0:T(8,128)(2,1)S(1)}, u32[]{:S(2)}, u32[]{:S(2)}) collective-permute-start(bf16[24,128,128]{2,1,0:T(8,128)(2,1)S(1)} %collective-permute-done.6.refs_8_), channel_id=1, source_target_pairs={{0,7},{1,6},{2,5},{3,4},{4,3},{5,2},{6,1},{7,0},{8,15},{9,14},{10,... | collective-permute-start | bytes 2359304 | tf_op jit(solution)/shard_map/ppermute | solution.py:407
  160.8 37.1 %collective-permute-start.16 = (bf16[24,128,128]{2,1,0:T(8,128)(2,1)}, bf16[24,128,128]{2,1,0:T(8,128)(2,1)S(1)}, u32[]{:S(2)}, u32[]{:S(2)}) collective-permute-start(bf16[24,128,128]{2,1,0:T(8,128)(2,1)} %get-tuple-element.32.refs_2_), channel_id=1, source_target_pairs={{0,1},{1,0},{2,3},{3,2},{4,5},{5,4},{6,7},{7,6},{8,9},{9,8},{10,11... | collective-permute-start | bytes 2359304 | tf_op jit(solution)/shard_map/ppermute | solution.py:407
  161.6 34.7 %collective-permute-start.1 = (bf16[18,128,128]{2,1,0:T(8,128)(2,1)S(1)}, bf16[18,128,128]{2,1,0:T(8,128)(2,1)S(1)}, u32[]{:S(2)}, u32[]{:S(2)}) collective-permute-start(bf16[18,128,128]{2,1,0:T(8,128)(2,1)S(1)} %collective-permute-done.refs_15_), channel_id=1, source_target_pairs={{0,3},{1,2},{2,1},{3,0},{4,7},{5,6},{6,5},{7,4},{8,11},{9,10},{10,... | collective-permute-start | bytes 1769480 | tf_op jit(solution)/shard_map/ppermute | solution.py:407
  171.6 25.1 %collective-permute-start.22 = (bf16[18,128,128]{2,1,0:T(8,128)(2,1)}, bf16[18,128,128]{2,1,0:T(8,128)(2,1)S(1)}, u32[]{:S(2)}, u32[]{:S(2)}) collective-permute-start(bf16[18,128,128]{2,1,0:T(8,128)(2,1)} %get-tuple-element.33), channel_id=1, source_target_pairs={{0,7},{1,6},{2,5},{3,4},{4,3},{5,2},{6,1},{7,0},{8,15},{9,14},{10,... | collective-permute-start | bytes 1769480 | tf_op jit(solution)/shard_map/ppermute | solution.py:407
  184.2 13.9 %collective-permute-start.20 = (bf16[18,128,128]{2,1,0:T(8,128)(2,1)S(1)}, bf16[18,128,128]{2,1,0:T(8,128)(2,1)S(1)}, u32[]{:S(2)}, u32[]{:S(2)}) collective-permute-start(bf16[18,128,128]{2,1,0:T(8,128)(2,1)S(1)} %collective-permute-done.4.refs_10_), channel_id=1, source_target_pairs={{0,1},{1,0},{2,3},{3,2},{4,5},{5,4},{6,7},{7,6},{8,9},{9,8},{10,11... | collective-permute-start | bytes 1769480 | tf_op jit(solution)/shard_map/ppermute | solution.py:407
  184.2 57.4 %collective-permute-start.21 = (bf16[24,128,128]{2,1,0:T(8,128)(2,1)S(1)}, bf16[24,128,128]{2,1,0:T(8,128)(2,1)S(1)}, u32[]{:S(2)}, u32[]{:S(2)}) collective-permute-start(bf16[24,128,128]{2,1,0:T(8,128)(2,1)S(1)} %collective-permute-done.7.refs_11_), channel_id=1, source_target_pairs={{0,1},{1,0},{2,3},{3,2},{4,5},{5,4},{6,7},{7,6},{8,9},{9,8},{10,11... | collective-permute-start | bytes 2359304 | tf_op jit(solution)/shard_map/ppermute | solution.py:407
  196.3 3.1 %collective-permute-start.19 = (bf16[18,128,128]{2,1,0:T(8,128)(2,1)S(1)}, bf16[18,128,128]{2,1,0:T(8,128)(2,1)S(1)}, u32[]{:S(2)}, u32[]{:S(2)}) collective-permute-start(bf16[18,128,128]{2,1,0:T(8,128)(2,1)S(1)} %collective-permute-done.1.refs_9_), channel_id=1, source_target_pairs={{0,1},{1,0},{2,3},{3,2},{4,5},{5,4},{6,7},{7,6},{8,9},{9,8},{10,11... | collective-permute-start | bytes 1769480 | tf_op jit(solution)/shard_map/ppermute | solution.py:407
  196.7 18.1 %collective-permute-start.5 = (bf16[18,128,128]{2,1,0:T(8,128)(2,1)S(1)}, bf16[18,128,128]{2,1,0:T(8,128)(2,1)S(1)}, u32[]{:S(2)}, u32[]{:S(2)}) collective-permute-start(bf16[18,128,128]{2,1,0:T(8,128)(2,1)S(1)} %collective-permute-done.4.refs_10_), channel_id=1, source_target_pairs={{0,8},{1,9},{2,10},{3,11},{4,124},{5,125},{6,126},{7,127},{8,16},{... | collective-permute-start | bytes 1769480 | tf_op jit(solution)/shard_map/ppermute | solution.py:407
  197.9 29.5 %collective-permute-start.2 = (bf16[18,128,128]{2,1,0:T(8,128)(2,1)S(1)}, bf16[18,128,128]{2,1,0:T(8,128)(2,1)S(1)}, u32[]{:S(2)}, u32[]{:S(2)}) collective-permute-start(bf16[18,128,128]{2,1,0:T(8,128)(2,1)S(1)} %collective-permute-done.1.refs_9_), channel_id=1, source_target_pairs={{0,8},{1,9},{2,10},{3,11},{4,124},{5,125},{6,126},{7,127},{8,16},{... | collective-permute-start | bytes 1769480 | tf_op jit(solution)/shard_map/ppermute | solution.py:407
  198.1 42.0 %collective-permute-start.8 = (bf16[18,128,128]{2,1,0:T(8,128)(2,1)S(1)}, bf16[18,128,128]{2,1,0:T(8,128)(2,1)S(1)}, u32[]{:S(2)}, u32[]{:S(2)}) collective-permute-start(bf16[18,128,128]{2,1,0:T(8,128)(2,1)S(1)} %slice.20), channel_id=1, source_target_pairs={{0,8},{1,9},{2,10},{3,11},{4,124},{5,125},{6,126},{7,127},{8,16},{... | collective-permute-start | bytes 1769480 | tf_op jit(solution)/shard_map/ppermute | solution.py:407
  199.4 53.3 %collective-permute-start.13 = (bf16[18,128,128]{2,1,0:T(8,128)(2,1)S(1)}, bf16[18,128,128]{2,1,0:T(8,128)(2,1)S(1)}, u32[]{:S(2)}, u32[]{:S(2)}) collective-permute-start(bf16[18,128,128]{2,1,0:T(8,128)(2,1)S(1)} %collective-permute-done.3.refs_16_), channel_id=1, source_target_pairs={{0,8},{1,9},{2,10},{3,11},{4,124},{5,125},{6,126},{7,127},{8,16},{... | collective-permute-start | bytes 1769480 | tf_op jit(solution)/shard_map/ppermute | solution.py:407
  214.8 50.6 %collective-permute-start.12 = (bf16[18,128,128]{2,1,0:T(8,128)(2,1)S(1)}, bf16[18,128,128]{2,1,0:T(8,128)(2,1)S(1)}, u32[]{:S(2)}, u32[]{:S(2)}) collective-permute-start(bf16[18,128,128]{2,1,0:T(8,128)(2,1)S(1)} %collective-permute-done.refs_15_), channel_id=1, source_target_pairs={{0,8},{1,9},{2,10},{3,11},{4,124},{5,125},{6,126},{7,127},{8,16},{... | collective-permute-start | bytes 1769480 | tf_op jit(solution)/shard_map/ppermute | solution.py:407
  227.5 37.9 %collective-permute-start.10 = (bf16[18,128,128]{2,1,0:T(8,128)(2,1)S(1)}, bf16[18,128,128]{2,1,0:T(8,128)(2,1)S(1)}, u32[]{:S(2)}, u32[]{:S(2)}) collective-permute-start(bf16[18,128,128]{2,1,0:T(8,128)(2,1)S(1)} %collective-permute-done.5.refs_1_), channel_id=1, source_target_pairs={{0,1},{1,0},{2,3},{3,2},{4,5},{5,4},{6,7},{7,6},{8,9},{9,8},{10,11... | collective-permute-start | bytes 1769480 | tf_op jit(solution)/shard_map/ppermute | solution.py:407
  240.1 25.3 %collective-permute-start.9 = (bf16[18,128,128]{2,1,0:T(8,128)(2,1)S(1)}, bf16[18,128,128]{2,1,0:T(8,128)(2,1)S(1)}, u32[]{:S(2)}, u32[]{:S(2)}) collective-permute-start(bf16[18,128,128]{2,1,0:T(8,128)(2,1)S(1)} %collective-permute-done.2.refs_0_), channel_id=1, source_target_pairs={{0,1},{1,0},{2,3},{3,2},{4,5},{5,4},{6,7},{7,6},{8,9},{9,8},{10,11... | collective-permute-start | bytes 1769480 | tf_op jit(solution)/shard_map/ppermute | solution.py:407
  241.6 23.7 %collective-permute-start.11 = (bf16[18,128,128]{2,1,0:T(8,128)(2,1)S(1)}, bf16[18,128,128]{2,1,0:T(8,128)(2,1)S(1)}, u32[]{:S(2)}, u32[]{:S(2)}) collective-permute-start(bf16[18,128,128]{2,1,0:T(8,128)(2,1)S(1)} %collective-permute-done.8.refs_2_), channel_id=1, source_target_pairs={{0,1},{1,0},{2,3},{3,2},{4,5},{5,4},{6,7},{7,6},{8,9},{9,8},{10,11... | collective-permute-start | bytes 1769480 | tf_op jit(solution)/shard_map/ppermute | solution.py:407
  241.7 1.1 copy-start.1
  242.8 1.1 copy-start.2

commit v5 on v4

--- a/solution.py
+++ b/solution.py
@@ -10,7 +10,9 @@
 C = 2
 
 
-def pack_kernel(base_ref, owner_ref, ent_ref, out_ref, staged, seen, load_sems, store_sem):
+def pack_kernel(
+    base_ref, owner_ref, ent_ref, out_ref, staged, seen, slots, load_sems, store_sem
+):
     count = ent_ref.shape[0]
     parts = load_sems.shape[0]
     size = count // parts
@@ -24,18 +26,22 @@
         seen[i] = 0
         return carry
 
-    def issue(i, carry):
+    def count_rank(i, carry):
         owner = owner_ref[base_ref[0] + i]
         rank = seen[owner]
         seen[owner] = rank + 1
-        slot = owner * C + rank
-        pltpu.make_async_copy(staged.at[i], out_ref.at[slot], store_sem).start()
+        slots[i] = owner * C + rank
         return carry
 
+    def issue(i, carry):
+        pltpu.make_async_copy(staged.at[i], out_ref.at[slots[i]], store_sem).start()
+        return carry
+
     lax.fori_loop(0, seen.shape[0], clear, 0, unroll=8)
+    lax.fori_loop(0, count, count_rank, 0, unroll=4)
     for p in range(parts):
         loads[p].wait()
-        lax.fori_loop(p * size, (p + 1) * size, issue, 0)
+        lax.fori_loop(p * size, (p + 1) * size, issue, 0, unroll=4)
     pltpu.make_async_copy(staged, out_ref.at[pl.ds(0, count)], store_sem).wait()
 
 
@@ -54,6 +60,7 @@
         scratch_shapes=[
             pltpu.VMEM(ent_blocks.shape, ent_blocks.dtype),
             pltpu.SMEM((device_count,), jnp.int32),
+            pltpu.SMEM((ent_blocks.shape[0],), jnp.int32),
             pltpu.SemaphoreType.DMA((4,)),
             pltpu.SemaphoreType.DMA,
         ],
@@ -117,6 +124,10 @@
 
 def near_count(part):
     return len([q for q in reach(part) if q < NEAR_PARTS])
+
+
+def inner_count(part):
+    return len([q for q in reach(part) if q < 3])
 
 
 def far_count(part):
@@ -197,12 +208,31 @@
     pieces = refs[: len(piece_starts)]
     outs = refs[len(piece_starts):]
     near_grids = outs[:9]
-    square_in, left, out_ref, table, grid, square, square_b, staged, sems, out_sem = outs[9:]
+    square_in, left, out_ref, table, grid, square, square_b, early, staged, sems, out_sem = outs[9:]
     near = 9 * row_count
     group = row_count * width
     zero_at = table_start + table_size
     copies = load_pieces(pieces, piece_starts, table, sems)
     table[table_size] = jnp.zeros((width, width), table.dtype)
+    middle = (3, 4, 5)
+
+    def mask(part, product):
+        for r in range(row_count):
+            for k in range(row_count):
+                listed = pos_ref[r * near + part * row_count + k] != zero_at
+                low = part * group + k * width
+                square_b[r * width:(r + 1) * width, low:low + width] = jnp.where(
+                    listed, product[r * width:(r + 1) * width, k * width:(k + 1) * width], 0.0
+                ).astype(jnp.bfloat16)
+
+    for part in middle:
+        mask(part, square_in[part])
+    for part in range(NEAR_PARTS):
+        early[part] = jnp.dot(
+            lanes_of(square_b, [q for q in reach(part) if q in middle], group),
+            near_grids[part][inner_count(part) * group:],
+            preferred_element_type=jnp.float32,
+        )
     for copy in copies:
         copy.wait()
 
@@ -225,23 +255,21 @@
                 preferred_element_type=jnp.float32,
             )
         square[part] = product
-        for r in range(row_count):
-            for k in range(row_count):
-                listed = pos_ref[r * near + part * row_count + k] != zero_at
-                low = part * group + k * width
-                square_b[r * width:(r + 1) * width, low:low + width] = jnp.where(
-                    listed, product[r * width:(r + 1) * width, k * width:(k + 1) * width], 0.0
-                ).astype(jnp.bfloat16)
+        if part not in middle:
+            mask(part, product)
 
     blocks = out_ref.shape[0]
     for part in range(9):
         parts = reach(part)
         base = near_count(part)
         far_base = sum(far_count(q) for q in range(part)) * group
+        inner = inner_count(part)
         product = jnp.dot(
-            lanes_of(square_b, parts[:base], group), near_grids[part][...],
+            lanes_of(square_b, parts[:inner], group), near_grids[part][:inner * group],
             preferred_element_type=jnp.float32,
         )
+        if part < NEAR_PARTS:
+            product = product + early[part]
         if base < len(parts):
             product = product + jnp.dot(
                 lanes_of(square_b, parts[base:], group),
@@ -282,6 +310,7 @@
             pltpu.VMEM((sum(far_count(part) for part in range(9)) * group, group), jnp.bfloat16),
             pltpu.VMEM((9, group, group), jnp.float32),
             pltpu.VMEM((group, span), jnp.bfloat16),
+            pltpu.VMEM((NEAR_PARTS, group, group), jnp.float32),
             pltpu.VMEM((blocks + 1, width, width), jnp.float32),
             pltpu.SemaphoreType.DMA((len(pieces),)),
             pltpu.SemaphoreType.DMA,
@@ -425,7 +454,7 @@
     far_across_1 = send(ring_across_1, onward)
     ring_same_1 = send(ring_across_1, across)
     own_chip_1 = send(own_1, chip)
-    far_across_2 = send(ring_across_2, onward)
+    far_across_2 = send(ring_across_2[:cut // 2], onward)
     ring_same_2 = send(ring_across_2, across)
     ring_same_3 = send(own_across_3, ring)
     ring_across_t = send(own_t, ring)
@@ -438,6 +467,7 @@
     ring_chip_3 = send(ring_same_3, chip)
     far_same_2 = send(ring_same_2, onward)
     ring_chip_2 = send(ring_same_2, chip)
+    far_across_3 = send(ring_across_2[cut // 2:], onward)
     far_chip_1 = send(far_same_1, chip)
     far_chip_3 = send(far_same_3, chip)
     far_chip_2 = send(far_same_2, chip)
@@ -453,7 +483,7 @@
     far_pieces = [
         (far_same_1, 6, 0), (far_same_2, 6, cut), (far_same_3, 6, 2 * cut),
         (far_chip_1, 7, 0), (far_chip_2, 7, cut), (far_chip_3, 7, 2 * cut),
-        (far_across_1, 8, 0), (far_across_2, 8, cut),
+        (far_across_1, 8, 0), (far_across_2, 8, cut), (far_across_3, 8, cut + cut // 2),
     ]
     far_start = starts[NEAR_PARTS]
     carried = square_near(

time: 279 us -> 273 us (0.978)
  waiting for transfers between devices: 192 us -> 189 us
    ppermute x23 -> x24, waiting for transfers between devices: 98.3 us -> 95.6 us  [send(): return lax.ppermute(array, axes, pairs)]
    ppermute x23 -> x24, starting transfers between devices: 28 us -> 25.8 us  [send(): return lax.ppermute(array, axes, pairs)]
  transfers between devices with their start and end apart: 24 -> 25, of which waited for: 10 -> 11; matrix products, arithmetic and copies ran while one was open for 2% -> 2% of each run, Pallas kernels for 6% -> 5%
where the time goes in v5:
time: 273 us; the launch traced here: 272 us
  waiting for transfers between devices  189 us (69%)
  Pallas kernels  38.8 us (14%)
  starting transfers between devices  37.8 us (14%)
  other arithmetic  3.34 us (1%)
    ppermute x24, waiting for transfers between devices, send(): return lax.ppermute(array, axes, pairs)  95.6 us
    all_to_all x1, waiting for transfers between devices, per_device(): lax.all_to_all(outgoing.reshape(device_count, C, width, width), ('gx', 'g...  93.6 us
    ppermute x24, starting transfers between devices, send(): return lax.ppermute(array, axes, pairs)  25.8 us
    pallas_call x1, Pallas kernels, purify_far(): pl.pallas_call(functools.partial(far_kernel, row_count, width, piece_star...  13.4 us
    pallas_call x2, Pallas kernels, admit(): pl.pallas_call(functools.partial(admit_kernel, spans), out_shape=[jax.Sha...  12.1 us
    all_to_all x1, starting transfers between devices, per_device(): lax.all_to_all(outgoing.reshape(device_count, C, width, width), ('gx', 'g...  12 us
    pallas_call x1, Pallas kernels, square_near(): pl.pallas_call(functools.partial(near_kernel, row_count, width, piece_sta...  9.07 us
  transfers between devices with their start and end apart: 25, of which 11 were waited for; matrix products, arithmetic and copies ran while one was open for 2% of the time, Pallas kernels for 5%

profile of v5, /device:TPU:1, one launch (start us, length us, event | category | flops | bytes accessed | tf_op | source)
XLA Modules:
  0.0 272.0 jit_solution(2000852026715238027)
XLA Ops:
  0.0 4.3 %pack.1 = bf16[256,128,128]{2,1,0:T(8,128)(2,1)} custom-call(s32[1]{0:T(128)} %bitcast.base_ref, s32[12288]{0:T(1024)} %owner_ref.1, bf16[96,128,128]{2,1,0:T(8,128)(2,1)} %ent_ref.1), custom_call_target="tpu_custom_call" | custom-call | tf_op jit(solution)/shard_map/pack/pallas_call | solution.py:49
  4.3 12.0 %all-to-all-start = ((bf16[128,2,128,128]{3,2,1,0:T(8,128)(2,1)}), bf16[128,2,128,128]{3,2,1,0:T(8,128)(2,1)}, u32[]{:S(2)}, u32[]{:S(2)}) async-start(bf16[128,2,128,128]{3,2,1,0:T(8,128)(2,1)} %bitcast.9), calls=%async_computation | async-start | bytes 16777216 | tf_op jit(solution)/shard_map/all_to_all | solution.py:385
  16.8 0.6 gather_fusion
  18.2 0.3 select_reduce_fusion
  19.8 0.7 select_reduce_fusion.4.source_ref
  20.5 0.7 convert_reduce_fusion.2.first_ref
  21.4 0.7 select_reduce_fusion.1.order_ref
  22.1 93.6 %all-to-all-done = bf16[128,2,128,128]{3,2,1,0:T(8,128)(2,1)} async-done(((bf16[128,2,128,128]{3,2,1,0:T(8,128)(2,1)}), bf16[128,2,128,128]{3,2,1,0:T(8,128)(2,1)}, u32[]{:S(2)}, u32[]{:S(2)}) %all-to-all-start) | async-done | bytes 8388640 | tf_op jit(solution)/shard_map/all_to_all | solution.py:385
  115.7 6.7 %admit.2 = (bf16[18,128,128]{2,1,0:T(8,128)(2,1)}, bf16[24,128,128]{2,1,0:T(8,128)(2,1)}, bf16[18,128,128]{2,1,0:T(8,128)(2,1)}) custom-call(s32[61]{0:T(128)} %convert_reduce_fusion.2.first_ref, s32[256]{0:T(256)} %select_reduce_fusion.1.order_ref, s32[60]{0:T(128)} %select_reduce_fusion.4.source_ref, bf16[60,128,128]{2,1,0:T(8,128)(2,1)} %bitcast.10, ...), custom_call_target="tpu_custom_call" | custom-call | tf_op jit(solution)/shard_map/admit/pallas_call | solution.py:98
  122.4 6.2 %collective-permute-start.6 = (bf16[24,128,128]{2,1,0:T(8,128)(2,1)}, bf16[24,128,128]{2,1,0:T(8,128)(2,1)S(1)}, u32[]{:S(2)}, u32[]{:S(2)}) collective-permute-start(bf16[24,128,128]{2,1,0:T(8,128)(2,1)} %get-tuple-element.32.refs_2_), channel_id=1, source_target_pairs={{0,3},{1,2},{2,1},{3,0},{4,7},{5,6},{6,5},{7,4},{8,11},{9,10},{10,... | collective-permute-start | bytes 2359304 | tf_op jit(solution)/shard_map/ppermute | solution.py:436
  128.6 5.4 %admit.3.refs_1_ = bf16[18,128,128]{2,1,0:T(8,128)(2,1)} custom-call(s32[61]{0:T(128)} %convert_reduce_fusion.2.first_ref, s32[256]{0:T(256)} %select_reduce_fusion.1.order_ref, s32[60]{0:T(128)} %select_reduce_fusion.4.source_ref, bf16[60,128,128]{2,1,0:T(8,128)(2,1)} %bitcast.11, bf16[256,128,128]{2,1,0:T(8,128)(2,1)} %bitcast.2.received_ref), custom_call_target="tpu_custom_call" | custom-call | tf_op jit(solution)/shard_map/admit/pallas_call | solution.py:98
  134.3 2.8 %collective-permute-start = (bf16[18,128,128]{2,1,0:T(8,128)(2,1)S(1)}, bf16[18,128,128]{2,1,0:T(8,128)(2,1)S(1)}, u32[]{:S(2)}, u32[]{:S(2)}) collective-permute-start(bf16[18,128,128]{2,1,0:T(8,128)(2,1)S(1)} %copy-done.2), channel_id=1, source_target_pairs={{0,7},{1,6},{2,5},{3,4},{4,3},{5,2},{6,1},{7,0},{8,15},{9,14},{10,... | collective-permute-start | bytes 1769480 | tf_op jit(solution)/shard_map/ppermute | solution.py:436
  137.2 14.3 %collective-permute-done.3.refs_16_ = bf16[18,128,128]{2,1,0:T(8,128)(2,1)S(1)} collective-permute-done((bf16[18,128,128]{2,1,0:T(8,128)(2,1)}, bf16[18,128,128]{2,1,0:T(8,128)(2,1)S(1)}, u32[]{:S(2)}, u32[]{:S(2)}) %collective-permute-start.3) | collective-permute-done | bytes 589856 | tf_op jit(solution)/shard_map/ppermute | solution.py:436
  151.5 8.4 %collective-permute-done.19.refs_7_ = bf16[18,128,128]{2,1,0:T(8,128)(2,1)S(1)} collective-permute-done((bf16[18,128,128]{2,1,0:T(8,128)(2,1)}, bf16[18,128,128]{2,1,0:T(8,128)(2,1)S(1)}, u32[]{:S(2)}, u32[]{:S(2)}) %collective-permute-start.19) | collective-permute-done | bytes 589856 | tf_op jit(solution)/shard_map/ppermute | solution.py:436
  159.9 1.4 collective-permute-start.4
  161.3 1.2 collective-permute-done.refs_15_
  162.7 9.9 %collective-permute-done.18.refs_6_ = bf16[18,128,128]{2,1,0:T(8,128)(2,1)S(1)} collective-permute-done((bf16[18,128,128]{2,1,0:T(8,128)(2,1)S(1)}, bf16[18,128,128]{2,1,0:T(8,128)(2,1)S(1)}, u32[]{:S(2)}, u32[]{:S(2)}) %collective-permute-start.18) | collective-permute-done | bytes 589856 | tf_op jit(solution)/shard_map/ppermute | solution.py:436
  172.5 12.6 %collective-permute-done.4.refs_10_ = bf16[18,128,128]{2,1,0:T(8,128)(2,1)S(1)} collective-permute-done((bf16[18,128,128]{2,1,0:T(8,128)(2,1)S(1)}, bf16[18,128,128]{2,1,0:T(8,128)(2,1)S(1)}, u32[]{:S(2)}, u32[]{:S(2)}) %collective-permute-start.4) | collective-permute-done | bytes 589856 | tf_op jit(solution)/shard_map/ppermute | solution.py:436
  185.2 1.5 collective-permute-start.13
  186.7 9.8 %collective-permute-done.1.refs_9_ = bf16[18,128,128]{2,1,0:T(8,128)(2,1)S(1)} collective-permute-done((bf16[18,128,128]{2,1,0:T(8,128)(2,1)S(1)}, bf16[18,128,128]{2,1,0:T(8,128)(2,1)S(1)}, u32[]{:S(2)}, u32[]{:S(2)}) %collective-permute-start.1) | collective-permute-done | bytes 589856 | tf_op jit(solution)/shard_map/ppermute | solution.py:436
  196.5 1.2 collective-permute-start.5
  197.9 0.8 collective-permute-start.22
  198.7 4.3 %collective-permute-start.12 = (bf16[18,128,128]{2,1,0:T(8,128)(2,1)S(1)}, bf16[18,128,128]{2,1,0:T(8,128)(2,1)S(1)}, u32[]{:S(2)}, u32[]{:S(2)}) collective-permute-start(bf16[18,128,128]{2,1,0:T(8,128)(2,1)S(1)} %collective-permute-done.refs_15_), channel_id=1, source_target_pairs={{0,8},{1,9},{2,10},{3,11},{4,124},{5,125},{6,126},{7,127},{8,16},{... | collective-permute-start | bytes 1769480 | tf_op jit(solution)/shard_map/ppermute | solution.py:436
  203.0 11.2 %collective-permute-done.5.refs_1_ = bf16[18,128,128]{2,1,0:T(8,128)(2,1)S(1)} collective-permute-done((bf16[18,128,128]{2,1,0:T(8,128)(2,1)S(1)}, bf16[18,128,128]{2,1,0:T(8,128)(2,1)S(1)}, u32[]{:S(2)}, u32[]{:S(2)}) %collective-permute-start.5) | collective-permute-done | bytes 589856 | tf_op jit(solution)/shard_map/ppermute | solution.py:436
  214.2 2.3 collective-permute-start.10
  216.6 10.3 %collective-permute-done.2.refs_0_ = bf16[18,128,128]{2,1,0:T(8,128)(2,1)S(1)} collective-permute-done((bf16[18,128,128]{2,1,0:T(8,128)(2,1)S(1)}, bf16[18,128,128]{2,1,0:T(8,128)(2,1)S(1)}, u32[]{:S(2)}, u32[]{:S(2)}) %collective-permute-start.2) | collective-permute-done | bytes 589856 | tf_op jit(solution)/shard_map/ppermute | solution.py:436
  226.9 2.3 collective-permute-start.9
  229.2 10.3 %collective-permute-done.8.refs_2_ = bf16[18,128,128]{2,1,0:T(8,128)(2,1)S(1)} collective-permute-done((bf16[18,128,128]{2,1,0:T(8,128)(2,1)S(1)}, bf16[18,128,128]{2,1,0:T(8,128)(2,1)S(1)}, u32[]{:S(2)}, u32[]{:S(2)}) %collective-permute-start.8) | collective-permute-done | bytes 589856 | tf_op jit(solution)/shard_map/ppermute | solution.py:436
  239.5 2.3 collective-permute-start.11
  241.9 9.1 %square_near.1 = (bf16[2304,384]{1,0:T(8,128)(2,1)S(1)}, bf16[1536,384]{1,0:T(8,128)(2,1)S(1)}, bf16[1536,384]{1,0:T(8,128)(2,1)S(1)}, bf16[2304,384]{1,0:T(8,12...) custom-call(s32[729]{0:T(1024)S(1)} %reshape.495.pos_ref, ...), custom_call_target="tpu_custom_call" | custom-call | tf_op jit(solution)/shard_map/square_near/pallas_call | solution.py:186
  250.9 7.5 %collective-permute-done.14.refs_8_ = bf16[9,128,128]{2,1,0:T(8,128)(2,1)S(1)} collective-permute-done((bf16[9,128,128]{2,1,0:T(8,128)(2,1)S(1)}, bf16[9,128,128]{2,1,0:T(8,128)(2,1)S(1)}, u32[]{:S(2)}, u32[]{:S(2)}) %collective-permute-start.14) | collective-permute-done | bytes 294944 | tf_op jit(solution)/shard_map/ppermute | solution.py:436
  258.5 13.4 %purify_far.1 = f32[60,128,128]{2,1,0:T(8,128)} custom-call(s32[729]{0:T(1024)S(1)} %reshape.495.pos_ref, s32[81]{0:T(128)S(1)} %reshape.496.slot_ref, bf16[18,128,128]{2,1,0:T(8,128)(2,1)S(1)} %collective-permute-done.2.refs_0_, bf16[18,128,128]{2,1,0:T(8,128)(2,1)S(1)} %collective-permute-done.5.refs_1_, ...), custom_call_target="tpu_custom_call" | custom-call | tf_op jit(solution)/shard_map/purify_far/pallas_call | solution.py:299
  (82 shorter events, 3.4 us)
Async XLA Ops:
  4.3 12.1 %copy-start.4 = (s32[32,4,3,20]{0,1,3,2:T(4,128)S(1)}, s32[32,4,3,20]{0,1,3,2:T(4,128)}, u32[]{:S(2)}) copy-start(s32[32,4,3,20]{0,1,3,2:T(4,128)} %param.6) | copy-start | bytes 92164
  4.3 14.6 %copy-start.3 = (s32[12288]{0:T(1024)S(1)}, s32[12288]{0:T(1024)}, u32[]{:S(2)}) copy-start(s32[12288]{0:T(1024)} %owner_ref.1) | copy-start | bytes 147460
  4.3 111.4 %all-to-all-start = ((bf16[128,2,128,128]{3,2,1,0:T(8,128)(2,1)}), bf16[128,2,128,128]{3,2,1,0:T(8,128)(2,1)}, u32[]{:S(2)}, u32[]{:S(2)}) async-start(bf16[128,2,128,128]{3,2,1,0:T(8,128)(2,1)} %bitcast.9), calls=%async_computation | async-start | bytes 16777216 | tf_op jit(solution)/shard_map/all_to_all | solution.py:385
  16.3 3.0 %copy-start.5 = (s32[12288]{0:T(1024)S(1)}, s32[12288]{0:T(1024)}, u32[]{:S(2)}) copy-start(s32[12288]{0:T(1024)} %param.9) | copy-start | bytes 147460
  122.4 12.0 %copy-start.2 = (bf16[18,128,128]{2,1,0:T(8,128)(2,1)S(1)}, bf16[18,128,128]{2,1,0:T(8,128)(2,1)}, u32[]{:S(2)}) copy-start(bf16[18,128,128]{2,1,0:T(8,128)(2,1)} %get-tuple-element.31.refs_0_) | copy-start | bytes 1769476
  122.4 40.2 %copy-start.1 = (bf16[24,128,128]{2,1,0:T(8,128)(2,1)S(1)}, bf16[24,128,128]{2,1,0:T(8,128)(2,1)}, u32[]{:S(2)}) copy-start(bf16[24,128,128]{2,1,0:T(8,128)(2,1)} %get-tuple-element.32.refs_2_) | copy-start | bytes 2359300
  122.4 50.1 %copy-start.6 = (bf16[18,128,128]{2,1,0:T(8,128)(2,1)S(1)}, bf16[18,128,128]{2,1,0:T(8,128)(2,1)}, u32[]{:S(2)}) copy-start(bf16[18,128,128]{2,1,0:T(8,128)(2,1)} %get-tuple-element.33) | copy-start | bytes 1769476
  122.4 38.9 %collective-permute-start.6 = (bf16[24,128,128]{2,1,0:T(8,128)(2,1)}, bf16[24,128,128]{2,1,0:T(8,128)(2,1)S(1)}, u32[]{:S(2)}, u32[]{:S(2)}) collective-permute-start(bf16[24,128,128]{2,1,0:T(8,128)(2,1)} %get-tuple-element.32.refs_2_), channel_id=1, source_target_pairs={{0,3},{1,2},{2,1},{3,0},{4,7},{5,6},{6,5},{7,4},{8,11},{9,10},{10,... | collective-permute-start | bytes 2359304 | tf_op jit(solution)/shard_map/ppermute | solution.py:436
  134.0 107.8 %copy-start = (bf16[18,128,128]{2,1,0:T(8,128)(2,1)S(1)}, bf16[18,128,128]{2,1,0:T(8,128)(2,1)}, u32[]{:S(2)}) copy-start(bf16[18,128,128]{2,1,0:T(8,128)(2,1)} %admit.3.refs_1_) | copy-start | bytes 1769476
  134.0 17.4 %collective-permute-start.3 = (bf16[18,128,128]{2,1,0:T(8,128)(2,1)}, bf16[18,128,128]{2,1,0:T(8,128)(2,1)S(1)}, u32[]{:S(2)}, u32[]{:S(2)}) collective-permute-start(bf16[18,128,128]{2,1,0:T(8,128)(2,1)} %admit.3.refs_1_), channel_id=1, source_target_pairs={{0,7},{1,6},{2,5},{3,4},{4,3},{5,2},{6,1},{7,0},{8,15},{9,14},{10,... | collective-permute-start | bytes 1769480 | tf_op jit(solution)/shard_map/ppermute | solution.py:436
  134.1 17.3 %collective-permute-start.16 = (bf16[18,128,128]{2,1,0:T(8,128)(2,1)}, bf16[18,128,128]{2,1,0:T(8,128)(2,1)S(1)}, u32[]{:S(2)}, u32[]{:S(2)}) collective-permute-start(bf16[18,128,128]{2,1,0:T(8,128)(2,1)} %admit.3.refs_1_), channel_id=1, source_target_pairs={{0,1},{1,0},{2,3},{3,2},{4,5},{5,4},{6,7},{7,6},{8,9},{9,8},{10,11... | collective-permute-start | bytes 1769480 | tf_op jit(solution)/shard_map/ppermute | solution.py:436
  134.2 25.6 %collective-permute-start.19 = (bf16[18,128,128]{2,1,0:T(8,128)(2,1)}, bf16[18,128,128]{2,1,0:T(8,128)(2,1)S(1)}, u32[]{:S(2)}, u32[]{:S(2)}) collective-permute-start(bf16[18,128,128]{2,1,0:T(8,128)(2,1)} %admit.3.refs_1_), channel_id=1, source_target_pairs={{0,3},{1,2},{2,1},{3,0},{4,7},{5,6},{6,5},{7,4},{8,11},{9,10},{10,... | collective-permute-start | bytes 1769480 | tf_op jit(solution)/shard_map/ppermute | solution.py:436
  134.3 28.2 %collective-permute-start = (bf16[18,128,128]{2,1,0:T(8,128)(2,1)S(1)}, bf16[18,128,128]{2,1,0:T(8,128)(2,1)S(1)}, u32[]{:S(2)}, u32[]{:S(2)}) collective-permute-start(bf16[18,128,128]{2,1,0:T(8,128)(2,1)S(1)} %copy-done.2), channel_id=1, source_target_pairs={{0,7},{1,6},{2,5},{3,4},{4,3},{5,2},{6,1},{7,0},{8,15},{9,14},{10,... | collective-permute-start | bytes 1769480 | tf_op jit(solution)/shard_map/ppermute | solution.py:436
  151.5 11.1 %collective-permute-start.15 = (bf16[18,128,128]{2,1,0:T(8,128)(2,1)S(1)}, bf16[18,128,128]{2,1,0:T(8,128)(2,1)S(1)}, u32[]{:S(2)}, u32[]{:S(2)}) collective-permute-start(bf16[18,128,128]{2,1,0:T(8,128)(2,1)S(1)} %copy-done.2), channel_id=1, source_target_pairs={{0,1},{1,0},{2,3},{3,2},{4,5},{5,4},{6,7},{7,6},{8,9},{9,8},{10,11... | collective-permute-start | bytes 1769480 | tf_op jit(solution)/shard_map/ppermute | solution.py:436
  151.5 21.0 %collective-permute-start.18 = (bf16[18,128,128]{2,1,0:T(8,128)(2,1)S(1)}, bf16[18,128,128]{2,1,0:T(8,128)(2,1)S(1)}, u32[]{:S(2)}, u32[]{:S(2)}) collective-permute-start(bf16[18,128,128]{2,1,0:T(8,128)(2,1)S(1)} %copy-done.2), channel_id=1, source_target_pairs={{0,3},{1,2},{2,1},{3,0},{4,7},{5,6},{6,5},{7,4},{8,11},{9,10},{10,... | collective-permute-start | bytes 1769480 | tf_op jit(solution)/shard_map/ppermute | solution.py:436
  159.9 25.3 %collective-permute-start.4 = (bf16[18,128,128]{2,1,0:T(8,128)(2,1)S(1)}, bf16[18,128,128]{2,1,0:T(8,128)(2,1)S(1)}, u32[]{:S(2)}, u32[]{:S(2)}) collective-permute-start(bf16[18,128,128]{2,1,0:T(8,128)(2,1)S(1)} %collective-permute-done.3.refs_16_), channel_id=1, source_target_pairs={{0,3},{1,2},{2,1},{3,0},{4,7},{5,6},{6,5},{7,4},{8,11},{9,10},{10,... | collective-permute-start | bytes 1769480 | tf_op jit(solution)/shard_map/ppermute | solution.py:436
  161.3 23.9 %collective-permute-start.7 = (bf16[24,128,128]{2,1,0:T(8,128)(2,1)S(1)}, bf16[24,128,128]{2,1,0:T(8,128)(2,1)S(1)}, u32[]{:S(2)}, u32[]{:S(2)}) collective-permute-start(bf16[24,128,128]{2,1,0:T(8,128)(2,1)S(1)} %collective-permute-done.6.refs_8_), channel_id=1, source_target_pairs={{0,7},{1,6},{2,5},{3,4},{4,3},{5,2},{6,1},{7,0},{8,15},{9,14},{10,... | collective-permute-start | bytes 2359304 | tf_op jit(solution)/shard_map/ppermute | solution.py:436
  162.6 35.2 %collective-permute-start.17 = (bf16[24,128,128]{2,1,0:T(8,128)(2,1)S(1)}, bf16[24,128,128]{2,1,0:T(8,128)(2,1)S(1)}, u32[]{:S(2)}, u32[]{:S(2)}) collective-permute-start(bf16[24,128,128]{2,1,0:T(8,128)(2,1)S(1)} %copy-done.1), channel_id=1, source_target_pairs={{0,1},{1,0},{2,3},{3,2},{4,5},{5,4},{6,7},{7,6},{8,9},{9,8},{10,11... | collective-permute-start | bytes 2359304 | tf_op jit(solution)/shard_map/ppermute | solution.py:436
  162.6 34.0 %collective-permute-start.1 = (bf16[18,128,128]{2,1,0:T(8,128)(2,1)S(1)}, bf16[18,128,128]{2,1,0:T(8,128)(2,1)S(1)}, u32[]{:S(2)}, u32[]{:S(2)}) collective-permute-start(bf16[18,128,128]{2,1,0:T(8,128)(2,1)S(1)} %collective-permute-done.refs_15_), channel_id=1, source_target_pairs={{0,3},{1,2},{2,1},{3,0},{4,7},{5,6},{6,5},{7,4},{8,11},{9,10},{10,... | collective-permute-start | bytes 1769480 | tf_op jit(solution)/shard_map/ppermute | solution.py:436
  172.5 24.0 %collective-permute-start.23 = (bf16[18,128,128]{2,1,0:T(8,128)(2,1)S(1)}, bf16[18,128,128]{2,1,0:T(8,128)(2,1)S(1)}, u32[]{:S(2)}, u32[]{:S(2)}) collective-permute-start(bf16[18,128,128]{2,1,0:T(8,128)(2,1)S(1)} %copy-done.6), channel_id=1, source_target_pairs={{0,7},{1,6},{2,5},{3,4},{4,3},{5,2},{6,1},{7,0},{8,15},{9,14},{10,... | collective-permute-start | bytes 1769480 | tf_op jit(solution)/shard_map/ppermute | solution.py:436
  185.2 12.8 %collective-permute-start.21 = (bf16[18,128,128]{2,1,0:T(8,128)(2,1)S(1)}, bf16[18,128,128]{2,1,0:T(8,128)(2,1)S(1)}, u32[]{:S(2)}, u32[]{:S(2)}) collective-permute-start(bf16[18,128,128]{2,1,0:T(8,128)(2,1)S(1)} %collective-permute-done.4.refs_10_), channel_id=1, source_target_pairs={{0,1},{1,0},{2,3},{3,2},{4,5},{5,4},{6,7},{7,6},{8,9},{9,8},{10,11... | collective-permute-start | bytes 1769480 | tf_op jit(solution)/shard_map/ppermute | solution.py:436
  185.2 12.6 %collective-permute-start.13 = (bf16[9,128,128]{2,1,0:T(8,128)(2,1)S(1)}, bf16[9,128,128]{2,1,0:T(8,128)(2,1)S(1)}, u32[]{:S(2)}, u32[]{:S(2)}) collective-permute-start(bf16[9,128,128]{2,1,0:T(8,128)(2,1)S(1)} %get-tuple-element.50), channel_id=1, source_target_pairs={{0,8},{1,9},{2,10},{3,11},{4,124},{5,125},{6,126},{7,127},{8,16},{... | collective-permute-start | bytes 884744 | tf_op jit(solution)/shard_map/ppermute | solution.py:436
  196.5 2.2 collective-permute-start.20
  196.5 17.7 %collective-permute-start.5 = (bf16[18,128,128]{2,1,0:T(8,128)(2,1)S(1)}, bf16[18,128,128]{2,1,0:T(8,128)(2,1)S(1)}, u32[]{:S(2)}, u32[]{:S(2)}) collective-permute-start(bf16[18,128,128]{2,1,0:T(8,128)(2,1)S(1)} %collective-permute-done.4.refs_10_), channel_id=1, source_target_pairs={{0,8},{1,9},{2,10},{3,11},{4,124},{5,125},{6,126},{7,127},{8,16},{... | collective-permute-start | bytes 1769480 | tf_op jit(solution)/shard_map/ppermute | solution.py:436
  197.8 29.1 %collective-permute-start.2 = (bf16[18,128,128]{2,1,0:T(8,128)(2,1)S(1)}, bf16[18,128,128]{2,1,0:T(8,128)(2,1)S(1)}, u32[]{:S(2)}, u32[]{:S(2)}) collective-permute-start(bf16[18,128,128]{2,1,0:T(8,128)(2,1)S(1)} %collective-permute-done.1.refs_9_), channel_id=1, source_target_pairs={{0,8},{1,9},{2,10},{3,11},{4,124},{5,125},{6,126},{7,127},{8,16},{... | collective-permute-start | bytes 1769480 | tf_op jit(solution)/shard_map/ppermute | solution.py:436
  197.9 41.7 %collective-permute-start.8 = (bf16[18,128,128]{2,1,0:T(8,128)(2,1)S(1)}, bf16[18,128,128]{2,1,0:T(8,128)(2,1)S(1)}, u32[]{:S(2)}, u32[]{:S(2)}) collective-permute-start(bf16[18,128,128]{2,1,0:T(8,128)(2,1)S(1)} %slice.28), channel_id=1, source_target_pairs={{0,8},{1,9},{2,10},{3,11},{4,124},{5,125},{6,126},{7,127},{8,16},{... | collective-permute-start | bytes 1769480 | tf_op jit(solution)/shard_map/ppermute | solution.py:436
  197.9 43.9 %collective-permute-start.22 = (bf16[24,128,128]{2,1,0:T(8,128)(2,1)S(1)}, bf16[24,128,128]{2,1,0:T(8,128)(2,1)S(1)}, u32[]{:S(2)}, u32[]{:S(2)}) collective-permute-start(bf16[24,128,128]{2,1,0:T(8,128)(2,1)S(1)} %collective-permute-done.7.refs_11_), channel_id=1, source_target_pairs={{0,1},{1,0},{2,3},{3,2},{4,5},{5,4},{6,7},{7,6},{8,9},{9,8},{10,11... | collective-permute-start | bytes 2359304 | tf_op jit(solution)/shard_map/ppermute | solution.py:436
  198.7 59.7 %collective-permute-start.12 = (bf16[18,128,128]{2,1,0:T(8,128)(2,1)S(1)}, bf16[18,128,128]{2,1,0:T(8,128)(2,1)S(1)}, u32[]{:S(2)}, u32[]{:S(2)}) collective-permute-start(bf16[18,128,128]{2,1,0:T(8,128)(2,1)S(1)} %collective-permute-done.refs_15_), channel_id=1, source_target_pairs={{0,8},{1,9},{2,10},{3,11},{4,124},{5,125},{6,126},{7,127},{8,16},{... | collective-permute-start | bytes 1769480 | tf_op jit(solution)/shard_map/ppermute | solution.py:436
  214.2 44.2 %collective-permute-start.10 = (bf16[18,128,128]{2,1,0:T(8,128)(2,1)S(1)}, bf16[18,128,128]{2,1,0:T(8,128)(2,1)S(1)}, u32[]{:S(2)}, u32[]{:S(2)}) collective-permute-start(bf16[18,128,128]{2,1,0:T(8,128)(2,1)S(1)} %collective-permute-done.5.refs_1_), channel_id=1, source_target_pairs={{0,1},{1,0},{2,3},{3,2},{4,5},{5,4},{6,7},{7,6},{8,9},{9,8},{10,11... | collective-permute-start | bytes 1769480 | tf_op jit(solution)/shard_map/ppermute | solution.py:436
  226.9 31.6 %collective-permute-start.9 = (bf16[18,128,128]{2,1,0:T(8,128)(2,1)S(1)}, bf16[18,128,128]{2,1,0:T(8,128)(2,1)S(1)}, u32[]{:S(2)}, u32[]{:S(2)}) collective-permute-start(bf16[18,128,128]{2,1,0:T(8,128)(2,1)S(1)} %collective-permute-done.2.refs_0_), channel_id=1, source_target_pairs={{0,1},{1,0},{2,3},{3,2},{4,5},{5,4},{6,7},{7,6},{8,9},{9,8},{10,11... | collective-permute-start | bytes 1769480 | tf_op jit(solution)/shard_map/ppermute | solution.py:436
  239.5 19.0 %collective-permute-start.11 = (bf16[18,128,128]{2,1,0:T(8,128)(2,1)S(1)}, bf16[18,128,128]{2,1,0:T(8,128)(2,1)S(1)}, u32[]{:S(2)}, u32[]{:S(2)}) collective-permute-start(bf16[18,128,128]{2,1,0:T(8,128)(2,1)S(1)} %collective-permute-done.8.refs_2_), channel_id=1, source_target_pairs={{0,1},{1,0},{2,3},{3,2},{4,5},{5,4},{6,7},{7,6},{8,9},{9,8},{10,11... | collective-permute-start | bytes 1769480 | tf_op jit(solution)/shard_map/ppermute | solution.py:436
  241.9 16.6 %collective-permute-start.14 = (bf16[9,128,128]{2,1,0:T(8,128)(2,1)S(1)}, bf16[9,128,128]{2,1,0:T(8,128)(2,1)S(1)}, u32[]{:S(2)}, u32[]{:S(2)}) collective-permute-start(bf16[9,128,128]{2,1,0:T(8,128)(2,1)S(1)} %get-tuple-element.49), channel_id=1, source_target_pairs={{0,8},{1,9},{2,10},{3,11},{4,124},{5,125},{6,126},{7,127},{8,16},{... | collective-permute-start | bytes 884744 | tf_op jit(solution)/shard_map/ppermute | solution.py:436

commit v6 on v4

--- a/solution.py
+++ b/solution.py
@@ -124,12 +124,11 @@
 
 
 def load_pieces(pieces, piece_starts, table, sems):
-    copies = []
-    for i, (piece, start) in enumerate(zip(pieces, piece_starts)):
-        copies.append(
-            pltpu.make_async_copy(piece, table.at[pl.ds(start, piece.shape[0])], sems.at[i])
-        )
-        copies[-1].start()
+    copies = {}
+    for i, (piece, (part, start)) in enumerate(zip(pieces, piece_starts)):
+        copy = pltpu.make_async_copy(piece, table.at[pl.ds(start, piece.shape[0])], sems.at[i])
+        copy.start()
+        copies.setdefault(part, []).append(copy)
     return copies
 
 
@@ -145,25 +144,30 @@
     group = row_count * width
     copies = load_pieces(pieces, piece_starts, table, sems)
     table[table_size] = jnp.zeros((width, width), table.dtype)
-    for copy in copies:
-        copy.wait()
 
     def block(m, k):
         return table[jnp.minimum(pos_ref[m * near + k], table_size)]
 
-    for r in range(row_count):
-        for k in range(near):
-            left[r * width:(r + 1) * width, k * width:(k + 1) * width] = block(r, k)
-    left_far[...] = left[:, NEAR_PARTS * group:]
-    for part in range(9):
-        parts = [q for q in reach(part) if q < NEAR_PARTS]
-        for i, q in enumerate(parts):
+    for q in range(NEAR_PARTS):
+        for copy in copies[q]:
+            copy.wait()
+        if q == 0:
+            for r in range(row_count):
+                for k in range(near):
+                    left[r * width:(r + 1) * width, k * width:(k + 1) * width] = block(r, k)
+            left_far[...] = left[:, NEAR_PARTS * group:]
+        for part in range(9):
+            if q not in reach(part):
+                continue
+            i = reach(part).index(q)
             for r in range(row_count):
                 for k in range(row_count):
                     low = (i * row_count + r) * width
                     grids[part][low:low + width, k * width:(k + 1) * width] = block(
                         q * row_count + r, part * row_count + k
                     )
+    for part in range(9):
+        parts = [q for q in reach(part) if q < NEAR_PARTS]
         square[part] = jnp.dot(
             lanes_of(left, parts, group), grids[part][...], preferred_element_type=jnp.float32
         )
@@ -203,20 +207,25 @@
     zero_at = table_start + table_size
     copies = load_pieces(pieces, piece_starts, table, sems)
     table[table_size] = jnp.zeros((width, width), table.dtype)
-    for copy in copies:
-        copy.wait()
-
-    for part in range(9):
-        parts = reach(part)
-        base = near_count(part)
-        far_base = sum(far_count(q) for q in range(part)) * group
-        for i, q in enumerate(parts[base:]):
+    for q in (8, 6, 7):
+        for copy in copies[q]:
+            copy.wait()
+        for part in range(9):
+            if q not in reach(part):
+                continue
+            i = reach(part).index(q) - near_count(part)
+            far_base = sum(far_count(p) for p in range(part)) * group
             for r in range(row_count):
                 for k in range(row_count):
                     low = far_base + (i * row_count + r) * width
                     grid[low:low + width, k * width:(k + 1) * width] = table[
                         pos_ref[(q * row_count + r) * near + part * row_count + k] - table_start
                     ]
+
+    for part in range(9):
+        parts = reach(part)
+        base = near_count(part)
+        far_base = sum(far_count(q) for q in range(part)) * group
         product = square_in[part]
         if base < len(parts):
             product = product + jnp.dot(
@@ -425,7 +434,7 @@
     far_across_1 = send(ring_across_1, onward)
     ring_same_1 = send(ring_across_1, across)
     own_chip_1 = send(own_1, chip)
-    far_across_2 = send(ring_across_2, onward)
+    far_across_2 = send(ring_across_2[:cut // 2], onward)
     ring_same_2 = send(ring_across_2, across)
     ring_same_3 = send(own_across_3, ring)
     ring_across_t = send(own_t, ring)
@@ -438,6 +447,7 @@
     ring_chip_3 = send(ring_same_3, chip)
     far_same_2 = send(ring_same_2, onward)
     ring_chip_2 = send(ring_same_2, chip)
+    far_across_3 = send(far_same_2[cut // 2:], across)
     far_chip_1 = send(far_same_1, chip)
     far_chip_3 = send(far_same_3, chip)
     far_chip_2 = send(far_same_2, chip)
@@ -451,19 +461,19 @@
         (ring_across_1, 5, 0), (ring_across_2, 5, cut), (ring_across_t, 5, tail),
     ]
     far_pieces = [
+        (far_across_1, 8, 0), (far_across_2, 8, cut), (far_across_3, 8, cut + cut // 2),
         (far_same_1, 6, 0), (far_same_2, 6, cut), (far_same_3, 6, 2 * cut),
         (far_chip_1, 7, 0), (far_chip_2, 7, cut), (far_chip_3, 7, 2 * cut),
-        (far_across_1, 8, 0), (far_across_2, 8, cut),
     ]
     far_start = starts[NEAR_PARTS]
     carried = square_near(
         positions, [piece for piece, _, _ in near_pieces],
-        [starts[part] + offset for _, part, offset in near_pieces],
+        [(part, starts[part] + offset) for _, part, offset in near_pieces],
         far_start, row_count, width,
     )
     purified = purify_far(
         positions, out_slots, [piece for piece, _, _ in far_pieces],
-        [starts[part] + offset - far_start for _, part, offset in far_pieces],
+        [(part, starts[part] + offset - far_start) for _, part, offset in far_pieces],
         carried, far_start, zero_at - far_start, row_count, slot_count, width,
     )
     return purified.reshape(density.shape)

time: 279 us -> 269 us (0.964)
  waiting for transfers between devices: 192 us -> 182 us
    ppermute x23 -> x24, waiting for transfers between devices: 98.3 us -> 88.1 us  [send(): return lax.ppermute(array, axes, pairs)]
    ppermute x23 -> x24, starting transfers between devices: 28 us -> 27.9 us  [send(): return lax.ppermute(array, axes, pairs)]
  transfers between devices with their start and end apart: 24 -> 25, of which waited for: 10 -> 10; matrix products, arithmetic and copies ran while one was open for 2% -> 2% of each run, Pallas kernels for 6% -> 6%
where the time goes in v6:
time: 269 us; the launch traced here: 268 us
  waiting for transfers between devices  182 us (68%)
  Pallas kernels  40.6 us (15%)
  starting transfers between devices  39.9 us (15%)
  other arithmetic  3.34 us (1%)
    all_to_all x1, waiting for transfers between devices, per_device(): lax.all_to_all(outgoing.reshape(device_count, C, width, width), ('gx', 'g...  93.6 us
    ppermute x24, waiting for transfers between devices, send(): return lax.ppermute(array, axes, pairs)  88.1 us
    ppermute x24, starting transfers between devices, send(): return lax.ppermute(array, axes, pairs)  27.9 us
    pallas_call x1, Pallas kernels, purify_far(): pl.pallas_call(functools.partial(far_kernel, row_count, width, piece_star...  13.5 us
    pallas_call x2, Pallas kernels, admit(): pl.pallas_call(functools.partial(admit_kernel, spans), out_shape=[jax.Sha...  12.1 us
    all_to_all x1, starting transfers between devices, per_device(): lax.all_to_all(outgoing.reshape(device_count, C, width, width), ('gx', 'g...  12 us
    pallas_call x1, Pallas kernels, square_near(): pl.pallas_call(functools.partial(near_kernel, row_count, width, piece_sta...  10.7 us
  transfers between devices with their start and end apart: 25, of which 10 were waited for; matrix products, arithmetic and copies ran while one was open for 2% of the time, Pallas kernels for 6%

profile of v6, /device:TPU:1, one launch (start us, length us, event | category | flops | bytes accessed | tf_op | source)
XLA Modules:
  0.0 268.5 jit_solution(6018463874563790090)
XLA Ops:
  0.0 4.4 %pack.1 = bf16[256,128,128]{2,1,0:T(8,128)(2,1)} custom-call(s32[1]{0:T(128)} %bitcast.base_ref, s32[12288]{0:T(1024)} %owner_ref.1, bf16[96,128,128]{2,1,0:T(8,128)(2,1)} %ent_ref.1), custom_call_target="tpu_custom_call" | custom-call | tf_op jit(solution)/shard_map/pack/pallas_call | solution.py:43
  4.4 12.0 %all-to-all-start = ((bf16[128,2,128,128]{3,2,1,0:T(8,128)(2,1)}), bf16[128,2,128,128]{3,2,1,0:T(8,128)(2,1)}, u32[]{:S(2)}, u32[]{:S(2)}) async-start(bf16[128,2,128,128]{3,2,1,0:T(8,128)(2,1)} %bitcast.9), calls=%async_computation | async-start | bytes 16777216 | tf_op jit(solution)/shard_map/all_to_all | solution.py:365
  16.8 0.6 gather_fusion
  18.3 0.3 select_reduce_fusion
  19.9 0.7 select_reduce_fusion.4.source_ref
  20.6 0.6 convert_reduce_fusion.2.first_ref
  21.4 0.7 select_reduce_fusion.1.order_ref
  22.1 93.6 %all-to-all-done = bf16[128,2,128,128]{3,2,1,0:T(8,128)(2,1)} async-done(((bf16[128,2,128,128]{3,2,1,0:T(8,128)(2,1)}), bf16[128,2,128,128]{3,2,1,0:T(8,128)(2,1)}, u32[]{:S(2)}, u32[]{:S(2)}) %all-to-all-start) | async-done | bytes 8388640 | tf_op jit(solution)/shard_map/all_to_all | solution.py:365
  115.8 6.7 %admit.2 = (bf16[18,128,128]{2,1,0:T(8,128)(2,1)}, bf16[24,128,128]{2,1,0:T(8,128)(2,1)}, bf16[18,128,128]{2,1,0:T(8,128)(2,1)}) custom-call(s32[61]{0:T(128)} %convert_reduce_fusion.2.first_ref, s32[256]{0:T(256)} %select_reduce_fusion.1.order_ref, s32[60]{0:T(128)} %select_reduce_fusion.4.source_ref, bf16[60,128,128]{2,1,0:T(8,128)(2,1)} %bitcast.10, ...), custom_call_target="tpu_custom_call" | custom-call | tf_op jit(solution)/shard_map/admit/pallas_call | solution.py:91
  122.5 6.2 %collective-permute-start.9 = (bf16[24,128,128]{2,1,0:T(8,128)(2,1)}, bf16[24,128,128]{2,1,0:T(8,128)(2,1)S(1)}, u32[]{:S(2)}, u32[]{:S(2)}) collective-permute-start(bf16[24,128,128]{2,1,0:T(8,128)(2,1)} %get-tuple-element.32.refs_2_), channel_id=1, source_target_pairs={{0,3},{1,2},{2,1},{3,0},{4,7},{5,6},{6,5},{7,4},{8,11},{9,10},{10,... | collective-permute-start | bytes 2359304 | tf_op jit(solution)/shard_map/ppermute | solution.py:416
  128.7 5.4 %admit.3.refs_1_ = bf16[18,128,128]{2,1,0:T(8,128)(2,1)} custom-call(s32[61]{0:T(128)} %convert_reduce_fusion.2.first_ref, s32[256]{0:T(256)} %select_reduce_fusion.1.order_ref, s32[60]{0:T(128)} %select_reduce_fusion.4.source_ref, bf16[60,128,128]{2,1,0:T(8,128)(2,1)} %bitcast.11, bf16[256,128,128]{2,1,0:T(8,128)(2,1)} %bitcast.2.received_ref), custom_call_target="tpu_custom_call" | custom-call | tf_op jit(solution)/shard_map/admit/pallas_call | solution.py:91
  134.4 2.8 %collective-permute-start = (bf16[18,128,128]{2,1,0:T(8,128)(2,1)S(1)}, bf16[18,128,128]{2,1,0:T(8,128)(2,1)S(1)}, u32[]{:S(2)}, u32[]{:S(2)}) collective-permute-start(bf16[18,128,128]{2,1,0:T(8,128)(2,1)S(1)} %copy-done.2), channel_id=1, source_target_pairs={{0,7},{1,6},{2,5},{3,4},{4,3},{5,2},{6,1},{7,0},{8,15},{9,14},{10,... | collective-permute-start | bytes 1769480 | tf_op jit(solution)/shard_map/ppermute | solution.py:416
  137.2 14.3 %collective-permute-done.2.refs_16_ = bf16[18,128,128]{2,1,0:T(8,128)(2,1)S(1)} collective-permute-done((bf16[18,128,128]{2,1,0:T(8,128)(2,1)}, bf16[18,128,128]{2,1,0:T(8,128)(2,1)S(1)}, u32[]{:S(2)}, u32[]{:S(2)}) %collective-permute-start.2) | collective-permute-done | bytes 589856 | tf_op jit(solution)/shard_map/ppermute | solution.py:416
  151.5 8.4 %collective-permute-done.19.refs_7_ = bf16[18,128,128]{2,1,0:T(8,128)(2,1)S(1)} collective-permute-done((bf16[18,128,128]{2,1,0:T(8,128)(2,1)}, bf16[18,128,128]{2,1,0:T(8,128)(2,1)S(1)}, u32[]{:S(2)}, u32[]{:S(2)}) %collective-permute-start.19) | collective-permute-done | bytes 589856 | tf_op jit(solution)/shard_map/ppermute | solution.py:416
  159.9 1.4 collective-permute-start.4
  161.4 1.2 collective-permute-done.refs_15_
  162.7 9.8 %collective-permute-done.18.refs_6_ = bf16[18,128,128]{2,1,0:T(8,128)(2,1)S(1)} collective-permute-done((bf16[18,128,128]{2,1,0:T(8,128)(2,1)S(1)}, bf16[18,128,128]{2,1,0:T(8,128)(2,1)S(1)}, u32[]{:S(2)}, u32[]{:S(2)}) %collective-permute-start.18) | collective-permute-done | bytes 589856 | tf_op jit(solution)/shard_map/ppermute | solution.py:416
  172.6 12.6 %collective-permute-done.4.refs_10_ = bf16[18,128,128]{2,1,0:T(8,128)(2,1)S(1)} collective-permute-done((bf16[18,128,128]{2,1,0:T(8,128)(2,1)S(1)}, bf16[18,128,128]{2,1,0:T(8,128)(2,1)S(1)}, u32[]{:S(2)}, u32[]{:S(2)}) %collective-permute-start.4) | collective-permute-done | bytes 589856 | tf_op jit(solution)/shard_map/ppermute | solution.py:416
  185.3 1.5 collective-permute-start.3
  186.8 9.8 %collective-permute-done.7.refs_9_ = bf16[18,128,128]{2,1,0:T(8,128)(2,1)S(1)} collective-permute-done((bf16[18,128,128]{2,1,0:T(8,128)(2,1)S(1)}, bf16[18,128,128]{2,1,0:T(8,128)(2,1)S(1)}, u32[]{:S(2)}, u32[]{:S(2)}) %collective-permute-start.7) | collective-permute-done | bytes 589856 | tf_op jit(solution)/shard_map/ppermute | solution.py:416
  196.6 1.2 collective-permute-start.5
  198.0 0.8 collective-permute-start.22
  198.8 4.3 %collective-permute-start.1 = (bf16[18,128,128]{2,1,0:T(8,128)(2,1)S(1)}, bf16[18,128,128]{2,1,0:T(8,128)(2,1)S(1)}, u32[]{:S(2)}, u32[]{:S(2)}) collective-permute-start(bf16[18,128,128]{2,1,0:T(8,128)(2,1)S(1)} %collective-permute-done.refs_15_), channel_id=1, source_target_pairs={{0,8},{1,9},{2,10},{3,11},{4,124},{5,125},{6,126},{7,127},{8,16},{... | collective-permute-start | bytes 1769480 | tf_op jit(solution)/shard_map/ppermute | solution.py:416
  203.1 11.2 %collective-permute-done.5.refs_4_ = bf16[18,128,128]{2,1,0:T(8,128)(2,1)S(1)} collective-permute-done((bf16[18,128,128]{2,1,0:T(8,128)(2,1)S(1)}, bf16[18,128,128]{2,1,0:T(8,128)(2,1)S(1)}, u32[]{:S(2)}, u32[]{:S(2)}) %collective-permute-start.5) | collective-permute-done | bytes 589856 | tf_op jit(solution)/shard_map/ppermute | solution.py:416
  214.3 2.3 collective-permute-start.13
  216.6 10.3 %collective-permute-done.8.refs_3_ = bf16[18,128,128]{2,1,0:T(8,128)(2,1)S(1)} collective-permute-done((bf16[18,128,128]{2,1,0:T(8,128)(2,1)S(1)}, bf16[18,128,128]{2,1,0:T(8,128)(2,1)S(1)}, u32[]{:S(2)}, u32[]{:S(2)}) %collective-permute-start.8) | collective-permute-done | bytes 589856 | tf_op jit(solution)/shard_map/ppermute | solution.py:416
  226.9 2.3 collective-permute-start.12
  229.3 10.3 %collective-permute-done.11.refs_5_ = bf16[18,128,128]{2,1,0:T(8,128)(2,1)S(1)} collective-permute-done((bf16[18,128,128]{2,1,0:T(8,128)(2,1)S(1)}, bf16[18,128,128]{2,1,0:T(8,128)(2,1)S(1)}, u32[]{:S(2)}, u32[]{:S(2)}) %collective-permute-start.11) | collective-permute-done | bytes 589856 | tf_op jit(solution)/shard_map/ppermute | solution.py:416
  239.6 2.3 collective-permute-start.14
  241.9 2.1 collective-permute-start.6
  244.0 10.7 %square_near.1 = (bf16[2304,384]{1,0:T(8,128)(2,1)S(1)}, bf16[1536,384]{1,0:T(8,128)(2,1)S(1)}, bf16[1536,384]{1,0:T(8,128)(2,1)S(1)}, bf16[2304,384]{1,0:T(8,12...) custom-call(s32[729]{0:T(1024)S(1)} %reshape.495.pos_ref, ...), custom_call_target="tpu_custom_call" | custom-call | tf_op jit(solution)/shard_map/square_near/pallas_call | solution.py:179
  254.7 13.5 %purify_far.1 = f32[60,128,128]{2,1,0:T(8,128)} custom-call(s32[729]{0:T(1024)S(1)} %reshape.495.pos_ref, s32[81]{0:T(128)S(1)} %reshape.496.slot_ref, bf16[18,128,128]{2,1,0:T(8,128)(2,1)S(1)} %collective-permute-done.1.refs_0_, bf16[9,128,128]{2,1,0:T(8,128)(2,1)S(1)} %collective-permute-done.3.refs_1_, ...), custom_call_target="tpu_custom_call" | custom-call | tf_op jit(solution)/shard_map/purify_far/pallas_call | solution.py:280
  (83 shorter events, 3.4 us)
Async XLA Ops:
  4.4 12.1 %copy-start.4 = (s32[32,4,3,20]{0,1,3,2:T(4,128)S(1)}, s32[32,4,3,20]{0,1,3,2:T(4,128)}, u32[]{:S(2)}) copy-start(s32[32,4,3,20]{0,1,3,2:T(4,128)} %param.6) | copy-start | bytes 92164
  4.4 14.5 %copy-start.3 = (s32[12288]{0:T(1024)S(1)}, s32[12288]{0:T(1024)}, u32[]{:S(2)}) copy-start(s32[12288]{0:T(1024)} %owner_ref.1) | copy-start | bytes 147460
  4.4 111.4 %all-to-all-start = ((bf16[128,2,128,128]{3,2,1,0:T(8,128)(2,1)}), bf16[128,2,128,128]{3,2,1,0:T(8,128)(2,1)}, u32[]{:S(2)}, u32[]{:S(2)}) async-start(bf16[128,2,128,128]{3,2,1,0:T(8,128)(2,1)} %bitcast.9), calls=%async_computation | async-start | bytes 16777216 | tf_op jit(solution)/shard_map/all_to_all | solution.py:365
  16.4 3.0 %copy-start.5 = (s32[12288]{0:T(1024)S(1)}, s32[12288]{0:T(1024)}, u32[]{:S(2)}) copy-start(s32[12288]{0:T(1024)} %param.9) | copy-start | bytes 147460
  122.4 12.0 %copy-start.2 = (bf16[18,128,128]{2,1,0:T(8,128)(2,1)S(1)}, bf16[18,128,128]{2,1,0:T(8,128)(2,1)}, u32[]{:S(2)}) copy-start(bf16[18,128,128]{2,1,0:T(8,128)(2,1)} %get-tuple-element.31.refs_0_) | copy-start | bytes 1769476
  122.4 40.2 %copy-start.1 = (bf16[24,128,128]{2,1,0:T(8,128)(2,1)S(1)}, bf16[24,128,128]{2,1,0:T(8,128)(2,1)}, u32[]{:S(2)}) copy-start(bf16[24,128,128]{2,1,0:T(8,128)(2,1)} %get-tuple-element.32.refs_2_) | copy-start | bytes 2359300
  122.4 50.1 %copy-start.6 = (bf16[18,128,128]{2,1,0:T(8,128)(2,1)S(1)}, bf16[18,128,128]{2,1,0:T(8,128)(2,1)}, u32[]{:S(2)}) copy-start(bf16[18,128,128]{2,1,0:T(8,128)(2,1)} %get-tuple-element.33) | copy-start | bytes 1769476
  122.5 38.9 %collective-permute-start.9 = (bf16[24,128,128]{2,1,0:T(8,128)(2,1)}, bf16[24,128,128]{2,1,0:T(8,128)(2,1)S(1)}, u32[]{:S(2)}, u32[]{:S(2)}) collective-permute-start(bf16[24,128,128]{2,1,0:T(8,128)(2,1)} %get-tuple-element.32.refs_2_), channel_id=1, source_target_pairs={{0,3},{1,2},{2,1},{3,0},{4,7},{5,6},{6,5},{7,4},{8,11},{9,10},{10,... | collective-permute-start | bytes 2359304 | tf_op jit(solution)/shard_map/ppermute | solution.py:416
  134.1 109.9 %copy-start = (bf16[18,128,128]{2,1,0:T(8,128)(2,1)S(1)}, bf16[18,128,128]{2,1,0:T(8,128)(2,1)}, u32[]{:S(2)}) copy-start(bf16[18,128,128]{2,1,0:T(8,128)(2,1)} %admit.3.refs_1_) | copy-start | bytes 1769476
  134.1 17.4 %collective-permute-start.2 = (bf16[18,128,128]{2,1,0:T(8,128)(2,1)}, bf16[18,128,128]{2,1,0:T(8,128)(2,1)S(1)}, u32[]{:S(2)}, u32[]{:S(2)}) collective-permute-start(bf16[18,128,128]{2,1,0:T(8,128)(2,1)} %admit.3.refs_1_), channel_id=1, source_target_pairs={{0,7},{1,6},{2,5},{3,4},{4,3},{5,2},{6,1},{7,0},{8,15},{9,14},{10,... | collective-permute-start | bytes 1769480 | tf_op jit(solution)/shard_map/ppermute | solution.py:416
  134.2 17.3 %collective-permute-start.16 = (bf16[18,128,128]{2,1,0:T(8,128)(2,1)}, bf16[18,128,128]{2,1,0:T(8,128)(2,1)S(1)}, u32[]{:S(2)}, u32[]{:S(2)}) collective-permute-start(bf16[18,128,128]{2,1,0:T(8,128)(2,1)} %admit.3.refs_1_), channel_id=1, source_target_pairs={{0,1},{1,0},{2,3},{3,2},{4,5},{5,4},{6,7},{7,6},{8,9},{9,8},{10,11... | collective-permute-start | bytes 1769480 | tf_op jit(solution)/shard_map/ppermute | solution.py:416
  134.3 25.6 %collective-permute-start.19 = (bf16[18,128,128]{2,1,0:T(8,128)(2,1)}, bf16[18,128,128]{2,1,0:T(8,128)(2,1)S(1)}, u32[]{:S(2)}, u32[]{:S(2)}) collective-permute-start(bf16[18,128,128]{2,1,0:T(8,128)(2,1)} %admit.3.refs_1_), channel_id=1, source_target_pairs={{0,3},{1,2},{2,1},{3,0},{4,7},{5,6},{6,5},{7,4},{8,11},{9,10},{10,... | collective-permute-start | bytes 1769480 | tf_op jit(solution)/shard_map/ppermute | solution.py:416
  134.4 28.2 %collective-permute-start = (bf16[18,128,128]{2,1,0:T(8,128)(2,1)S(1)}, bf16[18,128,128]{2,1,0:T(8,128)(2,1)S(1)}, u32[]{:S(2)}, u32[]{:S(2)}) collective-permute-start(bf16[18,128,128]{2,1,0:T(8,128)(2,1)S(1)} %copy-done.2), channel_id=1, source_target_pairs={{0,7},{1,6},{2,5},{3,4},{4,3},{5,2},{6,1},{7,0},{8,15},{9,14},{10,... | collective-permute-start | bytes 1769480 | tf_op jit(solution)/shard_map/ppermute | solution.py:416
  151.5 11.1 %collective-permute-start.15 = (bf16[18,128,128]{2,1,0:T(8,128)(2,1)S(1)}, bf16[18,128,128]{2,1,0:T(8,128)(2,1)S(1)}, u32[]{:S(2)}, u32[]{:S(2)}) collective-permute-start(bf16[18,128,128]{2,1,0:T(8,128)(2,1)S(1)} %copy-done.2), channel_id=1, source_target_pairs={{0,1},{1,0},{2,3},{3,2},{4,5},{5,4},{6,7},{7,6},{8,9},{9,8},{10,11... | collective-permute-start | bytes 1769480 | tf_op jit(solution)/shard_map/ppermute | solution.py:416
  151.5 21.0 %collective-permute-start.18 = (bf16[18,128,128]{2,1,0:T(8,128)(2,1)S(1)}, bf16[18,128,128]{2,1,0:T(8,128)(2,1)S(1)}, u32[]{:S(2)}, u32[]{:S(2)}) collective-permute-start(bf16[18,128,128]{2,1,0:T(8,128)(2,1)S(1)} %copy-done.2), channel_id=1, source_target_pairs={{0,3},{1,2},{2,1},{3,0},{4,7},{5,6},{6,5},{7,4},{8,11},{9,10},{10,... | collective-permute-start | bytes 1769480 | tf_op jit(solution)/shard_map/ppermute | solution.py:416
  159.9 25.3 %collective-permute-start.4 = (bf16[18,128,128]{2,1,0:T(8,128)(2,1)S(1)}, bf16[18,128,128]{2,1,0:T(8,128)(2,1)S(1)}, u32[]{:S(2)}, u32[]{:S(2)}) collective-permute-start(bf16[18,128,128]{2,1,0:T(8,128)(2,1)S(1)} %collective-permute-done.2.refs_16_), channel_id=1, source_target_pairs={{0,3},{1,2},{2,1},{3,0},{4,7},{5,6},{6,5},{7,4},{8,11},{9,10},{10,... | collective-permute-start | bytes 1769480 | tf_op jit(solution)/shard_map/ppermute | solution.py:416
  161.4 23.9 %collective-permute-start.10 = (bf16[24,128,128]{2,1,0:T(8,128)(2,1)S(1)}, bf16[24,128,128]{2,1,0:T(8,128)(2,1)S(1)}, u32[]{:S(2)}, u32[]{:S(2)}) collective-permute-start(bf16[24,128,128]{2,1,0:T(8,128)(2,1)S(1)} %collective-permute-done.9.refs_8_), channel_id=1, source_target_pairs={{0,7},{1,6},{2,5},{3,4},{4,3},{5,2},{6,1},{7,0},{8,15},{9,14},{10,... | collective-permute-start | bytes 2359304 | tf_op jit(solution)/shard_map/ppermute | solution.py:416
  162.6 35.2 %collective-permute-start.17 = (bf16[24,128,128]{2,1,0:T(8,128)(2,1)S(1)}, bf16[24,128,128]{2,1,0:T(8,128)(2,1)S(1)}, u32[]{:S(2)}, u32[]{:S(2)}) collective-permute-start(bf16[24,128,128]{2,1,0:T(8,128)(2,1)S(1)} %copy-done.1), channel_id=1, source_target_pairs={{0,1},{1,0},{2,3},{3,2},{4,5},{5,4},{6,7},{7,6},{8,9},{9,8},{10,11... | collective-permute-start | bytes 2359304 | tf_op jit(solution)/shard_map/ppermute | solution.py:416
  162.6 34.0 %collective-permute-start.7 = (bf16[18,128,128]{2,1,0:T(8,128)(2,1)S(1)}, bf16[18,128,128]{2,1,0:T(8,128)(2,1)S(1)}, u32[]{:S(2)}, u32[]{:S(2)}) collective-permute-start(bf16[18,128,128]{2,1,0:T(8,128)(2,1)S(1)} %collective-permute-done.refs_15_), channel_id=1, source_target_pairs={{0,3},{1,2},{2,1},{3,0},{4,7},{5,6},{6,5},{7,4},{8,11},{9,10},{10,... | collective-permute-start | bytes 1769480 | tf_op jit(solution)/shard_map/ppermute | solution.py:416
  172.6 24.0 %collective-permute-start.23 = (bf16[18,128,128]{2,1,0:T(8,128)(2,1)S(1)}, bf16[18,128,128]{2,1,0:T(8,128)(2,1)S(1)}, u32[]{:S(2)}, u32[]{:S(2)}) collective-permute-start(bf16[18,128,128]{2,1,0:T(8,128)(2,1)S(1)} %copy-done.6), channel_id=1, source_target_pairs={{0,7},{1,6},{2,5},{3,4},{4,3},{5,2},{6,1},{7,0},{8,15},{9,14},{10,... | collective-permute-start | bytes 1769480 | tf_op jit(solution)/shard_map/ppermute | solution.py:416
  185.2 12.8 %collective-permute-start.21 = (bf16[18,128,128]{2,1,0:T(8,128)(2,1)S(1)}, bf16[18,128,128]{2,1,0:T(8,128)(2,1)S(1)}, u32[]{:S(2)}, u32[]{:S(2)}) collective-permute-start(bf16[18,128,128]{2,1,0:T(8,128)(2,1)S(1)} %collective-permute-done.4.refs_10_), channel_id=1, source_target_pairs={{0,1},{1,0},{2,3},{3,2},{4,5},{5,4},{6,7},{7,6},{8,9},{9,8},{10,11... | collective-permute-start | bytes 1769480 | tf_op jit(solution)/shard_map/ppermute | solution.py:416
  185.3 12.7 %collective-permute-start.3 = (bf16[9,128,128]{2,1,0:T(8,128)(2,1)S(1)}, bf16[9,128,128]{2,1,0:T(8,128)(2,1)S(1)}, u32[]{:S(2)}, u32[]{:S(2)}) collective-permute-start(bf16[9,128,128]{2,1,0:T(8,128)(2,1)S(1)} %slice.28), channel_id=1, source_target_pairs={{0,8},{1,9},{2,10},{3,11},{4,124},{5,125},{6,126},{7,127},{8,16},{... | collective-permute-start | bytes 884744 | tf_op jit(solution)/shard_map/ppermute | solution.py:416
  196.6 2.2 collective-permute-start.20
  196.6 17.7 %collective-permute-start.5 = (bf16[18,128,128]{2,1,0:T(8,128)(2,1)S(1)}, bf16[18,128,128]{2,1,0:T(8,128)(2,1)S(1)}, u32[]{:S(2)}, u32[]{:S(2)}) collective-permute-start(bf16[18,128,128]{2,1,0:T(8,128)(2,1)S(1)} %collective-permute-done.4.refs_10_), channel_id=1, source_target_pairs={{0,8},{1,9},{2,10},{3,11},{4,124},{5,125},{6,126},{7,127},{8,16},{... | collective-permute-start | bytes 1769480 | tf_op jit(solution)/shard_map/ppermute | solution.py:416
  197.8 29.1 %collective-permute-start.8 = (bf16[18,128,128]{2,1,0:T(8,128)(2,1)S(1)}, bf16[18,128,128]{2,1,0:T(8,128)(2,1)S(1)}, u32[]{:S(2)}, u32[]{:S(2)}) collective-permute-start(bf16[18,128,128]{2,1,0:T(8,128)(2,1)S(1)} %collective-permute-done.7.refs_9_), channel_id=1, source_target_pairs={{0,8},{1,9},{2,10},{3,11},{4,124},{5,125},{6,126},{7,127},{8,16},{... | collective-permute-start | bytes 1769480 | tf_op jit(solution)/shard_map/ppermute | solution.py:416
  197.9 41.7 %collective-permute-start.11 = (bf16[18,128,128]{2,1,0:T(8,128)(2,1)S(1)}, bf16[18,128,128]{2,1,0:T(8,128)(2,1)S(1)}, u32[]{:S(2)}, u32[]{:S(2)}) collective-permute-start(bf16[18,128,128]{2,1,0:T(8,128)(2,1)S(1)} %slice.30), channel_id=1, source_target_pairs={{0,8},{1,9},{2,10},{3,11},{4,124},{5,125},{6,126},{7,127},{8,16},{... | collective-permute-start | bytes 1769480 | tf_op jit(solution)/shard_map/ppermute | solution.py:416
  198.0 43.9 %collective-permute-start.22 = (bf16[24,128,128]{2,1,0:T(8,128)(2,1)S(1)}, bf16[24,128,128]{2,1,0:T(8,128)(2,1)S(1)}, u32[]{:S(2)}, u32[]{:S(2)}) collective-permute-start(bf16[24,128,128]{2,1,0:T(8,128)(2,1)S(1)} %collective-permute-done.10.refs_11_), channel_id=1, source_target_pairs={{0,1},{1,0},{2,3},{3,2},{4,5},{5,4},{6,7},{7,6},{8,9},{9,8},{10,11... | collective-permute-start | bytes 2359304 | tf_op jit(solution)/shard_map/ppermute | solution.py:416
  198.8 55.9 %collective-permute-start.1 = (bf16[18,128,128]{2,1,0:T(8,128)(2,1)S(1)}, bf16[18,128,128]{2,1,0:T(8,128)(2,1)S(1)}, u32[]{:S(2)}, u32[]{:S(2)}) collective-permute-start(bf16[18,128,128]{2,1,0:T(8,128)(2,1)S(1)} %collective-permute-done.refs_15_), channel_id=1, source_target_pairs={{0,8},{1,9},{2,10},{3,11},{4,124},{5,125},{6,126},{7,127},{8,16},{... | collective-permute-start | bytes 1769480 | tf_op jit(solution)/shard_map/ppermute | solution.py:416
  214.3 40.4 %collective-permute-start.13 = (bf16[18,128,128]{2,1,0:T(8,128)(2,1)S(1)}, bf16[18,128,128]{2,1,0:T(8,128)(2,1)S(1)}, u32[]{:S(2)}, u32[]{:S(2)}) collective-permute-start(bf16[18,128,128]{2,1,0:T(8,128)(2,1)S(1)} %collective-permute-done.5.refs_4_), channel_id=1, source_target_pairs={{0,1},{1,0},{2,3},{3,2},{4,5},{5,4},{6,7},{7,6},{8,9},{9,8},{10,11... | collective-permute-start | bytes 1769480 | tf_op jit(solution)/shard_map/ppermute | solution.py:416
  226.9 27.8 %collective-permute-start.12 = (bf16[18,128,128]{2,1,0:T(8,128)(2,1)S(1)}, bf16[18,128,128]{2,1,0:T(8,128)(2,1)S(1)}, u32[]{:S(2)}, u32[]{:S(2)}) collective-permute-start(bf16[18,128,128]{2,1,0:T(8,128)(2,1)S(1)} %collective-permute-done.8.refs_3_), channel_id=1, source_target_pairs={{0,1},{1,0},{2,3},{3,2},{4,5},{5,4},{6,7},{7,6},{8,9},{9,8},{10,11... | collective-permute-start | bytes 1769480 | tf_op jit(solution)/shard_map/ppermute | solution.py:416
  239.6 15.2 %collective-permute-start.14 = (bf16[18,128,128]{2,1,0:T(8,128)(2,1)S(1)}, bf16[18,128,128]{2,1,0:T(8,128)(2,1)S(1)}, u32[]{:S(2)}, u32[]{:S(2)}) collective-permute-start(bf16[18,128,128]{2,1,0:T(8,128)(2,1)S(1)} %collective-permute-done.11.refs_5_), channel_id=1, source_target_pairs={{0,1},{1,0},{2,3},{3,2},{4,5},{5,4},{6,7},{7,6},{8,9},{9,8},{10,11... | collective-permute-start | bytes 1769480 | tf_op jit(solution)/shard_map/ppermute | solution.py:416
  241.9 12.8 %collective-permute-start.6 = (bf16[9,128,128]{2,1,0:T(8,128)(2,1)S(1)}, bf16[9,128,128]{2,1,0:T(8,128)(2,1)S(1)}, u32[]{:S(2)}, u32[]{:S(2)}) collective-permute-start(bf16[9,128,128]{2,1,0:T(8,128)(2,1)S(1)} %slice.29), channel_id=1, source_target_pairs={{0,3},{1,2},{2,1},{3,0},{4,7},{5,6},{6,5},{7,4},{8,11},{9,10},{10,... | collective-permute-start | bytes 884744 | tf_op jit(solution)/shard_map/ppermute | solution.py:416

commit v7 on v4

--- a/solution.py
+++ b/solution.py
@@ -123,14 +123,21 @@
     return len(reach(part)) - near_count(part)
 
 
-def load_pieces(pieces, piece_starts, table, sems):
-    copies = []
-    for i, (piece, start) in enumerate(zip(pieces, piece_starts)):
-        copies.append(
-            pltpu.make_async_copy(piece, table.at[pl.ds(start, piece.shape[0])], sems.at[i])
-        )
-        copies[-1].start()
+def load_pieces(pieces, piece_starts, table, sems, order):
+    copies = {part: [] for part in order}
+    for i, (piece, (part, start)) in enumerate(zip(pieces, piece_starts)):
+        place = table.at[pl.ds(start, piece.shape[0])]
+        copies[part].append(pltpu.make_async_copy(piece, place, sems.at[i]))
+    for part in order:
+        for copy in copies[part]:
+            copy.start()
     return copies
+
+
+def wait_for(copies, parts):
+    for part in parts:
+        for copy in copies.pop(part, ()):
+            copy.wait()
 
 
 def lanes_of(ref, parts, group):
@@ -143,10 +150,9 @@
     grids, (square, left_far, table, left, sems) = outs[:9], outs[9:]
     near = 9 * row_count
     group = row_count * width
-    copies = load_pieces(pieces, piece_starts, table, sems)
+    copies = load_pieces(pieces, piece_starts, table, sems, (0, 1, 3, 4, 2, 5))
     table[table_size] = jnp.zeros((width, width), table.dtype)
-    for copy in copies:
-        copy.wait()
+    wait_for(copies, (0,))
 
     def block(m, k):
         return table[jnp.minimum(pos_ref[m * near + k], table_size)]
@@ -155,8 +161,9 @@
         for k in range(near):
             left[r * width:(r + 1) * width, k * width:(k + 1) * width] = block(r, k)
     left_far[...] = left[:, NEAR_PARTS * group:]
-    for part in range(9):
+    for part in (7, 4, 1, 8, 6, 5, 2, 3, 0):
         parts = [q for q in reach(part) if q < NEAR_PARTS]
+        wait_for(copies, parts)
         for i, q in enumerate(parts):
             for r in range(row_count):
                 for k in range(row_count):
@@ -201,14 +208,13 @@
     near = 9 * row_count
     group = row_count * width
     zero_at = table_start + table_size
-    copies = load_pieces(pieces, piece_starts, table, sems)
+    copies = load_pieces(pieces, piece_starts, table, sems, (8, 6, 7))
     table[table_size] = jnp.zeros((width, width), table.dtype)
-    for copy in copies:
-        copy.wait()
-
-    for part in range(9):
+
+    for part in (3, 4, 5, 2, 8, 1, 7, 0, 6):
         parts = reach(part)
         base = near_count(part)
+        wait_for(copies, parts[base:])
         far_base = sum(far_count(q) for q in range(part)) * group
         for i, q in enumerate(parts[base:]):
             for r in range(row_count):
@@ -425,7 +431,7 @@
     far_across_1 = send(ring_across_1, onward)
     ring_same_1 = send(ring_across_1, across)
     own_chip_1 = send(own_1, chip)
-    far_across_2 = send(ring_across_2, onward)
+    far_across_2 = send(ring_across_2[:cut // 2], onward)
     ring_same_2 = send(ring_across_2, across)
     ring_same_3 = send(own_across_3, ring)
     ring_across_t = send(own_t, ring)
@@ -438,6 +444,7 @@
     ring_chip_3 = send(ring_same_3, chip)
     far_same_2 = send(ring_same_2, onward)
     ring_chip_2 = send(ring_same_2, chip)
+    far_across_3 = send(far_same_2[cut // 2:], across)
     far_chip_1 = send(far_same_1, chip)
     far_chip_3 = send(far_same_3, chip)
     far_chip_2 = send(far_same_2, chip)
@@ -453,17 +460,17 @@
     far_pieces = [
         (far_same_1, 6, 0), (far_same_2, 6, cut), (far_same_3, 6, 2 * cut),
         (far_chip_1, 7, 0), (far_chip_2, 7, cut), (far_chip_3, 7, 2 * cut),
-        (far_across_1, 8, 0), (far_across_2, 8, cut),
+        (far_across_1, 8, 0), (far_across_2, 8, cut), (far_across_3, 8, cut + cut // 2),
     ]
     far_start = starts[NEAR_PARTS]
     carried = square_near(
         positions, [piece for piece, _, _ in near_pieces],
-        [starts[part] + offset for _, part, offset in near_pieces],
+        [(part, starts[part] + offset) for _, part, offset in near_pieces],
         far_start, row_count, width,
     )
     purified = purify_far(
         positions, out_slots, [piece for piece, _, _ in far_pieces],
-        [starts[part] + offset - far_start for _, part, offset in far_pieces],
+        [(part, starts[part] + offset - far_start) for _, part, offset in far_pieces],
         carried, far_start, zero_at - far_start, row_count, slot_count, width,
     )
     return purified.reshape(density.shape)

time: 279 us -> 268 us (0.961)
  waiting for transfers between devices: 192 us -> 182 us
    ppermute x23 -> x24, waiting for transfers between devices: 98.3 us -> 88.1 us  [send(): return lax.ppermute(array, axes, pairs)]
    ppermute x23 -> x24, starting transfers between devices: 28 us -> 27.9 us  [send(): return lax.ppermute(array, axes, pairs)]
  transfers between devices with their start and end apart: 24 -> 25, of which waited for: 10 -> 10; matrix products, arithmetic and copies ran while one was open for 2% -> 2% of each run, Pallas kernels for 6% -> 6%
where the time goes in v7:
time: 268 us
  waiting for transfers between devices  182 us (68%)
  Pallas kernels  40.2 us (15%)
  starting transfers between devices  39.9 us (15%)
  other arithmetic  3.34 us (1%)
    all_to_all x1, waiting for transfers between devices, per_device(): lax.all_to_all(outgoing.reshape(device_count, C, width, width), ('gx', 'g...  93.6 us
    ppermute x24, waiting for transfers between devices, send(): return lax.ppermute(array, axes, pairs)  88.1 us
    ppermute x24, starting transfers between devices, send(): return lax.ppermute(array, axes, pairs)  27.9 us
    pallas_call x1, Pallas kernels, purify_far(): pl.pallas_call(functools.partial(far_kernel, row_count, width, piece_star...  13.7 us
    pallas_call x2, Pallas kernels, admit(): pl.pallas_call(functools.partial(admit_kernel, spans), out_shape=[jax.Sha...  12.1 us
    all_to_all x1, starting transfers between devices, per_device(): lax.all_to_all(outgoing.reshape(device_count, C, width, width), ('gx', 'g...  12 us
    pallas_call x1, Pallas kernels, square_near(): pl.pallas_call(functools.partial(near_kernel, row_count, width, piece_sta...  10.1 us
  transfers between devices with their start and end apart: 25, of which 10 were waited for; matrix products, arithmetic and copies ran while one was open for 2% of the time, Pallas kernels for 6%

profile of v7, /device:TPU:1, one launch (start us, length us, event | category | flops | bytes accessed | tf_op | source)
XLA Modules:
  0.0 268.0 jit_solution(7063326748275997274)
XLA Ops:
  0.0 4.4 %pack.1 = bf16[256,128,128]{2,1,0:T(8,128)(2,1)} custom-call(s32[1]{0:T(128)} %bitcast.base_ref, s32[12288]{0:T(1024)} %owner_ref.1, bf16[96,128,128]{2,1,0:T(8,128)(2,1)} %ent_ref.1), custom_call_target="tpu_custom_call" | custom-call | tf_op jit(solution)/shard_map/pack/pallas_call | solution.py:43
  4.4 12.0 %all-to-all-start = ((bf16[128,2,128,128]{3,2,1,0:T(8,128)(2,1)}), bf16[128,2,128,128]{3,2,1,0:T(8,128)(2,1)}, u32[]{:S(2)}, u32[]{:S(2)}) async-start(bf16[128,2,128,128]{3,2,1,0:T(8,128)(2,1)} %bitcast.9), calls=%async_computation | async-start | bytes 16777216 | tf_op jit(solution)/shard_map/all_to_all | solution.py:362
  16.8 0.6 gather_fusion
  18.3 0.3 select_reduce_fusion
  19.9 0.7 select_reduce_fusion.4.source_ref
  20.6 0.6 convert_reduce_fusion.2.first_ref
  21.4 0.7 select_reduce_fusion.1.order_ref
  22.1 93.6 %all-to-all-done = bf16[128,2,128,128]{3,2,1,0:T(8,128)(2,1)} async-done(((bf16[128,2,128,128]{3,2,1,0:T(8,128)(2,1)}), bf16[128,2,128,128]{3,2,1,0:T(8,128)(2,1)}, u32[]{:S(2)}, u32[]{:S(2)}) %all-to-all-start) | async-done | bytes 8388640 | tf_op jit(solution)/shard_map/all_to_all | solution.py:362
  115.8 6.7 %admit.2 = (bf16[18,128,128]{2,1,0:T(8,128)(2,1)}, bf16[24,128,128]{2,1,0:T(8,128)(2,1)}, bf16[18,128,128]{2,1,0:T(8,128)(2,1)}) custom-call(s32[61]{0:T(128)} %convert_reduce_fusion.2.first_ref, s32[256]{0:T(256)} %select_reduce_fusion.1.order_ref, s32[60]{0:T(128)} %select_reduce_fusion.4.source_ref, bf16[60,128,128]{2,1,0:T(8,128)(2,1)} %bitcast.10, ...), custom_call_target="tpu_custom_call" | custom-call | tf_op jit(solution)/shard_map/admit/pallas_call | solution.py:91
  122.5 6.2 %collective-permute-start.6 = (bf16[24,128,128]{2,1,0:T(8,128)(2,1)}, bf16[24,128,128]{2,1,0:T(8,128)(2,1)S(1)}, u32[]{:S(2)}, u32[]{:S(2)}) collective-permute-start(bf16[24,128,128]{2,1,0:T(8,128)(2,1)} %get-tuple-element.32.refs_2_), channel_id=1, source_target_pairs={{0,3},{1,2},{2,1},{3,0},{4,7},{5,6},{6,5},{7,4},{8,11},{9,10},{10,... | collective-permute-start | bytes 2359304 | tf_op jit(solution)/shard_map/ppermute | solution.py:413
  128.7 5.4 %admit.3.refs_1_ = bf16[18,128,128]{2,1,0:T(8,128)(2,1)} custom-call(s32[61]{0:T(128)} %convert_reduce_fusion.2.first_ref, s32[256]{0:T(256)} %select_reduce_fusion.1.order_ref, s32[60]{0:T(128)} %select_reduce_fusion.4.source_ref, bf16[60,128,128]{2,1,0:T(8,128)(2,1)} %bitcast.11, bf16[256,128,128]{2,1,0:T(8,128)(2,1)} %bitcast.2.received_ref), custom_call_target="tpu_custom_call" | custom-call | tf_op jit(solution)/shard_map/admit/pallas_call | solution.py:91
  134.4 2.8 %collective-permute-start = (bf16[18,128,128]{2,1,0:T(8,128)(2,1)S(1)}, bf16[18,128,128]{2,1,0:T(8,128)(2,1)S(1)}, u32[]{:S(2)}, u32[]{:S(2)}) collective-permute-start(bf16[18,128,128]{2,1,0:T(8,128)(2,1)S(1)} %copy-done.2), channel_id=1, source_target_pairs={{0,7},{1,6},{2,5},{3,4},{4,3},{5,2},{6,1},{7,0},{8,15},{9,14},{10,... | collective-permute-start | bytes 1769480 | tf_op jit(solution)/shard_map/ppermute | solution.py:413
  137.2 14.3 %collective-permute-done.3.refs_16_ = bf16[18,128,128]{2,1,0:T(8,128)(2,1)S(1)} collective-permute-done((bf16[18,128,128]{2,1,0:T(8,128)(2,1)}, bf16[18,128,128]{2,1,0:T(8,128)(2,1)S(1)}, u32[]{:S(2)}, u32[]{:S(2)}) %collective-permute-start.3) | collective-permute-done | bytes 589856 | tf_op jit(solution)/shard_map/ppermute | solution.py:413
  151.5 8.4 %collective-permute-done.19.refs_7_ = bf16[18,128,128]{2,1,0:T(8,128)(2,1)S(1)} collective-permute-done((bf16[18,128,128]{2,1,0:T(8,128)(2,1)}, bf16[18,128,128]{2,1,0:T(8,128)(2,1)S(1)}, u32[]{:S(2)}, u32[]{:S(2)}) %collective-permute-start.19) | collective-permute-done | bytes 589856 | tf_op jit(solution)/shard_map/ppermute | solution.py:413
  159.9 1.4 collective-permute-start.4
  161.4 1.2 collective-permute-done.refs_15_
  162.7 9.8 %collective-permute-done.18.refs_6_ = bf16[18,128,128]{2,1,0:T(8,128)(2,1)S(1)} collective-permute-done((bf16[18,128,128]{2,1,0:T(8,128)(2,1)S(1)}, bf16[18,128,128]{2,1,0:T(8,128)(2,1)S(1)}, u32[]{:S(2)}, u32[]{:S(2)}) %collective-permute-start.18) | collective-permute-done | bytes 589856 | tf_op jit(solution)/shard_map/ppermute | solution.py:413
  172.6 12.6 %collective-permute-done.4.refs_10_ = bf16[18,128,128]{2,1,0:T(8,128)(2,1)S(1)} collective-permute-done((bf16[18,128,128]{2,1,0:T(8,128)(2,1)S(1)}, bf16[18,128,128]{2,1,0:T(8,128)(2,1)S(1)}, u32[]{:S(2)}, u32[]{:S(2)}) %collective-permute-start.4) | collective-permute-done | bytes 589856 | tf_op jit(solution)/shard_map/ppermute | solution.py:413
  185.3 1.5 collective-permute-start.13
  186.8 9.8 %collective-permute-done.1.refs_9_ = bf16[18,128,128]{2,1,0:T(8,128)(2,1)S(1)} collective-permute-done((bf16[18,128,128]{2,1,0:T(8,128)(2,1)S(1)}, bf16[18,128,128]{2,1,0:T(8,128)(2,1)S(1)}, u32[]{:S(2)}, u32[]{:S(2)}) %collective-permute-start.1) | collective-permute-done | bytes 589856 | tf_op jit(solution)/shard_map/ppermute | solution.py:413
  196.6 1.2 collective-permute-start.5
  198.0 0.8 collective-permute-start.22
  198.8 4.3 %collective-permute-start.12 = (bf16[18,128,128]{2,1,0:T(8,128)(2,1)S(1)}, bf16[18,128,128]{2,1,0:T(8,128)(2,1)S(1)}, u32[]{:S(2)}, u32[]{:S(2)}) collective-permute-start(bf16[18,128,128]{2,1,0:T(8,128)(2,1)S(1)} %collective-permute-done.refs_15_), channel_id=1, source_target_pairs={{0,8},{1,9},{2,10},{3,11},{4,124},{5,125},{6,126},{7,127},{8,16},{... | collective-permute-start | bytes 1769480 | tf_op jit(solution)/shard_map/ppermute | solution.py:413
  203.1 11.2 %collective-permute-done.5.refs_1_ = bf16[18,128,128]{2,1,0:T(8,128)(2,1)S(1)} collective-permute-done((bf16[18,128,128]{2,1,0:T(8,128)(2,1)S(1)}, bf16[18,128,128]{2,1,0:T(8,128)(2,1)S(1)}, u32[]{:S(2)}, u32[]{:S(2)}) %collective-permute-start.5) | collective-permute-done | bytes 589856 | tf_op jit(solution)/shard_map/ppermute | solution.py:413
  214.3 2.3 collective-permute-start.10
  216.6 10.3 %collective-permute-done.2.refs_0_ = bf16[18,128,128]{2,1,0:T(8,128)(2,1)S(1)} collective-permute-done((bf16[18,128,128]{2,1,0:T(8,128)(2,1)S(1)}, bf16[18,128,128]{2,1,0:T(8,128)(2,1)S(1)}, u32[]{:S(2)}, u32[]{:S(2)}) %collective-permute-start.2) | collective-permute-done | bytes 589856 | tf_op jit(solution)/shard_map/ppermute | solution.py:413
  226.9 2.3 collective-permute-start.9
  229.3 10.3 %collective-permute-done.8.refs_2_ = bf16[18,128,128]{2,1,0:T(8,128)(2,1)S(1)} collective-permute-done((bf16[18,128,128]{2,1,0:T(8,128)(2,1)S(1)}, bf16[18,128,128]{2,1,0:T(8,128)(2,1)S(1)}, u32[]{:S(2)}, u32[]{:S(2)}) %collective-permute-start.8) | collective-permute-done | bytes 589856 | tf_op jit(solution)/shard_map/ppermute | solution.py:413
  239.6 2.3 collective-permute-start.11
  241.9 2.1 collective-permute-start.14
  244.0 10.1 %square_near.1 = (bf16[2304,384]{1,0:T(8,128)(2,1)S(1)}, bf16[1536,384]{1,0:T(8,128)(2,1)S(1)}, bf16[1536,384]{1,0:T(8,128)(2,1)S(1)}, bf16[2304,384]{1,0:T(8,12...) custom-call(s32[729]{0:T(1024)S(1)} %reshape.495.pos_ref, ...), custom_call_target="tpu_custom_call" | custom-call | tf_op jit(solution)/shard_map/square_near/pallas_call | solution.py:182
  254.2 13.7 %purify_far.1 = f32[60,128,128]{2,1,0:T(8,128)} custom-call(s32[729]{0:T(1024)S(1)} %reshape.495.pos_ref, s32[81]{0:T(128)S(1)} %reshape.496.slot_ref, bf16[18,128,128]{2,1,0:T(8,128)(2,1)S(1)} %collective-permute-done.2.refs_0_, bf16[18,128,128]{2,1,0:T(8,128)(2,1)S(1)} %collective-permute-done.5.refs_1_, ...), custom_call_target="tpu_custom_call" | custom-call | tf_op jit(solution)/shard_map/purify_far/pallas_call | solution.py:277
  (83 shorter events, 3.4 us)
Async XLA Ops:
  4.4 12.1 %copy-start.4 = (s32[32,4,3,20]{0,1,3,2:T(4,128)S(1)}, s32[32,4,3,20]{0,1,3,2:T(4,128)}, u32[]{:S(2)}) copy-start(s32[32,4,3,20]{0,1,3,2:T(4,128)} %param.6) | copy-start | bytes 92164
  4.4 14.5 %copy-start.3 = (s32[12288]{0:T(1024)S(1)}, s32[12288]{0:T(1024)}, u32[]{:S(2)}) copy-start(s32[12288]{0:T(1024)} %owner_ref.1) | copy-start | bytes 147460
  4.4 111.4 %all-to-all-start = ((bf16[128,2,128,128]{3,2,1,0:T(8,128)(2,1)}), bf16[128,2,128,128]{3,2,1,0:T(8,128)(2,1)}, u32[]{:S(2)}, u32[]{:S(2)}) async-start(bf16[128,2,128,128]{3,2,1,0:T(8,128)(2,1)} %bitcast.9), calls=%async_computation | async-start | bytes 16777216 | tf_op jit(solution)/shard_map/all_to_all | solution.py:362
  16.4 3.0 %copy-start.5 = (s32[12288]{0:T(1024)S(1)}, s32[12288]{0:T(1024)}, u32[]{:S(2)}) copy-start(s32[12288]{0:T(1024)} %param.9) | copy-start | bytes 147460
  122.4 12.0 %copy-start.2 = (bf16[18,128,128]{2,1,0:T(8,128)(2,1)S(1)}, bf16[18,128,128]{2,1,0:T(8,128)(2,1)}, u32[]{:S(2)}) copy-start(bf16[18,128,128]{2,1,0:T(8,128)(2,1)} %get-tuple-element.31.refs_0_) | copy-start | bytes 1769476
  122.4 40.2 %copy-start.1 = (bf16[24,128,128]{2,1,0:T(8,128)(2,1)S(1)}, bf16[24,128,128]{2,1,0:T(8,128)(2,1)}, u32[]{:S(2)}) copy-start(bf16[24,128,128]{2,1,0:T(8,128)(2,1)} %get-tuple-element.32.refs_2_) | copy-start | bytes 2359300
  122.4 50.1 %copy-start.6 = (bf16[18,128,128]{2,1,0:T(8,128)(2,1)S(1)}, bf16[18,128,128]{2,1,0:T(8,128)(2,1)}, u32[]{:S(2)}) copy-start(bf16[18,128,128]{2,1,0:T(8,128)(2,1)} %get-tuple-element.33) | copy-start | bytes 1769476
  122.5 38.9 %collective-permute-start.6 = (bf16[24,128,128]{2,1,0:T(8,128)(2,1)}, bf16[24,128,128]{2,1,0:T(8,128)(2,1)S(1)}, u32[]{:S(2)}, u32[]{:S(2)}) collective-permute-start(bf16[24,128,128]{2,1,0:T(8,128)(2,1)} %get-tuple-element.32.refs_2_), channel_id=1, source_target_pairs={{0,3},{1,2},{2,1},{3,0},{4,7},{5,6},{6,5},{7,4},{8,11},{9,10},{10,... | collective-permute-start | bytes 2359304 | tf_op jit(solution)/shard_map/ppermute | solution.py:413
  134.1 109.9 %copy-start = (bf16[18,128,128]{2,1,0:T(8,128)(2,1)S(1)}, bf16[18,128,128]{2,1,0:T(8,128)(2,1)}, u32[]{:S(2)}) copy-start(bf16[18,128,128]{2,1,0:T(8,128)(2,1)} %admit.3.refs_1_) | copy-start | bytes 1769476
  134.1 17.4 %collective-permute-start.3 = (bf16[18,128,128]{2,1,0:T(8,128)(2,1)}, bf16[18,128,128]{2,1,0:T(8,128)(2,1)S(1)}, u32[]{:S(2)}, u32[]{:S(2)}) collective-permute-start(bf16[18,128,128]{2,1,0:T(8,128)(2,1)} %admit.3.refs_1_), channel_id=1, source_target_pairs={{0,7},{1,6},{2,5},{3,4},{4,3},{5,2},{6,1},{7,0},{8,15},{9,14},{10,... | collective-permute-start | bytes 1769480 | tf_op jit(solution)/shard_map/ppermute | solution.py:413
  134.2 17.3 %collective-permute-start.16 = (bf16[18,128,128]{2,1,0:T(8,128)(2,1)}, bf16[18,128,128]{2,1,0:T(8,128)(2,1)S(1)}, u32[]{:S(2)}, u32[]{:S(2)}) collective-permute-start(bf16[18,128,128]{2,1,0:T(8,128)(2,1)} %admit.3.refs_1_), channel_id=1, source_target_pairs={{0,1},{1,0},{2,3},{3,2},{4,5},{5,4},{6,7},{7,6},{8,9},{9,8},{10,11... | collective-permute-start | bytes 1769480 | tf_op jit(solution)/shard_map/ppermute | solution.py:413
  134.3 25.6 %collective-permute-start.19 = (bf16[18,128,128]{2,1,0:T(8,128)(2,1)}, bf16[18,128,128]{2,1,0:T(8,128)(2,1)S(1)}, u32[]{:S(2)}, u32[]{:S(2)}) collective-permute-start(bf16[18,128,128]{2,1,0:T(8,128)(2,1)} %admit.3.refs_1_), channel_id=1, source_target_pairs={{0,3},{1,2},{2,1},{3,0},{4,7},{5,6},{6,5},{7,4},{8,11},{9,10},{10,... | collective-permute-start | bytes 1769480 | tf_op jit(solution)/shard_map/ppermute | solution.py:413
  134.4 28.2 %collective-permute-start = (bf16[18,128,128]{2,1,0:T(8,128)(2,1)S(1)}, bf16[18,128,128]{2,1,0:T(8,128)(2,1)S(1)}, u32[]{:S(2)}, u32[]{:S(2)}) collective-permute-start(bf16[18,128,128]{2,1,0:T(8,128)(2,1)S(1)} %copy-done.2), channel_id=1, source_target_pairs={{0,7},{1,6},{2,5},{3,4},{4,3},{5,2},{6,1},{7,0},{8,15},{9,14},{10,... | collective-permute-start | bytes 1769480 | tf_op jit(solution)/shard_map/ppermute | solution.py:413
  151.5 11.1 %collective-permute-start.15 = (bf16[18,128,128]{2,1,0:T(8,128)(2,1)S(1)}, bf16[18,128,128]{2,1,0:T(8,128)(2,1)S(1)}, u32[]{:S(2)}, u32[]{:S(2)}) collective-permute-start(bf16[18,128,128]{2,1,0:T(8,128)(2,1)S(1)} %copy-done.2), channel_id=1, source_target_pairs={{0,1},{1,0},{2,3},{3,2},{4,5},{5,4},{6,7},{7,6},{8,9},{9,8},{10,11... | collective-permute-start | bytes 1769480 | tf_op jit(solution)/shard_map/ppermute | solution.py:413
  151.5 21.0 %collective-permute-start.18 = (bf16[18,128,128]{2,1,0:T(8,128)(2,1)S(1)}, bf16[18,128,128]{2,1,0:T(8,128)(2,1)S(1)}, u32[]{:S(2)}, u32[]{:S(2)}) collective-permute-start(bf16[18,128,128]{2,1,0:T(8,128)(2,1)S(1)} %copy-done.2), channel_id=1, source_target_pairs={{0,3},{1,2},{2,1},{3,0},{4,7},{5,6},{6,5},{7,4},{8,11},{9,10},{10,... | collective-permute-start | bytes 1769480 | tf_op jit(solution)/shard_map/ppermute | solution.py:413
  159.9 25.3 %collective-permute-start.4 = (bf16[18,128,128]{2,1,0:T(8,128)(2,1)S(1)}, bf16[18,128,128]{2,1,0:T(8,128)(2,1)S(1)}, u32[]{:S(2)}, u32[]{:S(2)}) collective-permute-start(bf16[18,128,128]{2,1,0:T(8,128)(2,1)S(1)} %collective-permute-done.3.refs_16_), channel_id=1, source_target_pairs={{0,3},{1,2},{2,1},{3,0},{4,7},{5,6},{6,5},{7,4},{8,11},{9,10},{10,... | collective-permute-start | bytes 1769480 | tf_op jit(solution)/shard_map/ppermute | solution.py:413
  161.4 23.9 %collective-permute-start.7 = (bf16[24,128,128]{2,1,0:T(8,128)(2,1)S(1)}, bf16[24,128,128]{2,1,0:T(8,128)(2,1)S(1)}, u32[]{:S(2)}, u32[]{:S(2)}) collective-permute-start(bf16[24,128,128]{2,1,0:T(8,128)(2,1)S(1)} %collective-permute-done.6.refs_8_), channel_id=1, source_target_pairs={{0,7},{1,6},{2,5},{3,4},{4,3},{5,2},{6,1},{7,0},{8,15},{9,14},{10,... | collective-permute-start | bytes 2359304 | tf_op jit(solution)/shard_map/ppermute | solution.py:413
  162.6 35.2 %collective-permute-start.17 = (bf16[24,128,128]{2,1,0:T(8,128)(2,1)S(1)}, bf16[24,128,128]{2,1,0:T(8,128)(2,1)S(1)}, u32[]{:S(2)}, u32[]{:S(2)}) collective-permute-start(bf16[24,128,128]{2,1,0:T(8,128)(2,1)S(1)} %copy-done.1), channel_id=1, source_target_pairs={{0,1},{1,0},{2,3},{3,2},{4,5},{5,4},{6,7},{7,6},{8,9},{9,8},{10,11... | collective-permute-start | bytes 2359304 | tf_op jit(solution)/shard_map/ppermute | solution.py:413
  162.6 34.0 %collective-permute-start.1 = (bf16[18,128,128]{2,1,0:T(8,128)(2,1)S(1)}, bf16[18,128,128]{2,1,0:T(8,128)(2,1)S(1)}, u32[]{:S(2)}, u32[]{:S(2)}) collective-permute-start(bf16[18,128,128]{2,1,0:T(8,128)(2,1)S(1)} %collective-permute-done.refs_15_), channel_id=1, source_target_pairs={{0,3},{1,2},{2,1},{3,0},{4,7},{5,6},{6,5},{7,4},{8,11},{9,10},{10,... | collective-permute-start | bytes 1769480 | tf_op jit(solution)/shard_map/ppermute | solution.py:413
  172.6 24.0 %collective-permute-start.23 = (bf16[18,128,128]{2,1,0:T(8,128)(2,1)S(1)}, bf16[18,128,128]{2,1,0:T(8,128)(2,1)S(1)}, u32[]{:S(2)}, u32[]{:S(2)}) collective-permute-start(bf16[18,128,128]{2,1,0:T(8,128)(2,1)S(1)} %copy-done.6), channel_id=1, source_target_pairs={{0,7},{1,6},{2,5},{3,4},{4,3},{5,2},{6,1},{7,0},{8,15},{9,14},{10,... | collective-permute-start | bytes 1769480 | tf_op jit(solution)/shard_map/ppermute | solution.py:413
  185.2 12.8 %collective-permute-start.21 = (bf16[18,128,128]{2,1,0:T(8,128)(2,1)S(1)}, bf16[18,128,128]{2,1,0:T(8,128)(2,1)S(1)}, u32[]{:S(2)}, u32[]{:S(2)}) collective-permute-start(bf16[18,128,128]{2,1,0:T(8,128)(2,1)S(1)} %collective-permute-done.4.refs_10_), channel_id=1, source_target_pairs={{0,1},{1,0},{2,3},{3,2},{4,5},{5,4},{6,7},{7,6},{8,9},{9,8},{10,11... | collective-permute-start | bytes 1769480 | tf_op jit(solution)/shard_map/ppermute | solution.py:413
  185.3 12.7 %collective-permute-start.13 = (bf16[9,128,128]{2,1,0:T(8,128)(2,1)S(1)}, bf16[9,128,128]{2,1,0:T(8,128)(2,1)S(1)}, u32[]{:S(2)}, u32[]{:S(2)}) collective-permute-start(bf16[9,128,128]{2,1,0:T(8,128)(2,1)S(1)} %slice.29), channel_id=1, source_target_pairs={{0,8},{1,9},{2,10},{3,11},{4,124},{5,125},{6,126},{7,127},{8,16},{... | collective-permute-start | bytes 884744 | tf_op jit(solution)/shard_map/ppermute | solution.py:413
  196.6 2.2 collective-permute-start.20
  196.6 17.7 %collective-permute-start.5 = (bf16[18,128,128]{2,1,0:T(8,128)(2,1)S(1)}, bf16[18,128,128]{2,1,0:T(8,128)(2,1)S(1)}, u32[]{:S(2)}, u32[]{:S(2)}) collective-permute-start(bf16[18,128,128]{2,1,0:T(8,128)(2,1)S(1)} %collective-permute-done.4.refs_10_), channel_id=1, source_target_pairs={{0,8},{1,9},{2,10},{3,11},{4,124},{5,125},{6,126},{7,127},{8,16},{... | collective-permute-start | bytes 1769480 | tf_op jit(solution)/shard_map/ppermute | solution.py:413
  197.8 29.1 %collective-permute-start.2 = (bf16[18,128,128]{2,1,0:T(8,128)(2,1)S(1)}, bf16[18,128,128]{2,1,0:T(8,128)(2,1)S(1)}, u32[]{:S(2)}, u32[]{:S(2)}) collective-permute-start(bf16[18,128,128]{2,1,0:T(8,128)(2,1)S(1)} %collective-permute-done.1.refs_9_), channel_id=1, source_target_pairs={{0,8},{1,9},{2,10},{3,11},{4,124},{5,125},{6,126},{7,127},{8,16},{... | collective-permute-start | bytes 1769480 | tf_op jit(solution)/shard_map/ppermute | solution.py:413
  197.9 41.7 %collective-permute-start.8 = (bf16[18,128,128]{2,1,0:T(8,128)(2,1)S(1)}, bf16[18,128,128]{2,1,0:T(8,128)(2,1)S(1)}, u32[]{:S(2)}, u32[]{:S(2)}) collective-permute-start(bf16[18,128,128]{2,1,0:T(8,128)(2,1)S(1)} %slice.28), channel_id=1, source_target_pairs={{0,8},{1,9},{2,10},{3,11},{4,124},{5,125},{6,126},{7,127},{8,16},{... | collective-permute-start | bytes 1769480 | tf_op jit(solution)/shard_map/ppermute | solution.py:413
  198.0 43.9 %collective-permute-start.22 = (bf16[24,128,128]{2,1,0:T(8,128)(2,1)S(1)}, bf16[24,128,128]{2,1,0:T(8,128)(2,1)S(1)}, u32[]{:S(2)}, u32[]{:S(2)}) collective-permute-start(bf16[24,128,128]{2,1,0:T(8,128)(2,1)S(1)} %collective-permute-done.7.refs_11_), channel_id=1, source_target_pairs={{0,1},{1,0},{2,3},{3,2},{4,5},{5,4},{6,7},{7,6},{8,9},{9,8},{10,11... | collective-permute-start | bytes 2359304 | tf_op jit(solution)/shard_map/ppermute | solution.py:413
  198.8 55.4 %collective-permute-start.12 = (bf16[18,128,128]{2,1,0:T(8,128)(2,1)S(1)}, bf16[18,128,128]{2,1,0:T(8,128)(2,1)S(1)}, u32[]{:S(2)}, u32[]{:S(2)}) collective-permute-start(bf16[18,128,128]{2,1,0:T(8,128)(2,1)S(1)} %collective-permute-done.refs_15_), channel_id=1, source_target_pairs={{0,8},{1,9},{2,10},{3,11},{4,124},{5,125},{6,126},{7,127},{8,16},{... | collective-permute-start | bytes 1769480 | tf_op jit(solution)/shard_map/ppermute | solution.py:413
  214.3 39.9 %collective-permute-start.10 = (bf16[18,128,128]{2,1,0:T(8,128)(2,1)S(1)}, bf16[18,128,128]{2,1,0:T(8,128)(2,1)S(1)}, u32[]{:S(2)}, u32[]{:S(2)}) collective-permute-start(bf16[18,128,128]{2,1,0:T(8,128)(2,1)S(1)} %collective-permute-done.5.refs_1_), channel_id=1, source_target_pairs={{0,1},{1,0},{2,3},{3,2},{4,5},{5,4},{6,7},{7,6},{8,9},{9,8},{10,11... | collective-permute-start | bytes 1769480 | tf_op jit(solution)/shard_map/ppermute | solution.py:413
  226.9 27.2 %collective-permute-start.9 = (bf16[18,128,128]{2,1,0:T(8,128)(2,1)S(1)}, bf16[18,128,128]{2,1,0:T(8,128)(2,1)S(1)}, u32[]{:S(2)}, u32[]{:S(2)}) collective-permute-start(bf16[18,128,128]{2,1,0:T(8,128)(2,1)S(1)} %collective-permute-done.2.refs_0_), channel_id=1, source_target_pairs={{0,1},{1,0},{2,3},{3,2},{4,5},{5,4},{6,7},{7,6},{8,9},{9,8},{10,11... | collective-permute-start | bytes 1769480 | tf_op jit(solution)/shard_map/ppermute | solution.py:413
  239.6 14.6 %collective-permute-start.11 = (bf16[18,128,128]{2,1,0:T(8,128)(2,1)S(1)}, bf16[18,128,128]{2,1,0:T(8,128)(2,1)S(1)}, u32[]{:S(2)}, u32[]{:S(2)}) collective-permute-start(bf16[18,128,128]{2,1,0:T(8,128)(2,1)S(1)} %collective-permute-done.8.refs_2_), channel_id=1, source_target_pairs={{0,1},{1,0},{2,3},{3,2},{4,5},{5,4},{6,7},{7,6},{8,9},{9,8},{10,11... | collective-permute-start | bytes 1769480 | tf_op jit(solution)/shard_map/ppermute | solution.py:413
  241.9 12.2 %collective-permute-start.14 = (bf16[9,128,128]{2,1,0:T(8,128)(2,1)S(1)}, bf16[9,128,128]{2,1,0:T(8,128)(2,1)S(1)}, u32[]{:S(2)}, u32[]{:S(2)}) collective-permute-start(bf16[9,128,128]{2,1,0:T(8,128)(2,1)S(1)} %slice.30), channel_id=1, source_target_pairs={{0,3},{1,2},{2,1},{3,0},{4,7},{5,6},{6,5},{7,4},{8,11},{9,10},{10,... | collective-permute-start | bytes 884744 | tf_op jit(solution)/shard_map/ppermute | solution.py:413

commit v8 on v4

--- a/solution.py
+++ b/solution.py
@@ -101,6 +101,7 @@
             pltpu.VMEM(density.shape, density.dtype),
             pltpu.SemaphoreType.DMA((len(spans),)),
         ],
+        compiler_params=pltpu.CompilerParams(vmem_limit_bytes=16 << 20),
         name="admit",
     )(first, order, source, density, received)
 
@@ -425,7 +426,7 @@
     far_across_1 = send(ring_across_1, onward)
     ring_same_1 = send(ring_across_1, across)
     own_chip_1 = send(own_1, chip)
-    far_across_2 = send(ring_across_2, onward)
+    far_across_2 = send(ring_across_2[:cut // 2], onward)
     ring_same_2 = send(ring_across_2, across)
     ring_same_3 = send(own_across_3, ring)
     ring_across_t = send(own_t, ring)
@@ -438,6 +439,7 @@
     ring_chip_3 = send(ring_same_3, chip)
     far_same_2 = send(ring_same_2, onward)
     ring_chip_2 = send(ring_same_2, chip)
+    far_across_3 = send(far_same_2[cut // 2:], across)
     far_chip_1 = send(far_same_1, chip)
     far_chip_3 = send(far_same_3, chip)
     far_chip_2 = send(far_same_2, chip)
@@ -453,7 +455,7 @@
     far_pieces = [
         (far_same_1, 6, 0), (far_same_2, 6, cut), (far_same_3, 6, 2 * cut),
         (far_chip_1, 7, 0), (far_chip_2, 7, cut), (far_chip_3, 7, 2 * cut),
-        (far_across_1, 8, 0), (far_across_2, 8, cut),
+        (far_across_1, 8, 0), (far_across_2, 8, cut), (far_across_3, 8, cut + cut // 2),
     ]
     far_start = starts[NEAR_PARTS]
     carried = square_near(

time: 279 us -> 265 us (0.950)
  waiting for transfers between devices: 192 us -> 184 us
    ppermute x23 -> x24, waiting for transfers between devices: 98.3 us -> 88.9 us  [send(): return lax.ppermute(array, axes, pairs)]
    ppermute x23 -> x24, starting transfers between devices: 28 us -> 28.2 us  [send(): return lax.ppermute(array, axes, pairs)]
  transfers between devices with their start and end apart: 24 -> 25, of which waited for: 10 -> 9; matrix products, arithmetic and copies ran while one was open for 2% -> 1% of each run, Pallas kernels for 6% -> 5%
where the time goes in v8:
time: 265 us; the launch traced here: 264 us
  waiting for transfers between devices  184 us (69%)
  starting transfers between devices  40.1 us (15%)
  Pallas kernels  35.7 us (13%)
    all_to_all x1, waiting for transfers between devices, per_device(): lax.all_to_all(outgoing.reshape(device_count, C, width, width), ('gx', 'g...  95.3 us
    ppermute x24, waiting for transfers between devices, send(): return lax.ppermute(array, axes, pairs)  88.9 us
    ppermute x24, starting transfers between devices, send(): return lax.ppermute(array, axes, pairs)  28.2 us
    pallas_call x1, Pallas kernels, purify_far(): pl.pallas_call(functools.partial(far_kernel, row_count, width, piece_star...  13 us
    all_to_all x1, starting transfers between devices, per_device(): lax.all_to_all(outgoing.reshape(device_count, C, width, width), ('gx', 'g...  11.9 us
    pallas_call x2, Pallas kernels, admit(): pl.pallas_call(functools.partial(admit_kernel, spans), out_shape=[jax.Sha...  9.38 us
    pallas_call x1, Pallas kernels, square_near(): pl.pallas_call(functools.partial(near_kernel, row_count, width, piece_sta...  9.03 us
  transfers between devices with their start and end apart: 25, of which 9 were waited for; matrix products, arithmetic and copies ran while one was open for 1% of the time, Pallas kernels for 5%

profile of v8, /device:TPU:1, one launch (start us, length us, event | category | flops | bytes accessed | tf_op | source)
XLA Modules:
  0.0 264.5 jit_solution(15883607845394883864)
XLA Ops:
  0.0 4.3 %pack.1 = bf16[256,128,128]{2,1,0:T(8,128)(2,1)} custom-call(s32[1]{0:T(128)} %bitcast.base_ref, s32[12288]{0:T(1024)} %owner_ref.1, bf16[96,128,128]{2,1,0:T(8,128)(2,1)} %ent_ref.1), custom_call_target="tpu_custom_call" | custom-call | tf_op jit(solution)/shard_map/pack/pallas_call | solution.py:43
  4.3 11.9 %all-to-all-start = ((bf16[128,2,128,128]{3,2,1,0:T(8,128)(2,1)}), bf16[128,2,128,128]{3,2,1,0:T(8,128)(2,1)}, u32[]{:S(2)}, u32[]{:S(2)}) async-start(bf16[128,2,128,128]{3,2,1,0:T(8,128)(2,1)} %bitcast.11), calls=%async_computation | async-start | bytes 16777216 | tf_op jit(solution)/shard_map/all_to_all | solution.py:357
  16.3 0.2 copy.29
  16.7 0.6 gather_fusion
  17.6 0.2 broadcast_compare_fusion
  18.2 0.3 select_reduce_fusion
  20.0 0.2 convert_reduce_fusion
  20.3 95.3 %all-to-all-done = bf16[128,2,128,128]{3,2,1,0:T(8,128)(2,1)} async-done(((bf16[128,2,128,128]{3,2,1,0:T(8,128)(2,1)}), bf16[128,2,128,128]{3,2,1,0:T(8,128)(2,1)}, u32[]{:S(2)}, u32[]{:S(2)}) %all-to-all-start) | async-done | bytes 8388640 | tf_op jit(solution)/shard_map/all_to_all | solution.py:357
  115.6 5.3 %admit.2 = (bf16[18,128,128]{2,1,0:T(8,128)(2,1)S(1)}, bf16[24,128,128]{2,1,0:T(8,128)(2,1)S(1)}, bf16[18,128,128]{2,1,0:T(8,128)(2,1)S(1)}) custom-call(s32[61]{0:T(128)S(1)} %convert_reduce_fusion.2.first_ref, s32[256]{0:T(256)S(1)} %select_reduce_fusion.1.order_ref, s32[60]{0:T(128)S(1)} %select_reduce_fusion.4.source_ref, ...), custom_call_target="tpu_custom_call" | custom-call | tf_op jit(solution)/shard_map/admit/pallas_call | solution.py:91
  120.9 6.2 %collective-permute-start.6 = (bf16[24,128,128]{2,1,0:T(8,128)(2,1)S(1)}, bf16[24,128,128]{2,1,0:T(8,128)(2,1)S(1)}, u32[]{:S(2)}, u32[]{:S(2)}) collective-permute-start(bf16[24,128,128]{2,1,0:T(8,128)(2,1)S(1)} %get-tuple-element.32.refs_2_), channel_id=1, source_target_pairs={{0,3},{1,2},{2,1},{3,0},{4,7},{5,6},{6,5},{7,4},{8,11},{9,10},{10,... | collective-permute-start | bytes 2359304 | tf_op jit(solution)/shard_map/ppermute | solution.py:408
  127.1 4.1 %admit.3.refs_1_ = bf16[18,128,128]{2,1,0:T(8,128)(2,1)S(1)} custom-call(s32[61]{0:T(128)S(1)} %convert_reduce_fusion.2.first_ref, s32[256]{0:T(256)S(1)} %select_reduce_fusion.1.order_ref, s32[60]{0:T(128)S(1)} %select_reduce_fusion.4.source_ref, bf16[60,128,128]{2,1,0:T(8,128)(2,1)S(1)} %bitcast.10, bf16[256,128,128]{2,1,0:T(8,128)(2,1)} %bitcast.2.received_ref), custom_call_target="tpu_custom_call" | custom-call | tf_op jit(solution)/shard_map/admit/pallas_call | solution.py:91
  131.5 2.8 %collective-permute-start = (bf16[18,128,128]{2,1,0:T(8,128)(2,1)S(1)}, bf16[18,128,128]{2,1,0:T(8,128)(2,1)S(1)}, u32[]{:S(2)}, u32[]{:S(2)}) collective-permute-start(bf16[18,128,128]{2,1,0:T(8,128)(2,1)S(1)} %get-tuple-element.31.refs_0_), channel_id=1, source_target_pairs={{0,7},{1,6},{2,5},{3,4},{4,3},{5,2},{6,1},{7,0},{8,15},{9,14},{10,... | collective-permute-start | bytes 1769480 | tf_op jit(solution)/shard_map/ppermute | solution.py:408
  134.3 14.2 %collective-permute-done.3.refs_16_ = bf16[18,128,128]{2,1,0:T(8,128)(2,1)S(1)} collective-permute-done((bf16[18,128,128]{2,1,0:T(8,128)(2,1)S(1)}, bf16[18,128,128]{2,1,0:T(8,128)(2,1)S(1)}, u32[]{:S(2)}, u32[]{:S(2)}) %collective-permute-start.3) | collective-permute-done | bytes 589856 | tf_op jit(solution)/shard_map/ppermute | solution.py:408
  148.5 9.7 %collective-permute-done.19.refs_7_ = bf16[18,128,128]{2,1,0:T(8,128)(2,1)S(1)} collective-permute-done((bf16[18,128,128]{2,1,0:T(8,128)(2,1)S(1)}, bf16[18,128,128]{2,1,0:T(8,128)(2,1)S(1)}, u32[]{:S(2)}, u32[]{:S(2)}) %collective-permute-start.19) | collective-permute-done | bytes 589856 | tf_op jit(solution)/shard_map/ppermute | solution.py:408
  158.2 1.4 collective-permute-start.4
  159.7 0.4 collective-permute-start.1
  160.1 10.7 %collective-permute-done.18.refs_6_ = bf16[18,128,128]{2,1,0:T(8,128)(2,1)S(1)} collective-permute-done((bf16[18,128,128]{2,1,0:T(8,128)(2,1)S(1)}, bf16[18,128,128]{2,1,0:T(8,128)(2,1)S(1)}, u32[]{:S(2)}, u32[]{:S(2)}) %collective-permute-start.18) | collective-permute-done | bytes 589856 | tf_op jit(solution)/shard_map/ppermute | solution.py:408
  170.8 12.6 %collective-permute-done.4.refs_10_ = bf16[18,128,128]{2,1,0:T(8,128)(2,1)S(1)} collective-permute-done((bf16[18,128,128]{2,1,0:T(8,128)(2,1)S(1)}, bf16[18,128,128]{2,1,0:T(8,128)(2,1)S(1)}, u32[]{:S(2)}, u32[]{:S(2)}) %collective-permute-start.4) | collective-permute-done | bytes 589856 | tf_op jit(solution)/shard_map/ppermute | solution.py:408
  183.5 1.5 collective-permute-start.13
  185.0 9.8 %collective-permute-done.1.refs_9_ = bf16[18,128,128]{2,1,0:T(8,128)(2,1)S(1)} collective-permute-done((bf16[18,128,128]{2,1,0:T(8,128)(2,1)S(1)}, bf16[18,128,128]{2,1,0:T(8,128)(2,1)S(1)}, u32[]{:S(2)}, u32[]{:S(2)}) %collective-permute-start.1) | collective-permute-done | bytes 589856 | tf_op jit(solution)/shard_map/ppermute | solution.py:408
  194.8 1.2 collective-permute-start.5
  196.2 0.8 collective-permute-start.22
  197.0 4.3 %collective-permute-start.12 = (bf16[18,128,128]{2,1,0:T(8,128)(2,1)S(1)}, bf16[18,128,128]{2,1,0:T(8,128)(2,1)S(1)}, u32[]{:S(2)}, u32[]{:S(2)}) collective-permute-start(bf16[18,128,128]{2,1,0:T(8,128)(2,1)S(1)} %collective-permute-done.refs_15_), channel_id=1, source_target_pairs={{0,8},{1,9},{2,10},{3,11},{4,124},{5,125},{6,126},{7,127},{8,16},{... | collective-permute-start | bytes 1769480 | tf_op jit(solution)/shard_map/ppermute | solution.py:408
  201.3 11.2 %collective-permute-done.5.refs_1_ = bf16[18,128,128]{2,1,0:T(8,128)(2,1)S(1)} collective-permute-done((bf16[18,128,128]{2,1,0:T(8,128)(2,1)S(1)}, bf16[18,128,128]{2,1,0:T(8,128)(2,1)S(1)}, u32[]{:S(2)}, u32[]{:S(2)}) %collective-permute-start.5) | collective-permute-done | bytes 589856 | tf_op jit(solution)/shard_map/ppermute | solution.py:408
  212.5 2.3 collective-permute-start.10
  214.9 10.3 %collective-permute-done.2.refs_0_ = bf16[18,128,128]{2,1,0:T(8,128)(2,1)S(1)} collective-permute-done((bf16[18,128,128]{2,1,0:T(8,128)(2,1)S(1)}, bf16[18,128,128]{2,1,0:T(8,128)(2,1)S(1)}, u32[]{:S(2)}, u32[]{:S(2)}) %collective-permute-start.2) | collective-permute-done | bytes 589856 | tf_op jit(solution)/shard_map/ppermute | solution.py:408
  225.2 2.3 collective-permute-start.9
  227.5 10.3 %collective-permute-done.8.refs_2_ = bf16[18,128,128]{2,1,0:T(8,128)(2,1)S(1)} collective-permute-done((bf16[18,128,128]{2,1,0:T(8,128)(2,1)S(1)}, bf16[18,128,128]{2,1,0:T(8,128)(2,1)S(1)}, u32[]{:S(2)}, u32[]{:S(2)}) %collective-permute-start.8) | collective-permute-done | bytes 589856 | tf_op jit(solution)/shard_map/ppermute | solution.py:408
  237.8 2.3 collective-permute-start.11
  240.2 2.1 collective-permute-start.14
  242.2 9.0 %square_near.1 = (bf16[2304,384]{1,0:T(8,128)(2,1)S(1)}, bf16[1536,384]{1,0:T(8,128)(2,1)S(1)}, bf16[1536,384]{1,0:T(8,128)(2,1)S(1)}, bf16[2304,384]{1,0:T(8,12...) custom-call(s32[729]{0:T(1024)S(1)} %reshape.495.pos_ref, ...), custom_call_target="tpu_custom_call" | custom-call | tf_op jit(solution)/shard_map/square_near/pallas_call | solution.py:176
  251.3 13.0 %purify_far.1 = f32[60,128,128]{2,1,0:T(8,128)} custom-call(s32[729]{0:T(1024)S(1)} %reshape.495.pos_ref, s32[81]{0:T(128)S(1)} %reshape.496.slot_ref, bf16[18,128,128]{2,1,0:T(8,128)(2,1)S(1)} %collective-permute-done.2.refs_0_, bf16[18,128,128]{2,1,0:T(8,128)(2,1)S(1)} %collective-permute-done.5.refs_1_, ...), custom_call_target="tpu_custom_call" | custom-call | tf_op jit(solution)/shard_map/purify_far/pallas_call | solution.py:272
  (77 shorter events, 3.1 us)
Async XLA Ops:
  4.3 12.0 %copy-start.2 = (s32[32,4,3,20]{0,1,3,2:T(4,128)S(1)}, s32[32,4,3,20]{0,1,3,2:T(4,128)}, u32[]{:S(2)}) copy-start(s32[32,4,3,20]{0,1,3,2:T(4,128)} %param.6) | copy-start | bytes 92164
  4.3 14.5 %copy-start.1 = (s32[12288]{0:T(1024)S(1)}, s32[12288]{0:T(1024)}, u32[]{:S(2)}) copy-start(s32[12288]{0:T(1024)} %owner_ref.1) | copy-start | bytes 147460
  4.3 111.3 %all-to-all-start = ((bf16[128,2,128,128]{3,2,1,0:T(8,128)(2,1)}), bf16[128,2,128,128]{3,2,1,0:T(8,128)(2,1)}, u32[]{:S(2)}, u32[]{:S(2)}) async-start(bf16[128,2,128,128]{3,2,1,0:T(8,128)(2,1)} %bitcast.11), calls=%async_computation | async-start | bytes 16777216 | tf_op jit(solution)/shard_map/all_to_all | solution.py:357
  16.2 3.0 %copy-start.3 = (s32[12288]{0:T(1024)S(1)}, s32[12288]{0:T(1024)}, u32[]{:S(2)}) copy-start(s32[12288]{0:T(1024)} %param.9) | copy-start | bytes 147460
  16.3 99.4 %copy-start = (bf16[1,1,3,20,128,128]{5,4,3,2,1,0:T(8,128)(2,1)S(1)}, bf16[1,1,3,20,128,128]{5,4,3,2,1,0:T(8,128)(2,1)}, u32[]{:S(2)}) copy-start(bf16[1,1,3,20,128,128]{5,4,3,2,1,0:T(8,128)(2,1)} %param.5) | copy-start | bytes 5898244
  120.9 38.7 %collective-permute-start.6 = (bf16[24,128,128]{2,1,0:T(8,128)(2,1)S(1)}, bf16[24,128,128]{2,1,0:T(8,128)(2,1)S(1)}, u32[]{:S(2)}, u32[]{:S(2)}) collective-permute-start(bf16[24,128,128]{2,1,0:T(8,128)(2,1)S(1)} %get-tuple-element.32.refs_2_), channel_id=1, source_target_pairs={{0,3},{1,2},{2,1},{3,0},{4,7},{5,6},{6,5},{7,4},{8,11},{9,10},{10,... | collective-permute-start | bytes 2359304 | tf_op jit(solution)/shard_map/ppermute | solution.py:408
  131.2 17.2 %collective-permute-start.3 = (bf16[18,128,128]{2,1,0:T(8,128)(2,1)S(1)}, bf16[18,128,128]{2,1,0:T(8,128)(2,1)S(1)}, u32[]{:S(2)}, u32[]{:S(2)}) collective-permute-start(bf16[18,128,128]{2,1,0:T(8,128)(2,1)S(1)} %admit.3.refs_1_), channel_id=1, source_target_pairs={{0,7},{1,6},{2,5},{3,4},{4,3},{5,2},{6,1},{7,0},{8,15},{9,14},{10,... | collective-permute-start | bytes 1769480 | tf_op jit(solution)/shard_map/ppermute | solution.py:408
  131.3 17.1 %collective-permute-start.16 = (bf16[18,128,128]{2,1,0:T(8,128)(2,1)S(1)}, bf16[18,128,128]{2,1,0:T(8,128)(2,1)S(1)}, u32[]{:S(2)}, u32[]{:S(2)}) collective-permute-start(bf16[18,128,128]{2,1,0:T(8,128)(2,1)S(1)} %admit.3.refs_1_), channel_id=1, source_target_pairs={{0,1},{1,0},{2,3},{3,2},{4,5},{5,4},{6,7},{7,6},{8,9},{9,8},{10,11... | collective-permute-start | bytes 1769480 | tf_op jit(solution)/shard_map/ppermute | solution.py:408
  131.4 26.7 %collective-permute-start.19 = (bf16[18,128,128]{2,1,0:T(8,128)(2,1)S(1)}, bf16[18,128,128]{2,1,0:T(8,128)(2,1)S(1)}, u32[]{:S(2)}, u32[]{:S(2)}) collective-permute-start(bf16[18,128,128]{2,1,0:T(8,128)(2,1)S(1)} %admit.3.refs_1_), channel_id=1, source_target_pairs={{0,3},{1,2},{2,1},{3,0},{4,7},{5,6},{6,5},{7,4},{8,11},{9,10},{10,... | collective-permute-start | bytes 1769480 | tf_op jit(solution)/shard_map/ppermute | solution.py:408
  131.5 28.1 %collective-permute-start = (bf16[18,128,128]{2,1,0:T(8,128)(2,1)S(1)}, bf16[18,128,128]{2,1,0:T(8,128)(2,1)S(1)}, u32[]{:S(2)}, u32[]{:S(2)}) collective-permute-start(bf16[18,128,128]{2,1,0:T(8,128)(2,1)S(1)} %get-tuple-element.31.refs_0_), channel_id=1, source_target_pairs={{0,7},{1,6},{2,5},{3,4},{4,3},{5,2},{6,1},{7,0},{8,15},{9,14},{10,... | collective-permute-start | bytes 1769480 | tf_op jit(solution)/shard_map/ppermute | solution.py:408
  148.5 11.3 %collective-permute-start.15 = (bf16[18,128,128]{2,1,0:T(8,128)(2,1)S(1)}, bf16[18,128,128]{2,1,0:T(8,128)(2,1)S(1)}, u32[]{:S(2)}, u32[]{:S(2)}) collective-permute-start(bf16[18,128,128]{2,1,0:T(8,128)(2,1)S(1)} %get-tuple-element.31.refs_0_), channel_id=1, source_target_pairs={{0,1},{1,0},{2,3},{3,2},{4,5},{5,4},{6,7},{7,6},{8,9},{9,8},{10,11... | collective-permute-start | bytes 1769480 | tf_op jit(solution)/shard_map/ppermute | solution.py:408
  148.5 22.3 %collective-permute-start.18 = (bf16[18,128,128]{2,1,0:T(8,128)(2,1)S(1)}, bf16[18,128,128]{2,1,0:T(8,128)(2,1)S(1)}, u32[]{:S(2)}, u32[]{:S(2)}) collective-permute-start(bf16[18,128,128]{2,1,0:T(8,128)(2,1)S(1)} %get-tuple-element.31.refs_0_), channel_id=1, source_target_pairs={{0,3},{1,2},{2,1},{3,0},{4,7},{5,6},{6,5},{7,4},{8,11},{9,10},{10,... | collective-permute-start | bytes 1769480 | tf_op jit(solution)/shard_map/ppermute | solution.py:408
  158.2 25.3 %collective-permute-start.4 = (bf16[18,128,128]{2,1,0:T(8,128)(2,1)S(1)}, bf16[18,128,128]{2,1,0:T(8,128)(2,1)S(1)}, u32[]{:S(2)}, u32[]{:S(2)}) collective-permute-start(bf16[18,128,128]{2,1,0:T(8,128)(2,1)S(1)} %collective-permute-done.3.refs_16_), channel_id=1, source_target_pairs={{0,3},{1,2},{2,1},{3,0},{4,7},{5,6},{6,5},{7,4},{8,11},{9,10},{10,... | collective-permute-start | bytes 1769480 | tf_op jit(solution)/shard_map/ppermute | solution.py:408
  159.6 23.9 %collective-permute-start.7 = (bf16[24,128,128]{2,1,0:T(8,128)(2,1)S(1)}, bf16[24,128,128]{2,1,0:T(8,128)(2,1)S(1)}, u32[]{:S(2)}, u32[]{:S(2)}) collective-permute-start(bf16[24,128,128]{2,1,0:T(8,128)(2,1)S(1)} %collective-permute-done.6.refs_8_), channel_id=1, source_target_pairs={{0,7},{1,6},{2,5},{3,4},{4,3},{5,2},{6,1},{7,0},{8,15},{9,14},{10,... | collective-permute-start | bytes 2359304 | tf_op jit(solution)/shard_map/ppermute | solution.py:408
  159.6 36.4 %collective-permute-start.17 = (bf16[24,128,128]{2,1,0:T(8,128)(2,1)S(1)}, bf16[24,128,128]{2,1,0:T(8,128)(2,1)S(1)}, u32[]{:S(2)}, u32[]{:S(2)}) collective-permute-start(bf16[24,128,128]{2,1,0:T(8,128)(2,1)S(1)} %get-tuple-element.32.refs_2_), channel_id=1, source_target_pairs={{0,1},{1,0},{2,3},{3,2},{4,5},{5,4},{6,7},{7,6},{8,9},{9,8},{10,11... | collective-permute-start | bytes 2359304 | tf_op jit(solution)/shard_map/ppermute | solution.py:408
  159.7 35.1 %collective-permute-start.1 = (bf16[18,128,128]{2,1,0:T(8,128)(2,1)S(1)}, bf16[18,128,128]{2,1,0:T(8,128)(2,1)S(1)}, u32[]{:S(2)}, u32[]{:S(2)}) collective-permute-start(bf16[18,128,128]{2,1,0:T(8,128)(2,1)S(1)} %collective-permute-done.refs_15_), channel_id=1, source_target_pairs={{0,3},{1,2},{2,1},{3,0},{4,7},{5,6},{6,5},{7,4},{8,11},{9,10},{10,... | collective-permute-start | bytes 1769480 | tf_op jit(solution)/shard_map/ppermute | solution.py:408
  170.8 24.0 %collective-permute-start.23 = (bf16[18,128,128]{2,1,0:T(8,128)(2,1)S(1)}, bf16[18,128,128]{2,1,0:T(8,128)(2,1)S(1)}, u32[]{:S(2)}, u32[]{:S(2)}) collective-permute-start(bf16[18,128,128]{2,1,0:T(8,128)(2,1)S(1)} %get-tuple-element.33), channel_id=1, source_target_pairs={{0,7},{1,6},{2,5},{3,4},{4,3},{5,2},{6,1},{7,0},{8,15},{9,14},{10,... | collective-permute-start | bytes 1769480 | tf_op jit(solution)/shard_map/ppermute | solution.py:408
  183.4 12.8 %collective-permute-start.21 = (bf16[18,128,128]{2,1,0:T(8,128)(2,1)S(1)}, bf16[18,128,128]{2,1,0:T(8,128)(2,1)S(1)}, u32[]{:S(2)}, u32[]{:S(2)}) collective-permute-start(bf16[18,128,128]{2,1,0:T(8,128)(2,1)S(1)} %collective-permute-done.4.refs_10_), channel_id=1, source_target_pairs={{0,1},{1,0},{2,3},{3,2},{4,5},{5,4},{6,7},{7,6},{8,9},{9,8},{10,11... | collective-permute-start | bytes 1769480 | tf_op jit(solution)/shard_map/ppermute | solution.py:408
  183.5 12.7 %collective-permute-start.13 = (bf16[9,128,128]{2,1,0:T(8,128)(2,1)S(1)}, bf16[9,128,128]{2,1,0:T(8,128)(2,1)S(1)}, u32[]{:S(2)}, u32[]{:S(2)}) collective-permute-start(bf16[9,128,128]{2,1,0:T(8,128)(2,1)S(1)} %slice.29), channel_id=1, source_target_pairs={{0,8},{1,9},{2,10},{3,11},{4,124},{5,125},{6,126},{7,127},{8,16},{... | collective-permute-start | bytes 884744 | tf_op jit(solution)/shard_map/ppermute | solution.py:408
  194.8 2.2 collective-permute-start.20
  194.8 17.7 %collective-permute-start.5 = (bf16[18,128,128]{2,1,0:T(8,128)(2,1)S(1)}, bf16[18,128,128]{2,1,0:T(8,128)(2,1)S(1)}, u32[]{:S(2)}, u32[]{:S(2)}) collective-permute-start(bf16[18,128,128]{2,1,0:T(8,128)(2,1)S(1)} %collective-permute-done.4.refs_10_), channel_id=1, source_target_pairs={{0,8},{1,9},{2,10},{3,11},{4,124},{5,125},{6,126},{7,127},{8,16},{... | collective-permute-start | bytes 1769480 | tf_op jit(solution)/shard_map/ppermute | solution.py:408
  196.1 29.1 %collective-permute-start.2 = (bf16[18,128,128]{2,1,0:T(8,128)(2,1)S(1)}, bf16[18,128,128]{2,1,0:T(8,128)(2,1)S(1)}, u32[]{:S(2)}, u32[]{:S(2)}) collective-permute-start(bf16[18,128,128]{2,1,0:T(8,128)(2,1)S(1)} %collective-permute-done.1.refs_9_), channel_id=1, source_target_pairs={{0,8},{1,9},{2,10},{3,11},{4,124},{5,125},{6,126},{7,127},{8,16},{... | collective-permute-start | bytes 1769480 | tf_op jit(solution)/shard_map/ppermute | solution.py:408
  196.1 41.7 %collective-permute-start.8 = (bf16[18,128,128]{2,1,0:T(8,128)(2,1)S(1)}, bf16[18,128,128]{2,1,0:T(8,128)(2,1)S(1)}, u32[]{:S(2)}, u32[]{:S(2)}) collective-permute-start(bf16[18,128,128]{2,1,0:T(8,128)(2,1)S(1)} %slice.28), channel_id=1, source_target_pairs={{0,8},{1,9},{2,10},{3,11},{4,124},{5,125},{6,126},{7,127},{8,16},{... | collective-permute-start | bytes 1769480 | tf_op jit(solution)/shard_map/ppermute | solution.py:408
  196.2 43.9 %collective-permute-start.22 = (bf16[24,128,128]{2,1,0:T(8,128)(2,1)S(1)}, bf16[24,128,128]{2,1,0:T(8,128)(2,1)S(1)}, u32[]{:S(2)}, u32[]{:S(2)}) collective-permute-start(bf16[24,128,128]{2,1,0:T(8,128)(2,1)S(1)} %collective-permute-done.7.refs_11_), channel_id=1, source_target_pairs={{0,1},{1,0},{2,3},{3,2},{4,5},{5,4},{6,7},{7,6},{8,9},{9,8},{10,11... | collective-permute-start | bytes 2359304 | tf_op jit(solution)/shard_map/ppermute | solution.py:408
  197.0 54.3 %collective-permute-start.12 = (bf16[18,128,128]{2,1,0:T(8,128)(2,1)S(1)}, bf16[18,128,128]{2,1,0:T(8,128)(2,1)S(1)}, u32[]{:S(2)}, u32[]{:S(2)}) collective-permute-start(bf16[18,128,128]{2,1,0:T(8,128)(2,1)S(1)} %collective-permute-done.refs_15_), channel_id=1, source_target_pairs={{0,8},{1,9},{2,10},{3,11},{4,124},{5,125},{6,126},{7,127},{8,16},{... | collective-permute-start | bytes 1769480 | tf_op jit(solution)/shard_map/ppermute | solution.py:408
  212.5 38.8 %collective-permute-start.10 = (bf16[18,128,128]{2,1,0:T(8,128)(2,1)S(1)}, bf16[18,128,128]{2,1,0:T(8,128)(2,1)S(1)}, u32[]{:S(2)}, u32[]{:S(2)}) collective-permute-start(bf16[18,128,128]{2,1,0:T(8,128)(2,1)S(1)} %collective-permute-done.5.refs_1_), channel_id=1, source_target_pairs={{0,1},{1,0},{2,3},{3,2},{4,5},{5,4},{6,7},{7,6},{8,9},{9,8},{10,11... | collective-permute-start | bytes 1769480 | tf_op jit(solution)/shard_map/ppermute | solution.py:408
  225.2 26.1 %collective-permute-start.9 = (bf16[18,128,128]{2,1,0:T(8,128)(2,1)S(1)}, bf16[18,128,128]{2,1,0:T(8,128)(2,1)S(1)}, u32[]{:S(2)}, u32[]{:S(2)}) collective-permute-start(bf16[18,128,128]{2,1,0:T(8,128)(2,1)S(1)} %collective-permute-done.2.refs_0_), channel_id=1, source_target_pairs={{0,1},{1,0},{2,3},{3,2},{4,5},{5,4},{6,7},{7,6},{8,9},{9,8},{10,11... | collective-permute-start | bytes 1769480 | tf_op jit(solution)/shard_map/ppermute | solution.py:408
  237.8 13.5 %collective-permute-start.11 = (bf16[18,128,128]{2,1,0:T(8,128)(2,1)S(1)}, bf16[18,128,128]{2,1,0:T(8,128)(2,1)S(1)}, u32[]{:S(2)}, u32[]{:S(2)}) collective-permute-start(bf16[18,128,128]{2,1,0:T(8,128)(2,1)S(1)} %collective-permute-done.8.refs_2_), channel_id=1, source_target_pairs={{0,1},{1,0},{2,3},{3,2},{4,5},{5,4},{6,7},{7,6},{8,9},{9,8},{10,11... | collective-permute-start | bytes 1769480 | tf_op jit(solution)/shard_map/ppermute | solution.py:408
  240.2 11.1 %collective-permute-start.14 = (bf16[9,128,128]{2,1,0:T(8,128)(2,1)S(1)}, bf16[9,128,128]{2,1,0:T(8,128)(2,1)S(1)}, u32[]{:S(2)}, u32[]{:S(2)}) collective-permute-start(bf16[9,128,128]{2,1,0:T(8,128)(2,1)S(1)} %slice.30), channel_id=1, source_target_pairs={{0,3},{1,2},{2,1},{3,0},{4,7},{5,6},{6,5},{7,4},{8,11},{9,10},{10,... | collective-permute-start | bytes 884744 | tf_op jit(solution)/shard_map/ppermute | solution.py:408
